TPU v7x, 256 devices: a whole 4x4x8 slice. The times are simulated.
256 devices in a mesh: seq: 8 (over x, core), head: 8 (over z), dp: 4 (over y).
Axes of the slice: x: 4, y: 4, z: 8, core: 2. Of those that a mesh axis runs over, the one named last changes fastest.
Arguments:
- layer_input: bfloat16 [4, 4096, 2048], P('dp', 'seq'), may hold values from -6 to 6
- w_query: bfloat16 [2048, 2048], P(None, 'head'), may hold values from -0.125 to 0.125
- w_key: bfloat16 [2048, 2048], P(None, 'head'), may hold values from -0.125 to 0.125
- w_value: bfloat16 [2048, 2048], P(None, 'head'), may hold values from -0.125 to 0.125
- w_out: bfloat16 [2048, 2048], P('head'), may hold values from -0.125 to 0.125
- out_grad: bfloat16 [4, 4096, 2048], P('dp', 'seq'), may hold values from -6 to 6
Outputs:
- input_grad: bfloat16 [4, 4096, 2048], P('dp', 'seq', 'head')
- grad_query: float32 [2048, 2048], P(('seq', 'dp'), 'head')
- grad_key: float32 [2048, 2048], P(('seq', 'dp'), 'head')
- grad_value: float32 [2048, 2048], P(('seq', 'dp'), 'head')
- grad_out: float32 [2048, 2048], P('head', ('seq', 'dp'))
All inputs are finite; a program needn't handle non-finite values.
Results may differ from a plain program's by a relative error of at most 0.0073.
Values sent between devices are 32-bit elements; how exact they have to be, the bound alone decides.
A program may use at most 64 MiB of HBM per device.

v0:
```python
import jax
import jax.numpy as jnp
from jax import lax
from jax.sharding import PartitionSpec as P

HEAD_DIM = 128


def entering(x, axis, combine, identity, reverse):
    peers, here = (lax.axis_size(axis), lax.axis_index(axis))
    everything = lax.all_gather(x, axis)
    start = jnp.broadcast_to(jnp.asarray(identity, x.dtype), x.shape)

    def step(k, before):
        at = peers - 1 - k if reverse else k
        reached = at > here if reverse else at < here
        new = combine(before, everything[at])
        return jnp.where(reached, new, before)

    return lax.fori_loop(0, peers, step, start)


def add_states(earlier, later_sum):
    return earlier + later_sum


def local(layer_input, w_query, w_key, w_value, w_out, out_grad):
    num_rows = layer_input.shape[1]
    local_heads = w_query.shape[1] // HEAD_DIM
    in_rows = layer_input[0]
    grad_rows = out_grad[0]

    def project(weight):
        result = jnp.dot(in_rows, weight, preferred_element_type=jnp.float32).astype(jnp.bfloat16)
        return result.reshape(num_rows, local_heads, HEAD_DIM)

    queries = project(w_query)
    key_rows = project(w_key)
    value_rows = project(w_value)
    row_start = lax.axis_index("seq") * num_rows
    positions = (row_start + jnp.arange(num_rows, dtype=jnp.int32)).astype(jnp.float32)
    pos_scale = 1.0 / jnp.sqrt(HEAD_DIM * (positions + 1.0))
    backward = jnp.einsum("td,kd->tk", grad_rows, w_out, preferred_element_type=jnp.float32)
    grad_in = (
        (backward * pos_scale[:, None])
        .astype(jnp.bfloat16)
        .reshape(num_rows, local_heads, HEAD_DIM)
    )
    kv_state = jnp.einsum("thd,the->hde", key_rows, value_rows, preferred_element_type=jnp.float32)
    qg_state = jnp.einsum("thd,the->hde", queries, grad_in, preferred_element_type=jnp.float32)
    zero_state = jnp.zeros_like(kv_state)
    prefix = entering(kv_state, "seq", add_states, zero_state, False)
    suffix = entering(qg_state, "seq", add_states, zero_state, True)
    prefix = prefix.astype(jnp.bfloat16)
    suffix = suffix.astype(jnp.bfloat16)
    causal = (jnp.arange(num_rows)[:, None] >= jnp.arange(num_rows)[None, :])[None]
    scores = jnp.einsum("thd,shd->hts", queries, key_rows, preferred_element_type=jnp.float32)
    scores_qk = jnp.where(causal, scores, 0.0).astype(jnp.bfloat16)
    scores_g = jnp.einsum("thd,shd->hts", grad_in, value_rows, preferred_element_type=jnp.float32)
    scores_gv = jnp.where(causal, scores_g, 0.0).astype(jnp.bfloat16)
    inner_sum = jnp.einsum(
        "hts,she->the", scores_qk, value_rows, preferred_element_type=jnp.float32
    )
    cross_sum = jnp.einsum("thd,hde->the", queries, prefix, preferred_element_type=jnp.float32)
    attention = (
        ((inner_sum + cross_sum) * pos_scale[:, None, None])
        .astype(jnp.bfloat16)
        .reshape(num_rows, local_heads * HEAD_DIM)
    )
    d_query = jnp.einsum("hts,shd->thd", scores_gv, key_rows, preferred_element_type=jnp.float32)
    d_query = d_query + jnp.einsum(
        "the,hde->thd", grad_in, prefix, preferred_element_type=jnp.float32
    )
    d_keys = jnp.einsum("hts,thd->shd", scores_gv, queries, preferred_element_type=jnp.float32)
    d_keys = d_keys + jnp.einsum(
        "she,hde->shd", value_rows, suffix, preferred_element_type=jnp.float32
    )
    d_values = jnp.einsum("hts,the->she", scores_qk, grad_in, preferred_element_type=jnp.float32)
    d_values = d_values + jnp.einsum(
        "shd,hde->she", key_rows, suffix, preferred_element_type=jnp.float32
    )
    d_query = d_query.astype(jnp.bfloat16).reshape(num_rows, local_heads * HEAD_DIM)
    d_keys = d_keys.astype(jnp.bfloat16).reshape(num_rows, local_heads * HEAD_DIM)
    d_values = d_values.astype(jnp.bfloat16).reshape(num_rows, local_heads * HEAD_DIM)
    head_terms = jnp.einsum("tk,dk->td", d_query, w_query, preferred_element_type=jnp.float32)
    head_terms = head_terms + jnp.einsum(
        "tk,dk->td", d_keys, w_key, preferred_element_type=jnp.float32
    )
    head_terms = head_terms + jnp.einsum(
        "tk,dk->td", d_values, w_value, preferred_element_type=jnp.float32
    )
    input_grad = lax.psum_scatter(head_terms, "head", scatter_dimension=1, tiled=True).astype(
        jnp.bfloat16
    )[None]
    total_rows = lax.axis_size("seq") * lax.axis_size("dp") * num_rows
    grad_scale = jnp.float32(1.0) / jnp.sqrt(jnp.float32(total_rows))
    term_query = (
        jnp.einsum("td,tk->dk", in_rows, d_query, preferred_element_type=jnp.float32) * grad_scale
    )
    term_key = (
        jnp.einsum("td,tk->dk", in_rows, d_keys, preferred_element_type=jnp.float32) * grad_scale
    )
    term_value = (
        jnp.einsum("td,tk->dk", in_rows, d_values, preferred_element_type=jnp.float32) * grad_scale
    )
    term_out = (
        jnp.einsum("td,tk->dk", grad_rows, attention, preferred_element_type=jnp.float32)
        * grad_scale
    )
    summed = (
        lax.psum_scatter(term_query, ("seq", "dp"), scatter_dimension=0, tiled=True),
        lax.psum_scatter(term_key, ("seq", "dp"), scatter_dimension=0, tiled=True),
        lax.psum_scatter(term_value, ("seq", "dp"), scatter_dimension=0, tiled=True),
        lax.psum_scatter(term_out, ("seq", "dp"), scatter_dimension=0, tiled=True),
    )
    return (input_grad, summed[0], summed[1], summed[2], summed[3].T)


def solution(mesh):
    return jax.shard_map(
        local,
        mesh=mesh,
        in_specs=(
            P("dp", "seq", None),
            P(None, "head"),
            P(None, "head"),
            P(None, "head"),
            P("head", None),
            P("dp", "seq", None),
        ),
        out_specs=(
            P("dp", "seq", "head"),
            P(("seq", "dp"), "head"),
            P(("seq", "dp"), "head"),
            P(("seq", "dp"), "head"),
            P("head", ("seq", "dp")),
        ),
        check_vma=False,
    )
```

profile of v0, /device:TPU:8, one launch (start us, length us, event | category | flops | bytes accessed | tf_op | source)
XLA Modules:
  0.0 508.7 jit_solution(6462937614558508686)
XLA Ops:
  8.8 2.0 fusion.33
  12.5 2.0 fusion.27
  14.5 2.1 fusion.30
  20.7 20.7 %all-gather.7.cloned.1.call-done = f32[16,128,128]{2,1,0:T(8,128)} async-done(((f32[2,128,128]{2,1,0:T(8,128)}), f32[16,128,128]{2,1,0:T(8,128)}) %all-gather.7.cloned.1.call-update) | async-done | bytes 1048592 | tf_op jit(solution)/shard_map/all_gather | solution.py:11
  41.4 7.8 %while.31 = (s32[]{:T(128)}, f32[2,128,128]{2,1,0:T(8,128)S(1)}, s32[]{:T(128)}, f32[8,2,128,128]{3,2,1,0:T(8,128)}, s32[]{:T(128)}, /*index=5*/s32[]{:T(128)}, s32[]{:T(128)}, s32[]{:T(128)}) while((s32[]{:T(128)}, f32[2,128,128]{2,1,0:T(8,128)S(1)}, s32[]{:T(128)}, f32[8,2,128,128]{3,2,1,0:T(8,128)}, s32[]{:T(128)}, ...), condition=%wide.region_3.4_spmd.clone, body=%wide.region_2.3_spmd.clone.sunk | while | flops 98312 | bytes 393379 | solution.py:20
  49.2 2.0 fusion.38
  51.1 2.0 fusion.36
  53.2 15.9 %all-gather.5.cloned.1.call-done = f32[16,128,128]{2,1,0:T(8,128)} async-done(((f32[2,128,128]{2,1,0:T(8,128)}), f32[16,128,128]{2,1,0:T(8,128)}) %all-gather.5.cloned.1.call-update) | async-done | bytes 1048592 | tf_op jit(solution)/shard_map/all_gather | solution.py:11
  69.1 7.8 %while.30 = (s32[]{:T(128)}, f32[2,128,128]{2,1,0:T(8,128)S(1)}, s32[]{:T(128)}, f32[8,2,128,128]{3,2,1,0:T(8,128)}, s32[]{:T(128)}, /*index=5*/s32[]{:T(128)}) while((s32[]{:T(128)}, f32[2,128,128]{2,1,0:T(8,128)S(1)}, s32[]{:T(128)}, f32[8,2,128,128]{3,2,1,0:T(8,128)}, s32[]{:T(128)}, /*index=5*/s32[]{:T(128)}) %tuple.93), condition=%wide.region_1.2_spmd.clone, body=%wide.region_0.1_spmd.clone.sunk | while | flops 98308 | bytes 393317 | solution.py:20
  78.1 1.8 fusion.21
  84.2 2.7 add_add_fusion
  89.8 2.1 fusion
  91.9 2.9 copy.61
  95.8 2.1 fusion.1
  97.9 3.2 copy.59
  102.0 2.1 fusion.2
  104.1 3.0 copy.57
  108.0 2.0 fusion.3
  110.0 2.9 copy.55
  113.0 29.3 %reduce-scatter.14.cloned.1.call-done = f32[512,256]{1,0:T(8,128)} async-done(((f32[512,2048]{1,0:T(8,128)}), f32[512,256]{1,0:T(8,128)}) %reduce-scatter.14.cloned.1.call-update) | async-done | bytes 524304 | tf_op jit(solution)/shard_map/reduce_scatter | solution.py:92
  144.0 87.3 %reduce-scatter.22.cloned.1.call-done = f32[64,256]{1,0:T(8,128)} async-done(((f32[2048,256]{1,0:T(8,128)}), f32[64,256]{1,0:T(8,128)}) %reduce-scatter.22.cloned.1.call-update) | async-done | bytes 65552
  231.3 90.1 %reduce-scatter.20.cloned.1.call-done = f32[64,256]{1,0:T(8,128)} async-done(((f32[2048,256]{1,0:T(8,128)}), f32[64,256]{1,0:T(8,128)}) %reduce-scatter.20.cloned.1.call-update) | async-done | bytes 65552
  321.4 90.2 %reduce-scatter.18.cloned.1.call-done = f32[64,256]{1,0:T(8,128)} async-done(((f32[2048,256]{1,0:T(8,128)}), f32[64,256]{1,0:T(8,128)}) %reduce-scatter.18.cloned.1.call-update) | async-done | bytes 65552
  411.6 90.3 %reduce-scatter.16.cloned.1.call-done = f32[64,256]{1,0:T(8,128)} async-done(((f32[2048,256]{1,0:T(8,128)}), f32[64,256]{1,0:T(8,128)}) %reduce-scatter.16.cloned.1.call-update) | async-done | bytes 65552
  (91 shorter events, 35.3 us)
Async XLA Ops:
  7.2 1.6 copy-start
  7.2 34.2 %all-gather.7.cloned.1.call-start = ((), (), s32[]{:S(2)}) async-start(), calls=%async_computation.7 | async-start | bytes 1179648 | tf_op jit(solution)/shard_map/all_gather | solution.py:11
  7.2 3.5 copy-start.15
  7.2 3.5 copy-start.21
  11.5 6.2 %copy-start.10 = (bf16[512,256]{0,1:T(8,128)(2,1)}, bf16[512,256]{0,1:T(8,128)(2,1)S(1)}, u32[]{:S(2)}) copy-start(bf16[512,256]{0,1:T(8,128)(2,1)S(1)} %fusion.23) | copy-start | bytes 786436
  12.5 56.6 %all-gather.5.cloned.1.call-start = ((), (), s32[]{:S(2)}) async-start(), calls=%async_computation.6 | async-start | bytes 1179648 | tf_op jit(solution)/shard_map/all_gather | solution.py:11
  14.5 2.1 copy-start.12
  16.6 1.1 copy-start.6
  17.5 124.7 %reduce-scatter.14.cloned.1.call-start = ((), (), s32[]{:S(2)}) async-start(), calls=%async_computation.5 | async-start | bytes 4718592 | tf_op jit(solution)/shard_map/reduce_scatter | solution.py:92
  17.6 1.7 copy-start.13
  76.8 3.1 copy-start.1
  76.9 3.1 copy-start.14
  78.1 2.4 copy-start.18
  80.0 1.3 copy-start.4
  80.5 1.3 copy-start.19
  81.8 0.9 copy-start.11
  81.8 1.1 copy-start.17
  82.9 1.2 copy-start.20
  86.9 144.4 %reduce-scatter.22.cloned.1.call-start = ((), (), s32[]{:S(2)}) async-start(), calls=%async_computation.11 | async-start | bytes 2162688
  87.0 2.8 copy-start.16
  94.9 226.6 %reduce-scatter.20.cloned.1.call-start = ((), (), s32[]{:S(2)}) async-start(), calls=%async_computation.10 | async-start | bytes 2162688
  101.1 310.5 %reduce-scatter.18.cloned.1.call-start = ((), (), s32[]{:S(2)}) async-start(), calls=%async_computation.9 | async-start | bytes 2162688
  107.0 1.0 copy-start.3
  107.0 394.8 %reduce-scatter.16.cloned.1.call-start = ((), (), s32[]{:S(2)}) async-start(), calls=%async_computation.8 | async-start | bytes 2162688
  (5 other events, 4.2 us)
Sparse Core Ops, SparseCore 0:
  12.6 28.7 all-gather.6
  43.2 25.7 all-gather.4
  87.0 55.1 reduce-scatter.13
  146.5 84.7 reduce-scatter.21
  235.6 85.7 reduce-scatter.19
  325.7 85.8 reduce-scatter.17
  416.0 85.8 reduce-scatter.15
where the time goes:
time: 510 us; the launch traced here: 509 us
  waiting for transfers between devices  424 us (83%)
  matrix products  34.7 us (7%)
  local copies, waits for them, and re-layouts  18 us (4%)
  other arithmetic  17.1 us (3%)
  between operations  14.5 us (3%)
    unnamed x11, waiting for transfers between devices  358 us
    all_gather x2, waiting for transfers between devices, entering(): everything = lax.all_gather(x, axis)  36.6 us
    reduce_scatter x1, waiting for transfers between devices, local(): lax.psum_scatter(head_terms, 'head', scatter_dimension=1, tiled=True)  29.3 us
    unnamed x48, local copies, waits for them, and re-layouts  18 us
    select_n x16, other arithmetic, step(): return jnp.where(reached, new, before)  15.2 us
  transfers between devices with their start and end apart: 7, of which 7 were waited for; matrix products, arithmetic and copies ran while one was open for 9% of the time, Pallas kernels for 0%

commit v1 on v0

v1 whole, which is shorter than its diff:
```python
import jax
import jax.numpy as jnp
from jax import lax
from jax.sharding import PartitionSpec as P

HEAD_DIM = 128


def local(layer_input, w_query, w_key, w_value, w_out, out_grad):
    num_rows = layer_input.shape[1]
    local_heads = w_query.shape[1] // HEAD_DIM
    width = local_heads * HEAD_DIM
    in_rows = layer_input[0]
    grad_rows = out_grad[0]

    def project(weight):
        result = jnp.dot(in_rows, weight, preferred_element_type=jnp.float32).astype(jnp.bfloat16)
        return result.reshape(num_rows, local_heads, HEAD_DIM)

    queries = project(w_query)
    key_rows = project(w_key)
    value_rows = project(w_value)
    here = lax.axis_index("seq")
    peers = lax.axis_size("seq")
    row_start = here * num_rows
    positions = (row_start + jnp.arange(num_rows, dtype=jnp.int32)).astype(jnp.float32)
    pos_scale = 1.0 / jnp.sqrt(HEAD_DIM * (positions + 1.0))
    backward = jnp.einsum("td,kd->tk", grad_rows, w_out, preferred_element_type=jnp.float32)
    grad_in = (
        (backward * pos_scale[:, None])
        .astype(jnp.bfloat16)
        .reshape(num_rows, local_heads, HEAD_DIM)
    )
    kv_state = jnp.einsum("thd,the->hde", key_rows, value_rows, preferred_element_type=jnp.float32)
    qg_state = jnp.einsum("thd,the->hde", queries, grad_in, preferred_element_type=jnp.float32)
    states = lax.all_gather(jnp.stack([kv_state, qg_state]), "seq")
    blocks = jnp.arange(peers)[:, None, None, None]
    prefix = jnp.sum(jnp.where(blocks < here, states[:, 0], 0.0), axis=0).astype(jnp.bfloat16)
    suffix = jnp.sum(jnp.where(blocks > here, states[:, 1], 0.0), axis=0).astype(jnp.bfloat16)
    causal = (jnp.arange(num_rows)[:, None] >= jnp.arange(num_rows)[None, :])[None]
    scores = jnp.einsum("thd,shd->hts", queries, key_rows, preferred_element_type=jnp.float32)
    scores_qk = jnp.where(causal, scores, 0.0).astype(jnp.bfloat16)
    scores_g = jnp.einsum("thd,shd->hts", grad_in, value_rows, preferred_element_type=jnp.float32)
    scores_gv = jnp.where(causal, scores_g, 0.0).astype(jnp.bfloat16)
    inner_sum = jnp.einsum(
        "hts,she->the", scores_qk, value_rows, preferred_element_type=jnp.float32
    )
    cross_sum = jnp.einsum("thd,hde->the", queries, prefix, preferred_element_type=jnp.float32)
    attention = (
        ((inner_sum + cross_sum) * pos_scale[:, None, None])
        .astype(jnp.bfloat16)
        .reshape(num_rows, width)
    )
    d_query = jnp.einsum("hts,shd->thd", scores_gv, key_rows, preferred_element_type=jnp.float32)
    d_query = d_query + jnp.einsum(
        "the,hde->thd", grad_in, prefix, preferred_element_type=jnp.float32
    )
    d_keys = jnp.einsum("hts,thd->shd", scores_gv, queries, preferred_element_type=jnp.float32)
    d_keys = d_keys + jnp.einsum(
        "she,hde->shd", value_rows, suffix, preferred_element_type=jnp.float32
    )
    d_values = jnp.einsum("hts,the->she", scores_qk, grad_in, preferred_element_type=jnp.float32)
    d_values = d_values + jnp.einsum(
        "shd,hde->she", key_rows, suffix, preferred_element_type=jnp.float32
    )
    d_query = d_query.astype(jnp.bfloat16).reshape(num_rows, width)
    d_keys = d_keys.astype(jnp.bfloat16).reshape(num_rows, width)
    d_values = d_values.astype(jnp.bfloat16).reshape(num_rows, width)
    head_terms = jnp.einsum("tk,dk->td", d_query, w_query, preferred_element_type=jnp.float32)
    head_terms = head_terms + jnp.einsum(
        "tk,dk->td", d_keys, w_key, preferred_element_type=jnp.float32
    )
    head_terms = head_terms + jnp.einsum(
        "tk,dk->td", d_values, w_value, preferred_element_type=jnp.float32
    )
    input_grad = lax.psum_scatter(head_terms, "head", scatter_dimension=1, tiled=True).astype(
        jnp.bfloat16
    )[None]
    total_rows = lax.axis_size("seq") * lax.axis_size("dp") * num_rows
    grad_scale = jnp.float32(1.0) / jnp.sqrt(jnp.float32(total_rows))
    grads = jnp.concatenate([d_query, d_keys, d_values], axis=1)
    term_qkv = jnp.einsum("td,tk->dk", in_rows, grads, preferred_element_type=jnp.float32)
    term_out = jnp.einsum("td,tk->dk", grad_rows, attention, preferred_element_type=jnp.float32)
    terms = jnp.concatenate([term_qkv, term_out], axis=1) * grad_scale
    summed = lax.psum_scatter(terms, "seq", scatter_dimension=0, tiled=True)
    summed = lax.psum_scatter(summed, "dp", scatter_dimension=0, tiled=True)
    grad_query = summed[:, :width]
    grad_key = summed[:, width:2 * width]
    grad_value = summed[:, 2 * width:3 * width]
    grad_out = summed[:, 3 * width:].T
    return (input_grad, grad_query, grad_key, grad_value, grad_out)


def solution(mesh):
    return jax.shard_map(
        local,
        mesh=mesh,
        in_specs=(
            P("dp", "seq", None),
            P(None, "head"),
            P(None, "head"),
            P(None, "head"),
            P("head", None),
            P("dp", "seq", None),
        ),
        out_specs=(
            P("dp", "seq", "head"),
            P(("seq", "dp"), "head"),
            P(("seq", "dp"), "head"),
            P(("seq", "dp"), "head"),
            P("head", ("seq", "dp")),
        ),
        check_vma=False,
    )
```

time: 510 us -> 212 us (0.42)
  waiting for transfers between devices: 424 us -> 156 us
  matrix products: 34.7 us -> 18.7 us
  local copies, waits for them, and re-layouts: 18 us -> 9.26 us
  other arithmetic: 17.1 us -> 10.7 us
    unnamed x11 -> x5, waiting for transfers between devices: 358 us -> 23.5 us
    reduce_scatter x0 -> x1, waiting for transfers between devices: none -> 49.2 us  [local(): summed = lax.psum_scatter(terms, 'seq', scatter_dimension=0, tiled=True)]
    reduce_scatter x1, waiting for transfers between devices: 29.3 us -> 54.9 us  [local(): lax.psum_scatter(head_terms, 'head', scatter_dimension=1, tiled=True)]
    select_n x16 -> x0, other arithmetic: 15.2 us -> none  [step(): return jnp.where(reached, new, before)]
    unnamed x48 -> x47, local copies, waits for them, and re-layouts: 18 us -> 7.63 us
    all_gather x2 -> x1, waiting for transfers between devices: 36.6 us -> 28.5 us  [local(): states = lax.all_gather(jnp.stack([kv_state, qg_state]), 'seq')]
    mul x0 -> x1, other arithmetic: none -> 6.22 us  [local(): terms = jnp.concatenate([term_qkv, term_out], axis=1) * grad_scale]
  transfers between devices with their start and end apart: 7 -> 4, of which waited for: 7 -> 4; matrix products, arithmetic and copies ran while one was open for 9% -> 6% of each run, Pallas kernels for 0% -> 0%
where the time goes in v1:
time: 212 us; the launch traced here: 209 us
  waiting for transfers between devices  156 us (74%)
  matrix products  18.7 us (9%)
  between operations  14.1 us (7%)
  other arithmetic  10.7 us (5%)
  local copies, waits for them, and re-layouts  9.26 us (4%)
    reduce_scatter x1, waiting for transfers between devices, local(): lax.psum_scatter(head_terms, 'head', scatter_dimension=1, tiled=True)  54.9 us
    reduce_scatter x1, waiting for transfers between devices, local(): summed = lax.psum_scatter(terms, 'seq', scatter_dimension=0, tiled=True)  49.2 us
    all_gather x1, waiting for transfers between devices, local(): states = lax.all_gather(jnp.stack([kv_state, qg_state]), 'seq')  28.5 us
    unnamed x5, waiting for transfers between devices  23.5 us
    unnamed x47, local copies, waits for them, and re-layouts  7.63 us
    mul x1, other arithmetic, local(): terms = jnp.concatenate([term_qkv, term_out], axis=1) * grad_scale  6.22 us
  transfers between devices with their start and end apart: 4, of which 4 were waited for; matrix products, arithmetic and copies ran while one was open for 6% of the time, Pallas kernels for 0%

profile of v1, /device:TPU:8, one launch (start us, length us, event | category | flops | bytes accessed | tf_op | source)
XLA Modules:
  0.0 209.0 jit_solution(8024223371176328473)
XLA Ops:
  7.3 1.5 copy-done
  8.8 2.0 fusion.27
  10.8 0.8 fusion.21
  11.5 0.5 copy-done.20
  12.1 0.8 fusion.24
  12.9 0.9 copy-done.16
  14.0 0.7 fusion.17
  15.3 0.7 pad_maximum_fusion
  16.2 1.5 select_convert_fusion.1
  18.3 28.5 %all-gather.3.cloned.1.call-done = f32[16,2,128,128]{3,2,1,0:T(8,128)} async-done(((f32[2,2,128,128]{3,2,1,0:T(8,128)}), f32[16,2,128,128]{3,2,1,0:T(8,128)}) %all-gather.3.cloned.1.call-update) | async-done | bytes 2097168 | tf_op jit(solution)/shard_map/all_gather | solution.py:36
  46.8 1.9 fusion.31
  51.6 0.9 copy-done.17
  52.5 2.1 %convolution_bitcast_fusion.1 = f32[2048,256]{0,1:T(8,128)} fusion(bf16[512,256]{0,1:T(8,128)(2,1)S(1)} %bitcast.129, bf16[1,512,2048]{2,1,0:T(8,128)(2,1)S(1)} %copy-done.17), kind=kOutput, calls=%fused_computation.3 | convolution fusion | flops 536870912 | bytes 4456448 | tf_op jit(solution)/shard_map/td,tk->dk/dot_general | solution.py:83
  54.6 1.8 convolution_bitcast_fusion
  56.4 6.2 %maximum_multiply_fusion = f32[2048,1024]{0,1:T(8,128)} fusion(f32[2048,256]{0,1:T(8,128)} %convolution_bitcast_fusion.1, f32[2048,768]{0,1:T(8,128)S(1)} %convolution_bitcast_fusion), kind=kLoop, calls=%fused_computation | loop fusion | flops 4194304 | bytes 16777216 | tf_op jit(solution)/shard_map/mul | solution.py:84
  62.7 2.1 fusion.49
  64.8 0.8 fusion.48
  66.1 2.7 %add_add_fusion = f32[512,2048]{1,0:T(8,128)} fusion(f32[512,2048]{1,0:T(8,128)S(1)} %fusion.48, f32[512,2048]{1,0:T(8,128)S(1)} %fusion.49, bf16[512,256]{0,1:T(8,128)(2,1)S(1)} %bitcast.115, bf16[2048,256]{1,0:T(8,128)(2,1)S(1)} %copy-done.21), kind=kOutput, calls=%fused_computation.1 | convolution fusion | flops 538968064 | bytes 13893632 | tf_op jit(solution)/shard_map/tk,dk->td/dot_general | solution.py:73
  68.9 49.2 %reduce-scatter.8.cloned.1.call-done = f32[256,1024]{0,1:T(8,128)} async-done(((f32[2048,1024]{0,1:T(8,128)}), f32[256,1024]{0,1:T(8,128)}) %reduce-scatter.8.cloned.1.call-update) | async-done | bytes 1048592 | tf_op jit(solution)/shard_map/reduce_scatter | solution.py:85
  118.1 2.6 %copy.58 = f32[256,1024]{1,0:T(8,128)} copy(f32[256,1024]{0,1:T(8,128)} %reduce-scatter.8.cloned.1.call-done) | data formatting | bytes 2097152
  120.7 54.9 %reduce-scatter.6.cloned.1.call-done = f32[512,256]{1,0:T(8,128)} async-done(((f32[512,2048]{1,0:T(8,128)}), f32[512,256]{1,0:T(8,128)}) %reduce-scatter.6.cloned.1.call-update) | async-done | bytes 524304 | tf_op jit(solution)/shard_map/reduce_scatter | solution.py:76
  175.6 1.8 convert_bitcast_fusion
  177.4 23.4 %reduce-scatter.10.cloned.1.call-done = f32[64,1024]{1,0:T(8,128)} async-done(((f32[256,1024]{1,0:T(8,128)}), f32[64,1024]{1,0:T(8,128)}) %reduce-scatter.10.cloned.1.call-update) | async-done | bytes 262160
  200.8 1.6 slice_bitcast_fusion.2
  (64 shorter events, 5.1 us)
Async XLA Ops:
  7.2 1.6 copy-start
  7.2 3.6 %copy-start.18 = (bf16[2048,256]{1,0:T(8,128)(2,1)S(1)}, bf16[2048,256]{1,0:T(8,128)(2,1)}, u32[]{:S(2)}) copy-start(bf16[2048,256]{1,0:T(8,128)(2,1)} %param.8) | copy-start | bytes 3145732
  7.2 39.6 %all-gather.3.cloned.1.call-start = ((), (), s32[]{:S(2)}) async-start(), calls=%async_computation.5 | async-start | bytes 2359296 | tf_op jit(solution)/shard_map/all_gather | solution.py:36
  10.8 4.0 %copy-start.13 = (bf16[512,256]{0,1:T(8,128)(2,1)}, bf16[512,256]{0,1:T(8,128)(2,1)S(1)}, u32[]{:S(2)}) copy-start(bf16[512,256]{0,1:T(8,128)(2,1)S(1)} %fusion.27) | copy-start | bytes 786436
  10.8 1.3 copy-start.20
  12.1 3.0 %copy-start.10 = (bf16[512,256]{0,1:T(8,128)(2,1)}, bf16[512,256]{0,1:T(8,128)(2,1)S(1)}, u32[]{:S(2)}) copy-start(bf16[512,256]{0,1:T(8,128)(2,1)S(1)} %fusion.21) | copy-start | bytes 786436
  12.1 1.7 copy-start.16
  12.1 1.9 copy-start.22
  14.0 34.9 %copy-start.4 = (bf16[512,256]{0,1:T(8,128)(2,1)}, bf16[512,256]{0,1:T(8,128)(2,1)S(1)}, u32[]{:S(2)}) copy-start(bf16[512,256]{0,1:T(8,128)(2,1)S(1)} %fusion.24) | copy-start | bytes 786436
  14.8 1.4 copy-start.8
  16.0 102.1 %reduce-scatter.8.cloned.1.call-start = ((), (), s32[]{:S(2)}) async-start(), calls=%async_computation.4 | async-start | bytes 9437184 | tf_op jit(solution)/shard_map/reduce_scatter | solution.py:85
  16.1 1.7 copy-start.11
  16.1 1.7 copy-start.14
  46.7 1.9 copy-start.12
  46.7 2.4 %copy-start.15 = (bf16[512,256]{0,1:T(8,128)(2,1)S(1)}, bf16[512,256]{0,1:T(8,128)(2,1)}, u32[]{:S(2)}) copy-start(bf16[512,256]{0,1:T(8,128)(2,1)} %copy-done.13) | copy-start | bytes 786436
  46.8 2.7 %copy-start.9 = (bf16[512,256]{0,1:T(8,128)(2,1)S(1)}, bf16[512,256]{0,1:T(8,128)(2,1)}, u32[]{:S(2)}) copy-start(bf16[512,256]{0,1:T(8,128)(2,1)} %copy-done.8) | copy-start | bytes 786436
  50.8 3.8 %copy-start.2 = (bf16[2,128,512]{2,1,0:T(8,128)(2,1)}, bf16[2,128,512]{2,1,0:T(8,128)(2,1)S(1)}, u32[]{:S(2)}) copy-start(bf16[2,128,512]{2,1,0:T(8,128)(2,1)S(1)} %fusion.14) | copy-start | bytes 786436
  50.8 1.7 copy-start.17
  51.6 3.0 %copy-start.6 = (bf16[2,128,512]{2,1,0:T(8,128)(2,1)}, bf16[2,128,512]{2,1,0:T(8,128)(2,1)S(1)}, u32[]{:S(2)}) copy-start(bf16[2,128,512]{2,1,0:T(8,128)(2,1)S(1)} %fusion.16) | copy-start | bytes 786436
  62.6 2.2 %copy-start.3 = (bf16[2,128,512]{2,1,0:T(8,128)(2,1)S(1)}, bf16[2,128,512]{2,1,0:T(8,128)(2,1)}, u32[]{:S(2)}) copy-start(bf16[2,128,512]{2,1,0:T(8,128)(2,1)} %copy-done.2) | copy-start | bytes 786436
  62.6 113.0 %reduce-scatter.6.cloned.1.call-start = ((), (), s32[]{:S(2)}) async-start(), calls=%async_computation.3 | async-start | bytes 4718592 | tf_op jit(solution)/shard_map/reduce_scatter | solution.py:76
  62.7 2.1 %copy-start.19 = (bf16[2048,256]{1,0:T(8,128)(2,1)S(1)}, bf16[2048,256]{1,0:T(8,128)(2,1)}, u32[]{:S(2)}) copy-start(bf16[2048,256]{1,0:T(8,128)(2,1)} %param.7) | copy-start | bytes 3145732
  64.8 1.3 copy-start.21
  68.9 131.9 %reduce-scatter.10.cloned.1.call-start = ((), (), s32[]{:S(2)}) async-start(), calls=%async_computation.6 | async-start | bytes 1310720
  (3 other events, 3.1 us)
Sparse Core Ops, SparseCore 0:
  16.1 30.5 all-gather.2
  62.8 55.2 reduce-scatter.7
  120.7 54.9 reduce-scatter.5
  178.0 22.7 reduce-scatter.9

commit v2 on v1

--- a/solution.py
+++ b/solution.py
@@ -1,9 +1,76 @@
+import functools
+
 import jax
 import jax.numpy as jnp
 from jax import lax
+from jax.experimental import pallas as pl
+from jax.experimental.pallas import tpu as pltpu
 from jax.sharding import PartitionSpec as P
 
 HEAD_DIM = 128
+MESH = pl.DeviceIdType.MESH
+
+
+def ring_scatter_kernel(n, term_ref, out_ref, recv, sendbuf, send_sem, recv_sem):
+    me = lax.axis_index("head")
+    right, left = lax.rem(me + 1, n), lax.rem(me + n - 1, n)
+    half = out_ref.shape[1] // 2
+    barrier = pltpu.get_barrier_semaphore()
+    for neighbour in (left, right):
+        pl.semaphore_signal(barrier, inc=1, device_id={"head": neighbour}, device_id_type=MESH)
+    pl.semaphore_wait(barrier, 2)
+    routes = ((right, -1), (left, 1))
+    copies = [[], []]
+    for step in range(n - 1):
+        for way, (dest, sign) in enumerate(routes):
+            block = lax.rem(me + n + sign * (step + 1), n)
+            cols = pl.ds(way * half, half)
+            if step == 0:
+                src = term_ref.at[block, :, cols]
+            else:
+                copies[way][step - 1].wait_recv()
+                sendbuf[way, step] = recv[way, step - 1] + term_ref[block, :, cols]
+                src = sendbuf.at[way, step]
+            copy = pltpu.make_async_remote_copy(
+                src_ref=src,
+                dst_ref=recv.at[way, step],
+                send_sem=send_sem.at[way, step],
+                recv_sem=recv_sem.at[way, step],
+                device_id={"head": dest},
+                device_id_type=MESH,
+            )
+            copy.start()
+            copies[way].append(copy)
+    for way in range(2):
+        cols = pl.ds(way * half, half)
+        copies[way][n - 2].wait_recv()
+        out_ref[:, cols] = (recv[way, n - 2] + term_ref[me, :, cols]).astype(out_ref.dtype)
+    for way in range(2):
+        for copy in copies[way]:
+            copy.wait_send()
+
+
+def ring_scatter(terms):
+    n, rows, width = terms.shape
+    half = width // 2
+    return pl.pallas_call(
+        functools.partial(ring_scatter_kernel, n),
+        out_shape=jax.ShapeDtypeStruct((rows, width), jnp.bfloat16),
+        in_specs=[pl.BlockSpec(memory_space=pltpu.VMEM)],
+        out_specs=pl.BlockSpec(memory_space=pltpu.VMEM),
+        scratch_shapes=[
+            pltpu.VMEM((2, n - 1, rows, half), jnp.float32),
+            pltpu.VMEM((2, n - 1, rows, half), jnp.float32),
+            pltpu.SemaphoreType.DMA((2, n - 1)),
+            pltpu.SemaphoreType.DMA((2, n - 1)),
+        ],
+        compiler_params=pltpu.CompilerParams(
+            collective_id=0, has_side_effects=True, vmem_limit_bytes=48 * 1024 * 1024
+        ),
+        cost_estimate=pl.CostEstimate(
+            flops=2 * n * rows * width, bytes_accessed=8 * n * rows * width, transcendentals=0
+        ),
+    )(terms)
 
 
 def local(layer_input, w_query, w_key, w_value, w_out, out_grad):
@@ -66,23 +133,28 @@
     d_query = d_query.astype(jnp.bfloat16).reshape(num_rows, width)
     d_keys = d_keys.astype(jnp.bfloat16).reshape(num_rows, width)
     d_values = d_values.astype(jnp.bfloat16).reshape(num_rows, width)
-    head_terms = jnp.einsum("tk,dk->td", d_query, w_query, preferred_element_type=jnp.float32)
+    groups = lax.axis_size("head")
+
+    def by_block(weight):
+        return weight.reshape(groups, weight.shape[0] // groups, width)
+
+    head_terms = jnp.einsum("tk,bdk->btd", d_query, by_block(w_query), preferred_element_type=jnp.float32)
     head_terms = head_terms + jnp.einsum(
-        "tk,dk->td", d_keys, w_key, preferred_element_type=jnp.float32
+        "tk,bdk->btd", d_keys, by_block(w_key), preferred_element_type=jnp.float32
     )
     head_terms = head_terms + jnp.einsum(
-        "tk,dk->td", d_values, w_value, preferred_element_type=jnp.float32
+        "tk,bdk->btd", d_values, by_block(w_value), preferred_element_type=jnp.float32
     )
-    input_grad = lax.psum_scatter(head_terms, "head", scatter_dimension=1, tiled=True).astype(
-        jnp.bfloat16
-    )[None]
     total_rows = lax.axis_size("seq") * lax.axis_size("dp") * num_rows
     grad_scale = jnp.float32(1.0) / jnp.sqrt(jnp.float32(total_rows))
     grads = jnp.concatenate([d_query, d_keys, d_values], axis=1)
     term_qkv = jnp.einsum("td,tk->dk", in_rows, grads, preferred_element_type=jnp.float32)
     term_out = jnp.einsum("td,tk->dk", grad_rows, attention, preferred_element_type=jnp.float32)
     terms = jnp.concatenate([term_qkv, term_out], axis=1) * grad_scale
+    terms, head_terms = lax.optimization_barrier((terms, head_terms))
     summed = lax.psum_scatter(terms, "seq", scatter_dimension=0, tiled=True)
+    input_grad = ring_scatter(head_terms)[None]
+    summed, input_grad = lax.optimization_barrier((summed, input_grad))
     summed = lax.psum_scatter(summed, "dp", scatter_dimension=0, tiled=True)
     grad_query = summed[:, :width]
     grad_key = summed[:, width:2 * width]

time: 212 us -> 162 us (0.76)
  waiting for transfers between devices: 156 us -> 53.2 us
  Pallas kernels: 0 us -> 51.4 us
  local copies, waits for them, and re-layouts: 9.26 us -> 12.5 us
    reduce_scatter x1 -> x0, waiting for transfers between devices: 54.9 us -> none  [local(): lax.psum_scatter(head_terms, 'head', scatter_dimension=1, tiled=True)]
    pallas_call x0 -> x1, Pallas kernels: none -> 51.4 us  [ring_scatter(): pl.pallas_call(functools.partial(ring_scatter_kernel, n), out_shape=jax.S...]
    reduce_scatter x1, waiting for transfers between devices: 49.2 us -> 1.8 us  [local(): summed = lax.psum_scatter(terms, 'seq', scatter_dimension=0, tiled=True)]
    unnamed x47 -> x36, local copies, waits for them, and re-layouts: 7.63 us -> 10.9 us
    unnamed x5 -> x4, waiting for transfers between devices: 23.5 us -> 24 us
  transfers between devices with their start and end apart: 4 -> 3, of which waited for: 4 -> 3; matrix products, arithmetic and copies ran while one was open for 6% -> 2% of each run, Pallas kernels for 0% -> 32%
where the time goes in v2:
time: 162 us; the launch traced here: 160 us
  waiting for transfers between devices  53.2 us (33%)
  Pallas kernels  51.4 us (32%)
  matrix products  19.7 us (12%)
  between operations  14.1 us (9%)
  local copies, waits for them, and re-layouts  12.5 us (8%)
  other arithmetic  8.87 us (5%)
    pallas_call x1, Pallas kernels, ring_scatter(): pl.pallas_call(functools.partial(ring_scatter_kernel, n), out_shape=jax.S...  51.4 us
    all_gather x1, waiting for transfers between devices, local(): states = lax.all_gather(jnp.stack([kv_state, qg_state]), 'seq')  27.5 us
    unnamed x4, waiting for transfers between devices  24 us
    unnamed x36, local copies, waits for them, and re-layouts  10.9 us
    mul x1, other arithmetic, local(): terms = jnp.concatenate([term_qkv, term_out], axis=1) * grad_scale  6.19 us
    dot_general x3, matrix products, project(): jnp.dot(in_rows, weight, preferred_element_type=jnp.float32)  3.5 us
  transfers between devices with their start and end apart: 3, of which 3 were waited for; matrix products, arithmetic and copies ran while one was open for 2% of the time, Pallas kernels for 32%

profile of v2, /device:TPU:8, one launch (start us, length us, event | category | flops | bytes accessed | tf_op | source)
XLA Modules:
  0.0 159.9 jit_solution(12425924551880768777)
XLA Ops:
  7.3 1.5 copy-done
  8.8 2.0 %fusion.27 = bf16[512,256]{0,1:T(8,128)(2,1)S(1)} fusion(bf16[2048,256]{1,0:T(8,128)(2,1)} %param.7, bf16[1,512,2048]{2,1,0:T(8,128)(2,1)S(1)} %copy-done), kind=kOutput, calls=%fused_computation.29 | convolution fusion | flops 537001984 | bytes 3407872 | tf_op jit(solution)/shard_map/dot_general | solution.py:84
  10.8 0.8 fusion.21
  12.1 0.8 fusion.24
  12.9 0.9 copy-done.10
  14.0 0.8 fusion.17
  15.5 0.7 pad_maximum_fusion
  16.4 1.6 select_convert_fusion
  18.0 1.5 select_convert_fusion.1
  19.5 27.5 %all-gather.3.cloned.1.call-done = f32[16,2,128,128]{3,2,1,0:T(8,128)} async-done(((f32[2,2,128,128]{3,2,1,0:T(8,128)}), f32[16,2,128,128]{3,2,1,0:T(8,128)}) %all-gather.3.cloned.1.call-update) | async-done | bytes 2097168 | tf_op jit(solution)/shard_map/all_gather | solution.py:103
  47.0 1.9 %fusion.31 = (bf16[2,128,128]{2,1,0:T(8,128)(2,1)S(1)}, bf16[2,128,128]{2,1,0:T(8,128)(2,1)S(1)}) fusion(f32[8,2,2,128,128]{4,3,2,1,0:T(8,128)} %bitcast.139, pred[8]{0:T(512)(128)(4,1)S(1)} %get-tuple-element.29, pred[8]{0:T(512)(128)(4,1)S(1)} %get-tuple-element.30), kind=kLoop, calls=%fused_computation.34 | loop fusion | flops 983040 | bytes 2228240 | tf_op jit(solution)/shard_map/reduce_sum | solution.py:106
  50.9 2.1 %convolution_bitcast_fusion.1 = f32[2048,256]{0,1:T(8,128)} fusion(bf16[512,256]{0,1:T(8,128)(2,1)S(1)} %bitcast.140, bf16[1,512,2048]{2,1,0:T(8,128)(2,1)S(1)} %copy-done.11), kind=kOutput, calls=%fused_computation.3 | convolution fusion | flops 536870912 | bytes 4456448 | tf_op jit(solution)/shard_map/td,tk->dk/dot_general | solution.py:152
  53.3 0.9 copy-done.2
  55.0 1.8 %convolution_bitcast_fusion = f32[2048,768]{0,1:T(8,128)S(1)} fusion(bf16[1,512,2048]{2,1,0:T(8,128)(2,1)S(1)} %copy-done, bf16[512,256]{0,1:T(8,128)(2,1)S(1)} %bitcast.121, bf16[512,256]{0,1:T(8,128)(2,1)S(1)} %bitcast.135, bf16[512,256]{0,1:T(8,128)(2,1)S(1)} %bitcast.137), kind=kOutput, calls=%fused_computation.2 | convolution fusion | flops 1612972032 | bytes 9175040 | tf_op jit(solution)/shard_map/td,tk->dk/dot_general | solution.py:151
  56.8 6.2 %maximum_multiply_fusion = f32[2048,1024]{0,1:T(8,128)} fusion(f32[2048,256]{0,1:T(8,128)} %convolution_bitcast_fusion.1, f32[2048,768]{0,1:T(8,128)S(1)} %convolution_bitcast_fusion), kind=kLoop, calls=%fused_computation | loop fusion | flops 4194304 | bytes 16777216 | tf_op jit(solution)/shard_map/mul | solution.py:153
  63.0 2.1 %fusion.48 = f32[512,8,256]{2,0,1:T(8,128)S(1)} fusion(bf16[512,256,1]{0,1,2:T(8,128)(2,1)S(1)} %bitcast.138, bf16[8,256,256]{2,1,0:T(8,128)(2,1)} %bitcast.141), kind=kOutput, calls=%fused_computation.58 | convolution fusion | flops 536870912 | bytes 5505024 | tf_op jit(solution)/shard_map/tk,bdk->btd/dot_general | solution.py:141
  65.1 0.8 fusion.49
  66.3 2.7 %add_bitcast_fusion.term_ref = f32[8,512,256]{2,1,0:T(8,128)} fusion(f32[512,8,256]{2,0,1:T(8,128)S(1)} %fusion.48, f32[512,8,256]{2,0,1:T(8,128)S(1)} %fusion.49, bf16[512,256,1]{0,1,2:T(8,128)(2,1)S(1)} %bitcast.122, bf16[8,256,256]{2,1,0:T(8,128)(2,1)S(1)} %bitcast.143), kind=kOutput, calls=%fused_computation.1 | convolution fusion | flops 538968064 | bytes 13893632 | tf_op jit(solution)/shard_map/tk,bdk->btd/dot_general | solution.py:145
  69.2 2.2 %copy-done.1 = f32[8,512,256]{2,1,0:T(8,128)S(1)} copy-done((f32[8,512,256]{2,1,0:T(8,128)S(1)}, f32[8,512,256]{2,1,0:T(8,128)}, u32[]{:S(2)}) %copy-start.1) | copy-done | bytes 4194328
  71.3 51.4 %shard_map.101 = bf16[512,256]{1,0:T(8,128)(2,1)S(1)} custom-call(f32[8,512,256]{2,1,0:T(8,128)S(1)} %copy-done.1), custom_call_target="tpu_custom_call" | custom-call | flops 2097152 | bytes 8388608 | tf_op jit(solution)/shard_map/pallas_call | solution.py:56
  122.7 1.8 %reduce-scatter.5.cloned.1.call-done = f32[256,1024]{0,1:T(8,128)} async-done(((f32[2048,1024]{0,1:T(8,128)}), f32[256,1024]{0,1:T(8,128)}) %reduce-scatter.5.cloned.1.call-update) | async-done | bytes 1048592 | tf_op jit(solution)/shard_map/reduce_scatter | solution.py:155
  124.5 2.5 %copy.70 = f32[256,1024]{1,0:T(8,128)} copy(f32[256,1024]{0,1:T(8,128)} %reduce-scatter.5.cloned.1.call-done) | data formatting | bytes 2097152
  127.1 23.9 %reduce-scatter.7.cloned.1.call-done = f32[64,1024]{1,0:T(8,128)} async-done(((f32[256,1024]{1,0:T(8,128)}), f32[64,1024]{1,0:T(8,128)}) %reduce-scatter.7.cloned.1.call-update) | async-done | bytes 262160
  151.0 1.6 %slice_bitcast_fusion.2 = (f32[256,64]{0,1:T(8,128)}, f32[64,256]{1,0:T(8,128)}, f32[64,256]{1,0:T(8,128)}, f32[64,256]{1,0:T(8,128)}) fusion(f32[64,1024]{1,0:T(8,128)} %reduce-scatter.7.cloned.1.call-done), kind=kLoop, calls=%fused_computation.45 | loop fusion | bytes 524288 | tf_op jit(solution)/shard_map/transpose | solution.py:162
  (50 shorter events, 6.0 us)
Async XLA Ops:
  7.2 1.6 copy-start
  7.2 3.6 %copy-start.12 = (bf16[2048,256]{1,0:T(8,128)(2,1)S(1)}, bf16[2048,256]{1,0:T(8,128)(2,1)}, u32[]{:S(2)}) copy-start(bf16[2048,256]{1,0:T(8,128)(2,1)} %param.8) | copy-start | bytes 3145732
  7.2 39.8 %all-gather.3.cloned.1.call-start = ((), (), s32[]{:S(2)}) async-start(), calls=%async_computation.3 | async-start | bytes 2359296 | tf_op jit(solution)/shard_map/all_gather | solution.py:103
  10.8 4.1 %copy-start.5 = (bf16[512,256]{0,1:T(8,128)(2,1)}, bf16[512,256]{0,1:T(8,128)(2,1)S(1)}, u32[]{:S(2)}) copy-start(bf16[512,256]{0,1:T(8,128)(2,1)S(1)} %fusion.27) | copy-start | bytes 786436
  10.8 1.3 copy-start.14
  12.1 3.0 %copy-start.3 = (bf16[512,256]{0,1:T(8,128)(2,1)}, bf16[512,256]{0,1:T(8,128)(2,1)S(1)}, u32[]{:S(2)}) copy-start(bf16[512,256]{0,1:T(8,128)(2,1)S(1)} %fusion.21) | copy-start | bytes 786436
  12.1 1.7 %copy-start.10 = (bf16[1,512,2048]{2,1,0:T(8,128)(2,1)S(1)}, bf16[1,512,2048]{2,1,0:T(8,128)(2,1)}, u32[]{:S(2)}) copy-start(bf16[1,512,2048]{2,1,0:T(8,128)(2,1)} %param.11) | copy-start | bytes 6291460
  12.1 1.9 %copy-start.16 = (bf16[256,2048]{1,0:T(8,128)(2,1)S(1)}, bf16[256,2048]{1,0:T(8,128)(2,1)}, u32[]{:S(2)}) copy-start(bf16[256,2048]{1,0:T(8,128)(2,1)} %param.10) | copy-start | bytes 3145732
  14.8 0.7 copy-start.7
  16.2 108.3 %reduce-scatter.5.cloned.1.call-start = ((), (), s32[]{:S(2)}) async-start(), calls=%async_computation.2 | async-start | bytes 9437184 | tf_op jit(solution)/shard_map/reduce_scatter | solution.py:155
  16.3 1.7 %copy-start.8 = (bf16[512,256]{0,1:T(8,128)(2,1)S(1)}, bf16[512,256]{0,1:T(8,128)(2,1)}, u32[]{:S(2)}) copy-start(bf16[512,256]{0,1:T(8,128)(2,1)} %copy-done.7) | copy-start | bytes 786436
  47.0 1.9 %copy-start.4 = (bf16[512,256]{0,1:T(8,128)(2,1)S(1)}, bf16[512,256]{0,1:T(8,128)(2,1)}, u32[]{:S(2)}) copy-start(bf16[512,256]{0,1:T(8,128)(2,1)} %copy-done.3) | copy-start | bytes 786436
  47.0 2.4 %copy-start.6 = (bf16[512,256]{0,1:T(8,128)(2,1)S(1)}, bf16[512,256]{0,1:T(8,128)(2,1)}, u32[]{:S(2)}) copy-start(bf16[512,256]{0,1:T(8,128)(2,1)} %copy-done.5) | copy-start | bytes 786436
  47.0 2.6 %copy-start.9 = (bf16[512,256]{0,1:T(8,128)(2,1)S(1)}, bf16[512,256]{0,1:T(8,128)(2,1)}, u32[]{:S(2)}) copy-start(bf16[512,256]{0,1:T(8,128)(2,1)} %copy-done.7) | copy-start | bytes 786436
  49.3 1.6 copy-start.11
  53.0 1.2 copy-start.2
  63.0 2.1 %copy-start.13 = (bf16[2048,256]{1,0:T(8,128)(2,1)S(1)}, bf16[2048,256]{1,0:T(8,128)(2,1)}, u32[]{:S(2)}) copy-start(bf16[2048,256]{1,0:T(8,128)(2,1)} %param.8) | copy-start | bytes 3145732
  65.1 1.2 copy-start.15
  69.1 81.9 %reduce-scatter.7.cloned.1.call-start = ((), (), s32[]{:S(2)}) async-start(), calls=%async_computation.4 | async-start | bytes 1310720
  69.2 2.2 %copy-start.1 = (f32[8,512,256]{2,1,0:T(8,128)S(1)}, f32[8,512,256]{2,1,0:T(8,128)}, u32[]{:S(2)}) copy-start(f32[8,512,256]{2,1,0:T(8,128)} %add_bitcast_fusion.term_ref) | copy-start | bytes 12582916
Sparse Core Ops, SparseCore 0:
  16.4 30.5 all-gather.2
  69.2 55.2 reduce-scatter.4
  127.2 23.7 reduce-scatter.6

commit v3 on v2

--- a/solution.py
+++ b/solution.py
@@ -73,6 +73,24 @@
     )(terms)
 
 
+def exclusive_scan(x, axis, reverse):
+    peers = lax.axis_size(axis)
+    span = x
+    total = None
+    reach = 1
+    while reach < peers:
+        if reverse:
+            pairs = [(j, j - reach) for j in range(reach, peers)]
+        else:
+            pairs = [(j, j + reach) for j in range(peers - reach)]
+        arrived = lax.ppermute(span, axis, pairs)
+        total = arrived if total is None else total + arrived
+        if reach * 2 < peers:
+            span = span + arrived
+        reach *= 2
+    return total
+
+
 def local(layer_input, w_query, w_key, w_value, w_out, out_grad):
     num_rows = layer_input.shape[1]
     local_heads = w_query.shape[1] // HEAD_DIM
@@ -87,9 +105,7 @@
     queries = project(w_query)
     key_rows = project(w_key)
     value_rows = project(w_value)
-    here = lax.axis_index("seq")
-    peers = lax.axis_size("seq")
-    row_start = here * num_rows
+    row_start = lax.axis_index("seq") * num_rows
     positions = (row_start + jnp.arange(num_rows, dtype=jnp.int32)).astype(jnp.float32)
     pos_scale = 1.0 / jnp.sqrt(HEAD_DIM * (positions + 1.0))
     backward = jnp.einsum("td,kd->tk", grad_rows, w_out, preferred_element_type=jnp.float32)
@@ -100,10 +116,8 @@
     )
     kv_state = jnp.einsum("thd,the->hde", key_rows, value_rows, preferred_element_type=jnp.float32)
     qg_state = jnp.einsum("thd,the->hde", queries, grad_in, preferred_element_type=jnp.float32)
-    states = lax.all_gather(jnp.stack([kv_state, qg_state]), "seq")
-    blocks = jnp.arange(peers)[:, None, None, None]
-    prefix = jnp.sum(jnp.where(blocks < here, states[:, 0], 0.0), axis=0).astype(jnp.bfloat16)
-    suffix = jnp.sum(jnp.where(blocks > here, states[:, 1], 0.0), axis=0).astype(jnp.bfloat16)
+    prefix = exclusive_scan(kv_state, "seq", False).astype(jnp.bfloat16)
+    suffix = exclusive_scan(qg_state, "seq", True).astype(jnp.bfloat16)
     causal = (jnp.arange(num_rows)[:, None] >= jnp.arange(num_rows)[None, :])[None]
     scores = jnp.einsum("thd,shd->hts", queries, key_rows, preferred_element_type=jnp.float32)
     scores_qk = jnp.where(causal, scores, 0.0).astype(jnp.bfloat16)

time: 162 us -> 152 us (0.938)
  waiting for transfers between devices: 53.2 us -> 26.8 us
  starting transfers between devices: 0.12 us -> 17.4 us
  Pallas kernels: 51.4 us -> 56.1 us
  local copies, waits for them, and re-layouts: 12.5 us -> 9.08 us
  other arithmetic: 8.87 us -> 6.39 us
    all_gather x1 -> x0, waiting for transfers between devices: 27.5 us -> none  [local(): states = lax.all_gather(jnp.stack([kv_state, qg_state]), 'seq')]
    ppermute x0 -> x6, starting transfers between devices: none -> 17.3 us  [exclusive_scan(): arrived = lax.ppermute(span, axis, pairs)]
    ppermute x0 -> x6, waiting for transfers between devices: none -> 5.65 us  [exclusive_scan(): arrived = lax.ppermute(span, axis, pairs)]
    pallas_call x1, Pallas kernels: 51.4 us -> 56.1 us  [ring_scatter(): pl.pallas_call(functools.partial(ring_scatter_kernel, n), out_shape=jax.S...]
    unnamed x36 -> x16, local copies, waits for them, and re-layouts: 10.9 us -> 7.45 us
    unnamed x4 -> x3, waiting for transfers between devices: 24 us -> 21.1 us
    reduce_sum x1 -> x0, other arithmetic: 1.86 us -> none  [local(): jnp.sum(jnp.where(blocks > here, states[:, 1], 0.0), axis=0)]
    dot_general x1, matrix products: 0.76 us -> 2.6 us  [local(): jnp.einsum('td,kd->tk', grad_rows, w_out, preferred_element_type=jnp.floa...]
  transfers between devices with their start and end apart: 3 -> 8, of which waited for: 3 -> 4; matrix products, arithmetic and copies ran while one was open for 2% -> 6% of each run, Pallas kernels for 32% -> 37%
where the time goes in v3:
time: 152 us; the launch traced here: 150 us
  Pallas kernels  56.1 us (37%)
  waiting for transfers between devices  26.8 us (18%)
  matrix products  19.7 us (13%)
  starting transfers between devices  17.4 us (11%)
  between operations  14.4 us (9%)
  local copies, waits for them, and re-layouts  9.08 us (6%)
  other arithmetic  6.39 us (4%)
    pallas_call x1, Pallas kernels, ring_scatter(): pl.pallas_call(functools.partial(ring_scatter_kernel, n), out_shape=jax.S...  56.1 us
    unnamed x3, waiting for transfers between devices  21.1 us
    ppermute x6, starting transfers between devices, exclusive_scan(): arrived = lax.ppermute(span, axis, pairs)  17.3 us
    unnamed x16, local copies, waits for them, and re-layouts  7.45 us
    mul x1, other arithmetic, local(): terms = jnp.concatenate([term_qkv, term_out], axis=1) * grad_scale  6.19 us
    ppermute x6, waiting for transfers between devices, exclusive_scan(): arrived = lax.ppermute(span, axis, pairs)  5.65 us
    dot_general x3, matrix products, project(): jnp.dot(in_rows, weight, preferred_element_type=jnp.float32)  3.61 us
  transfers between devices with their start and end apart: 8, of which 4 were waited for; matrix products, arithmetic and copies ran while one was open for 6% of the time, Pallas kernels for 37%

profile of v3, /device:TPU:8, one launch (start us, length us, event | category | flops | bytes accessed | tf_op | source)
XLA Modules:
  0.0 149.8 jit_solution(14201027176558316650)
XLA Ops:
  7.2 1.5 %copy-done = bf16[1,512,2048]{2,1,0:T(8,128)(2,1)S(1)} copy-done((bf16[1,512,2048]{2,1,0:T(8,128)(2,1)S(1)}, bf16[1,512,2048]{2,1,0:T(8,128)(2,1)}, u32[]{:S(2)}) %copy-start) | copy-done | bytes 2097176
  8.8 2.1 %fusion.21 = bf16[512,256]{0,1:T(8,128)(2,1)S(1)} fusion(bf16[2048,256]{1,0:T(8,128)(2,1)} %param.9, bf16[1,512,2048]{2,1,0:T(8,128)(2,1)S(1)} %copy-done), kind=kOutput, calls=%fused_computation.25 | convolution fusion | flops 537001984 | bytes 3407872 | tf_op jit(solution)/shard_map/dot_general | solution.py:102
  10.9 0.8 fusion.18
  11.9 1.7 %collective-permute-start = (f32[2,128,128]{2,1,0:T(8,128)S(1)}, f32[2,128,128]{2,1,0:T(8,128)S(1)}, u32[]{:S(2)}, u32[]{:S(2)}) collective-permute-start(f32[2,128,128]{2,1,0:T(8,128)S(1)} %fusion.37), channel_id=1, source_target_pairs={{0,32},{32,64},{64,96},{96,128},{128,160},{160,192},{192,224},{1,3... | collective-permute-start | bytes 393224 | tf_op jit(solution)/shard_map/ppermute | solution.py:86
  13.6 0.8 fusion.24
  14.4 2.6 %fusion.14 = bf16[512,256]{0,1:T(8,128)(2,1)S(1)} fusion(bf16[256,2048]{1,0:T(8,128)(2,1)} %param.10, bf16[1,512,2048]{2,1,0:T(8,128)(2,1)} %param.11, f32[512]{0:T(512)S(1)} %multiply_rsqrt_fusion), kind=kOutput, calls=%fused_computation.22 | convolution fusion | flops 537133056 | bytes 3409920 | tf_op jit(solution)/shard_map/td,kd->tk/dot_general | solution.py:111
  17.3 1.3 collective-permute-start.3
  20.6 5.9 %collective-permute-start.1 = (f32[2,128,128]{2,1,0:T(8,128)S(1)}, f32[2,128,128]{2,1,0:T(8,128)S(1)}, u32[]{:S(2)}, u32[]{:S(2)}) collective-permute-start(f32[2,128,128]{2,1,0:T(8,128)S(1)} %add.82), channel_id=1, source_target_pairs={{0,64},{32,96},{64,128},{96,160},{128,192},{160,224},{1,65},{33,97... | collective-permute-start | bytes 393224 | tf_op jit(solution)/shard_map/ppermute | solution.py:86
  26.8 1.4 collective-permute-start.4
  28.3 1.0 collective-permute-done.1
  29.3 5.6 %collective-permute-start.2 = (f32[2,128,128]{2,1,0:T(8,128)S(1)}, f32[2,128,128]{2,1,0:T(8,128)S(1)}, u32[]{:S(2)}, u32[]{:S(2)}) collective-permute-start(f32[2,128,128]{2,1,0:T(8,128)S(1)} %add.84), channel_id=1, source_target_pairs={{0,128},{32,160},{64,192},{96,224},{1,129},{33,161},{65,193},{97,2... | collective-permute-start | bytes 393224 | tf_op jit(solution)/shard_map/ppermute | solution.py:86
  35.4 1.3 collective-permute-start.5
  37.7 2.1 %convolution_bitcast_fusion.1 = f32[2048,256]{0,1:T(8,128)} fusion(bf16[512,256]{0,1:T(8,128)(2,1)S(1)} %bitcast.118, bf16[1,512,2048]{2,1,0:T(8,128)(2,1)S(1)} %copy-done.2), kind=kOutput, calls=%fused_computation.3 | convolution fusion | flops 536870912 | bytes 4456448 | tf_op jit(solution)/shard_map/td,tk->dk/dot_general | solution.py:166
  39.8 4.0 %collective-permute-done.5 = f32[2,128,128]{2,1,0:T(8,128)S(1)} collective-permute-done((f32[2,128,128]{2,1,0:T(8,128)S(1)}, f32[2,128,128]{2,1,0:T(8,128)S(1)}, u32[]{:S(2)}, u32[]{:S(2)}) %collective-permute-start.5) | collective-permute-done | bytes 131104 | tf_op jit(solution)/shard_map/ppermute | solution.py:86
  44.5 1.8 %convolution_bitcast_fusion = f32[2048,768]{0,1:T(8,128)S(1)} fusion(bf16[1,512,2048]{2,1,0:T(8,128)(2,1)S(1)} %copy-done, bf16[512,256]{0,1:T(8,128)(2,1)S(1)} %bitcast.96, bf16[512,256]{0,1:T(8,128)(2,1)S(1)} %bitcast.114, bf16[512,256]{0,1:T(8,128)(2,1)S(1)} %bitcast.116), kind=kOutput, calls=%fused_computation.2 | convolution fusion | flops 1612972032 | bytes 9175040 | tf_op jit(solution)/shard_map/td,tk->dk/dot_general | solution.py:165
  46.3 6.2 %maximum_multiply_fusion = f32[2048,1024]{0,1:T(8,128)} fusion(f32[2048,256]{0,1:T(8,128)} %convolution_bitcast_fusion.1, f32[2048,768]{0,1:T(8,128)S(1)} %convolution_bitcast_fusion), kind=kLoop, calls=%fused_computation | loop fusion | flops 4194304 | bytes 16777216 | tf_op jit(solution)/shard_map/mul | solution.py:167
  52.5 2.1 %fusion.42 = f32[512,8,256]{2,0,1:T(8,128)S(1)} fusion(bf16[512,256,1]{0,1,2:T(8,128)(2,1)S(1)} %bitcast.117, bf16[8,256,256]{2,1,0:T(8,128)(2,1)} %bitcast.119), kind=kOutput, calls=%fused_computation.47 | convolution fusion | flops 536870912 | bytes 5505024 | tf_op jit(solution)/shard_map/tk,bdk->btd/dot_general | solution.py:155
  54.6 0.8 fusion.43
  55.8 2.7 %add_bitcast_fusion.term_ref = f32[8,512,256]{2,1,0:T(8,128)} fusion(f32[512,8,256]{2,0,1:T(8,128)S(1)} %fusion.42, f32[512,8,256]{2,0,1:T(8,128)S(1)} %fusion.43, bf16[512,256,1]{0,1,2:T(8,128)(2,1)S(1)} %bitcast.97, bf16[8,256,256]{2,1,0:T(8,128)(2,1)S(1)} %bitcast.121), kind=kOutput, calls=%fused_computation.1 | convolution fusion | flops 538968064 | bytes 13893632 | tf_op jit(solution)/shard_map/tk,bdk->btd/dot_general | solution.py:159
  58.6 2.2 %copy-done.1 = f32[8,512,256]{2,1,0:T(8,128)S(1)} copy-done((f32[8,512,256]{2,1,0:T(8,128)S(1)}, f32[8,512,256]{2,1,0:T(8,128)}, u32[]{:S(2)}) %copy-start.1) | copy-done | bytes 4194328
  60.8 56.1 %shard_map.101 = bf16[512,256]{1,0:T(8,128)(2,1)S(1)} custom-call(f32[8,512,256]{2,1,0:T(8,128)S(1)} %copy-done.1), custom_call_target="tpu_custom_call" | custom-call | flops 2097152 | bytes 8388608 | tf_op jit(solution)/shard_map/pallas_call | solution.py:56
  116.9 2.5 %copy.67 = f32[256,1024]{1,0:T(8,128)} copy(f32[256,1024]{0,1:T(8,128)} %reduce-scatter.5.cloned.1.call-done) | data formatting | bytes 2097152
  119.5 21.1 %reduce-scatter.7.cloned.1.call-done = f32[64,1024]{1,0:T(8,128)} async-done(((f32[256,1024]{1,0:T(8,128)}), f32[64,1024]{1,0:T(8,128)}) %reduce-scatter.7.cloned.1.call-update) | async-done | bytes 262160
  140.6 1.6 %slice_bitcast_fusion = (f32[256,64]{0,1:T(8,128)}, f32[64,256]{1,0:T(8,128)}, f32[64,256]{1,0:T(8,128)}, f32[64,256]{1,0:T(8,128)}) fusion(f32[64,1024]{1,0:T(8,128)} %reduce-scatter.7.cloned.1.call-done), kind=kLoop, calls=%fused_computation.38 | loop fusion | bytes 524288 | tf_op jit(solution)/shard_map/transpose | solution.py:176
  (42 shorter events, 6.2 us)
Async XLA Ops:
  7.2 1.6 %copy-start = (bf16[1,512,2048]{2,1,0:T(8,128)(2,1)S(1)}, bf16[1,512,2048]{2,1,0:T(8,128)(2,1)}, u32[]{:S(2)}) copy-start(bf16[1,512,2048]{2,1,0:T(8,128)(2,1)} %param.6) | copy-start | bytes 6291460
  7.2 109.8 %reduce-scatter.5.cloned.1.call-start = ((), (), s32[]{:S(2)}) async-start(), calls=%async_computation.2 | async-start | bytes 9437184 | tf_op jit(solution)/shard_map/reduce_scatter | solution.py:169
  8.8 2.1 %copy-start.4 = (bf16[2048,256]{1,0:T(8,128)(2,1)S(1)}, bf16[2048,256]{1,0:T(8,128)(2,1)}, u32[]{:S(2)}) copy-start(bf16[2048,256]{1,0:T(8,128)(2,1)} %param.8) | copy-start | bytes 3145732
  10.8 2.8 %copy-start.3 = (bf16[2048,256]{1,0:T(8,128)(2,1)S(1)}, bf16[2048,256]{1,0:T(8,128)(2,1)}, u32[]{:S(2)}) copy-start(bf16[2048,256]{1,0:T(8,128)(2,1)} %param.7) | copy-start | bytes 3145732
  11.9 8.7 %collective-permute-start = (f32[2,128,128]{2,1,0:T(8,128)S(1)}, f32[2,128,128]{2,1,0:T(8,128)S(1)}, u32[]{:S(2)}, u32[]{:S(2)}) collective-permute-start(f32[2,128,128]{2,1,0:T(8,128)S(1)} %fusion.37), channel_id=1, source_target_pairs={{0,32},{32,64},{64,96},{96,128},{128,160},{160,192},{192,224},{1,3... | collective-permute-start | bytes 393224 | tf_op jit(solution)/shard_map/ppermute | solution.py:86
  17.3 9.5 %collective-permute-start.3 = (f32[2,128,128]{2,1,0:T(8,128)S(1)}, f32[2,128,128]{2,1,0:T(8,128)S(1)}, u32[]{:S(2)}, u32[]{:S(2)}) collective-permute-start(f32[2,128,128]{2,1,0:T(8,128)S(1)} %fusion.39), channel_id=1, source_target_pairs={{32,0},{64,32},{96,64},{128,96},{160,128},{192,160},{224,192},{33,... | collective-permute-start | bytes 393224 | tf_op jit(solution)/shard_map/ppermute | solution.py:86
  20.6 8.7 %collective-permute-start.1 = (f32[2,128,128]{2,1,0:T(8,128)S(1)}, f32[2,128,128]{2,1,0:T(8,128)S(1)}, u32[]{:S(2)}, u32[]{:S(2)}) collective-permute-start(f32[2,128,128]{2,1,0:T(8,128)S(1)} %add.82), channel_id=1, source_target_pairs={{0,64},{32,96},{64,128},{96,160},{128,192},{160,224},{1,65},{33,97... | collective-permute-start | bytes 393224 | tf_op jit(solution)/shard_map/ppermute | solution.py:86
  26.8 10.9 %copy-start.2 = (bf16[1,512,2048]{2,1,0:T(8,128)(2,1)S(1)}, bf16[1,512,2048]{2,1,0:T(8,128)(2,1)}, u32[]{:S(2)}) copy-start(bf16[1,512,2048]{2,1,0:T(8,128)(2,1)} %param.11) | copy-start | bytes 6291460
  26.8 8.6 %collective-permute-start.4 = (f32[2,128,128]{2,1,0:T(8,128)S(1)}, f32[2,128,128]{2,1,0:T(8,128)S(1)}, u32[]{:S(2)}, u32[]{:S(2)}) collective-permute-start(f32[2,128,128]{2,1,0:T(8,128)S(1)} %add.87), channel_id=1, source_target_pairs={{64,0},{96,32},{128,64},{160,96},{192,128},{224,160},{65,1},{97,33... | collective-permute-start | bytes 393224 | tf_op jit(solution)/shard_map/ppermute | solution.py:86
  29.3 8.1 %collective-permute-start.2 = (f32[2,128,128]{2,1,0:T(8,128)S(1)}, f32[2,128,128]{2,1,0:T(8,128)S(1)}, u32[]{:S(2)}, u32[]{:S(2)}) collective-permute-start(f32[2,128,128]{2,1,0:T(8,128)S(1)} %add.84), channel_id=1, source_target_pairs={{0,128},{32,160},{64,192},{96,224},{1,129},{33,161},{65,193},{97,2... | collective-permute-start | bytes 393224 | tf_op jit(solution)/shard_map/ppermute | solution.py:86
  35.4 8.4 %collective-permute-start.5 = (f32[2,128,128]{2,1,0:T(8,128)S(1)}, f32[2,128,128]{2,1,0:T(8,128)S(1)}, u32[]{:S(2)}, u32[]{:S(2)}) collective-permute-start(f32[2,128,128]{2,1,0:T(8,128)S(1)} %add.89), channel_id=1, source_target_pairs={{128,0},{160,32},{192,64},{224,96},{129,1},{161,33},{193,65},{225,... | collective-permute-start | bytes 393224 | tf_op jit(solution)/shard_map/ppermute | solution.py:86
  52.5 2.1 %copy-start.5 = (bf16[2048,256]{1,0:T(8,128)(2,1)S(1)}, bf16[2048,256]{1,0:T(8,128)(2,1)}, u32[]{:S(2)}) copy-start(bf16[2048,256]{1,0:T(8,128)(2,1)} %param.8) | copy-start | bytes 3145732
  54.6 1.2 copy-start.6
  58.6 82.0 %reduce-scatter.7.cloned.1.call-start = ((), (), s32[]{:S(2)}) async-start(), calls=%async_computation.3 | async-start | bytes 1310720
  58.6 2.2 %copy-start.1 = (f32[8,512,256]{2,1,0:T(8,128)S(1)}, f32[8,512,256]{2,1,0:T(8,128)}, u32[]{:S(2)}) copy-start(f32[8,512,256]{2,1,0:T(8,128)} %add_bitcast_fusion.term_ref) | copy-start | bytes 12582916
Sparse Core Ops, SparseCore 0:
  58.7 55.3 reduce-scatter.4
  119.6 20.9 reduce-scatter.6

commit v4 on v3

--- a/solution.py
+++ b/solution.py
@@ -11,13 +11,13 @@
 MESH = pl.DeviceIdType.MESH
 
 
-def ring_scatter_kernel(n, term_ref, out_ref, recv, sendbuf, send_sem, recv_sem):
-    me = lax.axis_index("head")
+def ring_scatter_kernel(n, axis, term_ref, out_ref, recv, sendbuf, send_sem, recv_sem):
+    me = lax.axis_index(axis)
     right, left = lax.rem(me + 1, n), lax.rem(me + n - 1, n)
     half = out_ref.shape[1] // 2
     barrier = pltpu.get_barrier_semaphore()
     for neighbour in (left, right):
-        pl.semaphore_signal(barrier, inc=1, device_id={"head": neighbour}, device_id_type=MESH)
+        pl.semaphore_signal(barrier, inc=1, device_id={axis: neighbour}, device_id_type=MESH)
     pl.semaphore_wait(barrier, 2)
     routes = ((right, -1), (left, 1))
     copies = [[], []]
@@ -36,7 +36,7 @@
                 dst_ref=recv.at[way, step],
                 send_sem=send_sem.at[way, step],
                 recv_sem=recv_sem.at[way, step],
-                device_id={"head": dest},
+                device_id={axis: dest},
                 device_id_type=MESH,
             )
             copy.start()
@@ -50,12 +50,12 @@
             copy.wait_send()
 
 
-def ring_scatter(terms):
+def ring_scatter(terms, axis, out_dtype, channel):
     n, rows, width = terms.shape
     half = width // 2
     return pl.pallas_call(
-        functools.partial(ring_scatter_kernel, n),
-        out_shape=jax.ShapeDtypeStruct((rows, width), jnp.bfloat16),
+        functools.partial(ring_scatter_kernel, n, axis),
+        out_shape=jax.ShapeDtypeStruct((rows, width), out_dtype),
         in_specs=[pl.BlockSpec(memory_space=pltpu.VMEM)],
         out_specs=pl.BlockSpec(memory_space=pltpu.VMEM),
         scratch_shapes=[
@@ -65,7 +65,7 @@
             pltpu.SemaphoreType.DMA((2, n - 1)),
         ],
         compiler_params=pltpu.CompilerParams(
-            collective_id=0, has_side_effects=True, vmem_limit_bytes=48 * 1024 * 1024
+            collective_id=channel, has_side_effects=True, vmem_limit_bytes=48 * 1024 * 1024
         ),
         cost_estimate=pl.CostEstimate(
             flops=2 * n * rows * width, bytes_accessed=8 * n * rows * width, transcendentals=0
@@ -167,9 +167,12 @@
     terms = jnp.concatenate([term_qkv, term_out], axis=1) * grad_scale
     terms, head_terms = lax.optimization_barrier((terms, head_terms))
     summed = lax.psum_scatter(terms, "seq", scatter_dimension=0, tiled=True)
-    input_grad = ring_scatter(head_terms)[None]
+    input_grad = ring_scatter(head_terms, "head", jnp.bfloat16, 0)[None]
     summed, input_grad = lax.optimization_barrier((summed, input_grad))
-    summed = lax.psum_scatter(summed, "dp", scatter_dimension=0, tiled=True)
+    shares = lax.axis_size("dp")
+    summed = ring_scatter(
+        summed.reshape(shares, summed.shape[0] // shares, summed.shape[1]), "dp", jnp.float32, 1
+    )
     grad_query = summed[:, :width]
     grad_key = summed[:, width:2 * width]
     grad_value = summed[:, 2 * width:3 * width]

time: 152 us -> 143 us (0.941)
  waiting for transfers between devices: 26.8 us -> 5.52 us
  Pallas kernels: 56.1 us -> 71.3 us
  local copies, waits for them, and re-layouts: 9.08 us -> 7.16 us
    unnamed x3 -> x1, waiting for transfers between devices: 21.1 us -> 0.02 us
    pallas_call x1 -> x2, Pallas kernels: 56.1 us -> 71.3 us  [ring_scatter(): pl.pallas_call(functools.partial(ring_scatter_kernel, n, axis), out_shape...]
    unnamed x16 -> x15, local copies, waits for them, and re-layouts: 7.45 us -> 4.9 us
    optimization_barrier x0 -> x1, local copies, waits for them, and re-layouts: none -> 1.56 us  [local(): summed, input_grad = lax.optimization_barrier((summed, input_grad))]
  transfers between devices with their start and end apart: 8 -> 7, of which waited for: 4 -> 3; matrix products, arithmetic and copies ran while one was open for 6% -> 6% of each run, Pallas kernels for 37% -> 39%
where the time goes in v4:
time: 143 us; the launch traced here: 142 us
  Pallas kernels  71.3 us (50%)
  matrix products  19.7 us (14%)
  starting transfers between devices  17.5 us (12%)
  between operations  14.4 us (10%)
  local copies, waits for them, and re-layouts  7.16 us (5%)
  other arithmetic  6.39 us (4%)
  waiting for transfers between devices  5.52 us (4%)
    pallas_call x2, Pallas kernels, ring_scatter(): pl.pallas_call(functools.partial(ring_scatter_kernel, n, axis), out_shape...  71.3 us
    ppermute x6, starting transfers between devices, exclusive_scan(): arrived = lax.ppermute(span, axis, pairs)  17.5 us
    mul x1, other arithmetic, local(): terms = jnp.concatenate([term_qkv, term_out], axis=1) * grad_scale  6.19 us
    ppermute x6, waiting for transfers between devices, exclusive_scan(): arrived = lax.ppermute(span, axis, pairs)  5.48 us
    unnamed x15, local copies, waits for them, and re-layouts  4.9 us
    dot_general x3, matrix products, project(): jnp.dot(in_rows, weight, preferred_element_type=jnp.float32)  3.61 us
  transfers between devices with their start and end apart: 7, of which 3 were waited for; matrix products, arithmetic and copies ran while one was open for 6% of the time, Pallas kernels for 39%

profile of v4, /device:TPU:8, one launch (start us, length us, event | category | flops | bytes accessed | tf_op | source)
XLA Modules:
  0.0 142.0 jit_solution(12220068215292587280)
XLA Ops:
  7.2 1.5 %copy-done = bf16[1,512,2048]{2,1,0:T(8,128)(2,1)S(1)} copy-done((bf16[1,512,2048]{2,1,0:T(8,128)(2,1)S(1)}, bf16[1,512,2048]{2,1,0:T(8,128)(2,1)}, u32[]{:S(2)}) %copy-start) | copy-done | bytes 2097176
  8.8 2.1 %fusion.21 = bf16[512,256]{0,1:T(8,128)(2,1)S(1)} fusion(bf16[2048,256]{1,0:T(8,128)(2,1)} %param.9, bf16[1,512,2048]{2,1,0:T(8,128)(2,1)S(1)} %copy-done), kind=kOutput, calls=%fused_computation.25 | convolution fusion | flops 537001984 | bytes 3407872 | tf_op jit(solution)/shard_map/dot_general | solution.py:102
  10.9 0.8 fusion.18
  11.9 1.7 %collective-permute-start = (f32[2,128,128]{2,1,0:T(8,128)S(1)}, f32[2,128,128]{2,1,0:T(8,128)S(1)}, u32[]{:S(2)}, u32[]{:S(2)}) collective-permute-start(f32[2,128,128]{2,1,0:T(8,128)S(1)} %fusion.37), channel_id=1, source_target_pairs={{0,32},{32,64},{64,96},{96,128},{128,160},{160,192},{192,224},{1,3... | collective-permute-start | bytes 393224 | tf_op jit(solution)/shard_map/ppermute | solution.py:86
  13.6 0.8 fusion.24
  14.4 2.6 %fusion.14 = bf16[512,256]{0,1:T(8,128)(2,1)S(1)} fusion(bf16[256,2048]{1,0:T(8,128)(2,1)} %param.10, bf16[1,512,2048]{2,1,0:T(8,128)(2,1)} %param.11, f32[512]{0:T(512)S(1)} %multiply_rsqrt_fusion), kind=kOutput, calls=%fused_computation.22 | convolution fusion | flops 537133056 | bytes 3409920 | tf_op jit(solution)/shard_map/td,kd->tk/dot_general | solution.py:111
  17.3 1.3 collective-permute-start.3
  20.6 5.9 %collective-permute-start.1 = (f32[2,128,128]{2,1,0:T(8,128)S(1)}, f32[2,128,128]{2,1,0:T(8,128)S(1)}, u32[]{:S(2)}, u32[]{:S(2)}) collective-permute-start(f32[2,128,128]{2,1,0:T(8,128)S(1)} %add.80), channel_id=1, source_target_pairs={{0,64},{32,96},{64,128},{96,160},{128,192},{160,224},{1,65},{33,97... | collective-permute-start | bytes 393224 | tf_op jit(solution)/shard_map/ppermute | solution.py:86
  26.8 1.4 %collective-permute-start.4 = (f32[2,128,128]{2,1,0:T(8,128)S(1)}, f32[2,128,128]{2,1,0:T(8,128)S(1)}, u32[]{:S(2)}, u32[]{:S(2)}) collective-permute-start(f32[2,128,128]{2,1,0:T(8,128)S(1)} %add.85), channel_id=1, source_target_pairs={{64,0},{96,32},{128,64},{160,96},{192,128},{224,160},{65,1},{97,33... | collective-permute-start | bytes 393224 | tf_op jit(solution)/shard_map/ppermute | solution.py:86
  28.3 1.0 collective-permute-done.1
  29.3 5.6 %collective-permute-start.2 = (f32[2,128,128]{2,1,0:T(8,128)S(1)}, f32[2,128,128]{2,1,0:T(8,128)S(1)}, u32[]{:S(2)}, u32[]{:S(2)}) collective-permute-start(f32[2,128,128]{2,1,0:T(8,128)S(1)} %add.82), channel_id=1, source_target_pairs={{0,128},{32,160},{64,192},{96,224},{1,129},{33,161},{65,193},{97,2... | collective-permute-start | bytes 393224 | tf_op jit(solution)/shard_map/ppermute | solution.py:86
  35.4 1.5 %collective-permute-start.5 = (f32[2,128,128]{2,1,0:T(8,128)S(1)}, f32[2,128,128]{2,1,0:T(8,128)S(1)}, u32[]{:S(2)}, u32[]{:S(2)}) collective-permute-start(f32[2,128,128]{2,1,0:T(8,128)S(1)} %add.87), channel_id=1, source_target_pairs={{128,0},{160,32},{192,64},{224,96},{129,1},{161,33},{193,65},{225,... | collective-permute-start | bytes 393224 | tf_op jit(solution)/shard_map/ppermute | solution.py:86
  37.7 2.1 %convolution_bitcast_fusion.1 = f32[2048,256]{0,1:T(8,128)} fusion(bf16[512,256]{0,1:T(8,128)(2,1)S(1)} %bitcast.118, bf16[1,512,2048]{2,1,0:T(8,128)(2,1)S(1)} %copy-done.2), kind=kOutput, calls=%fused_computation.3 | convolution fusion | flops 536870912 | bytes 4456448 | tf_op jit(solution)/shard_map/td,tk->dk/dot_general | solution.py:166
  39.8 4.0 %collective-permute-done.5 = f32[2,128,128]{2,1,0:T(8,128)S(1)} collective-permute-done((f32[2,128,128]{2,1,0:T(8,128)S(1)}, f32[2,128,128]{2,1,0:T(8,128)S(1)}, u32[]{:S(2)}, u32[]{:S(2)}) %collective-permute-start.5) | collective-permute-done | bytes 131104 | tf_op jit(solution)/shard_map/ppermute | solution.py:86
  44.5 1.8 %convolution_bitcast_fusion = f32[2048,768]{0,1:T(8,128)S(1)} fusion(bf16[1,512,2048]{2,1,0:T(8,128)(2,1)S(1)} %copy-done, bf16[512,256]{0,1:T(8,128)(2,1)S(1)} %bitcast.96, bf16[512,256]{0,1:T(8,128)(2,1)S(1)} %bitcast.114, bf16[512,256]{0,1:T(8,128)(2,1)S(1)} %bitcast.116), kind=kOutput, calls=%fused_computation.2 | convolution fusion | flops 1612972032 | bytes 9175040 | tf_op jit(solution)/shard_map/td,tk->dk/dot_general | solution.py:165
  46.3 6.2 %maximum_multiply_fusion = f32[2048,1024]{0,1:T(8,128)} fusion(f32[2048,256]{0,1:T(8,128)} %convolution_bitcast_fusion.1, f32[2048,768]{0,1:T(8,128)S(1)} %convolution_bitcast_fusion), kind=kLoop, calls=%fused_computation | loop fusion | flops 4194304 | bytes 16777216 | tf_op jit(solution)/shard_map/mul | solution.py:167
  52.5 2.1 %fusion.42 = f32[512,8,256]{2,0,1:T(8,128)S(1)} fusion(bf16[512,256,1]{0,1,2:T(8,128)(2,1)S(1)} %bitcast.117, bf16[8,256,256]{2,1,0:T(8,128)(2,1)} %bitcast.119), kind=kOutput, calls=%fused_computation.47 | convolution fusion | flops 536870912 | bytes 5505024 | tf_op jit(solution)/shard_map/tk,bdk->btd/dot_general | solution.py:155
  54.6 0.8 fusion.43
  55.8 2.7 %add_bitcast_fusion.term_ref = f32[8,512,256]{2,1,0:T(8,128)} fusion(f32[512,8,256]{2,0,1:T(8,128)S(1)} %fusion.42, f32[512,8,256]{2,0,1:T(8,128)S(1)} %fusion.43, bf16[512,256,1]{0,1,2:T(8,128)(2,1)S(1)} %bitcast.97, bf16[8,256,256]{2,1,0:T(8,128)(2,1)S(1)} %bitcast.121), kind=kOutput, calls=%fused_computation.1 | convolution fusion | flops 538968064 | bytes 13893632 | tf_op jit(solution)/shard_map/tk,bdk->btd/dot_general | solution.py:159
  58.6 2.2 %copy-done.1 = f32[8,512,256]{2,1,0:T(8,128)S(1)} copy-done((f32[8,512,256]{2,1,0:T(8,128)S(1)}, f32[8,512,256]{2,1,0:T(8,128)}, u32[]{:S(2)}) %copy-start.1) | copy-done | bytes 4194328
  60.8 56.1 %shard_map.101 = bf16[512,256]{1,0:T(8,128)(2,1)S(1)} custom-call(f32[8,512,256]{2,1,0:T(8,128)S(1)} %copy-done.1), custom_call_target="tpu_custom_call" | custom-call | flops 2097152 | bytes 8388608 | tf_op jit(solution)/shard_map/pallas_call | solution.py:56
  116.9 1.6 %copy.26 = f32[256,1024]{1,0:T(8,128)S(1)} copy(f32[256,1024]{0,1:T(8,128)} %reduce-scatter.2.cloned.1.call-done) | data formatting | bytes 2097152 | tf_op jit(solution)/shard_map/optimization_barrier | solution.py:171
  118.4 15.2 %shard_map.102 = f32[64,1024]{1,0:T(8,128)S(1)} custom-call(f32[4,64,1024]{2,1,0:T(8,128)S(1)} %bitcast.94), custom_call_target="tpu_custom_call" | custom-call | flops 524288 | bytes 2097152 | tf_op jit(solution)/shard_map/pallas_call | solution.py:56
  134.4 0.7 copy.46
  (40 shorter events, 6.0 us)
Async XLA Ops:
  7.2 1.6 %copy-start = (bf16[1,512,2048]{2,1,0:T(8,128)(2,1)S(1)}, bf16[1,512,2048]{2,1,0:T(8,128)(2,1)}, u32[]{:S(2)}) copy-start(bf16[1,512,2048]{2,1,0:T(8,128)(2,1)} %param.6) | copy-start | bytes 6291460
  7.2 109.7 %reduce-scatter.2.cloned.1.call-start = ((), (), s32[]{:S(2)}) async-start(), calls=%async_computation.1 | async-start | bytes 9437184 | tf_op jit(solution)/shard_map/reduce_scatter | solution.py:169
  8.8 2.1 %copy-start.4 = (bf16[2048,256]{1,0:T(8,128)(2,1)S(1)}, bf16[2048,256]{1,0:T(8,128)(2,1)}, u32[]{:S(2)}) copy-start(bf16[2048,256]{1,0:T(8,128)(2,1)} %param.8) | copy-start | bytes 3145732
  10.8 2.8 %copy-start.3 = (bf16[2048,256]{1,0:T(8,128)(2,1)S(1)}, bf16[2048,256]{1,0:T(8,128)(2,1)}, u32[]{:S(2)}) copy-start(bf16[2048,256]{1,0:T(8,128)(2,1)} %param.7) | copy-start | bytes 3145732
  11.9 8.7 %collective-permute-start = (f32[2,128,128]{2,1,0:T(8,128)S(1)}, f32[2,128,128]{2,1,0:T(8,128)S(1)}, u32[]{:S(2)}, u32[]{:S(2)}) collective-permute-start(f32[2,128,128]{2,1,0:T(8,128)S(1)} %fusion.37), channel_id=1, source_target_pairs={{0,32},{32,64},{64,96},{96,128},{128,160},{160,192},{192,224},{1,3... | collective-permute-start | bytes 393224 | tf_op jit(solution)/shard_map/ppermute | solution.py:86
  17.3 9.5 %collective-permute-start.3 = (f32[2,128,128]{2,1,0:T(8,128)S(1)}, f32[2,128,128]{2,1,0:T(8,128)S(1)}, u32[]{:S(2)}, u32[]{:S(2)}) collective-permute-start(f32[2,128,128]{2,1,0:T(8,128)S(1)} %fusion.39), channel_id=1, source_target_pairs={{32,0},{64,32},{96,64},{128,96},{160,128},{192,160},{224,192},{33,... | collective-permute-start | bytes 393224 | tf_op jit(solution)/shard_map/ppermute | solution.py:86
  20.6 8.7 %collective-permute-start.1 = (f32[2,128,128]{2,1,0:T(8,128)S(1)}, f32[2,128,128]{2,1,0:T(8,128)S(1)}, u32[]{:S(2)}, u32[]{:S(2)}) collective-permute-start(f32[2,128,128]{2,1,0:T(8,128)S(1)} %add.80), channel_id=1, source_target_pairs={{0,64},{32,96},{64,128},{96,160},{128,192},{160,224},{1,65},{33,97... | collective-permute-start | bytes 393224 | tf_op jit(solution)/shard_map/ppermute | solution.py:86
  26.8 10.9 %copy-start.2 = (bf16[1,512,2048]{2,1,0:T(8,128)(2,1)S(1)}, bf16[1,512,2048]{2,1,0:T(8,128)(2,1)}, u32[]{:S(2)}) copy-start(bf16[1,512,2048]{2,1,0:T(8,128)(2,1)} %param.11) | copy-start | bytes 6291460
  26.8 8.6 %collective-permute-start.4 = (f32[2,128,128]{2,1,0:T(8,128)S(1)}, f32[2,128,128]{2,1,0:T(8,128)S(1)}, u32[]{:S(2)}, u32[]{:S(2)}) collective-permute-start(f32[2,128,128]{2,1,0:T(8,128)S(1)} %add.85), channel_id=1, source_target_pairs={{64,0},{96,32},{128,64},{160,96},{192,128},{224,160},{65,1},{97,33... | collective-permute-start | bytes 393224 | tf_op jit(solution)/shard_map/ppermute | solution.py:86
  29.3 8.1 %collective-permute-start.2 = (f32[2,128,128]{2,1,0:T(8,128)S(1)}, f32[2,128,128]{2,1,0:T(8,128)S(1)}, u32[]{:S(2)}, u32[]{:S(2)}) collective-permute-start(f32[2,128,128]{2,1,0:T(8,128)S(1)} %add.82), channel_id=1, source_target_pairs={{0,128},{32,160},{64,192},{96,224},{1,129},{33,161},{65,193},{97,2... | collective-permute-start | bytes 393224 | tf_op jit(solution)/shard_map/ppermute | solution.py:86
  35.4 8.4 %collective-permute-start.5 = (f32[2,128,128]{2,1,0:T(8,128)S(1)}, f32[2,128,128]{2,1,0:T(8,128)S(1)}, u32[]{:S(2)}, u32[]{:S(2)}) collective-permute-start(f32[2,128,128]{2,1,0:T(8,128)S(1)} %add.87), channel_id=1, source_target_pairs={{128,0},{160,32},{192,64},{224,96},{129,1},{161,33},{193,65},{225,... | collective-permute-start | bytes 393224 | tf_op jit(solution)/shard_map/ppermute | solution.py:86
  52.5 2.1 %copy-start.5 = (bf16[2048,256]{1,0:T(8,128)(2,1)S(1)}, bf16[2048,256]{1,0:T(8,128)(2,1)}, u32[]{:S(2)}) copy-start(bf16[2048,256]{1,0:T(8,128)(2,1)} %param.8) | copy-start | bytes 3145732
  54.6 1.2 copy-start.6
  58.6 2.2 %copy-start.1 = (f32[8,512,256]{2,1,0:T(8,128)S(1)}, f32[8,512,256]{2,1,0:T(8,128)}, u32[]{:S(2)}) copy-start(f32[8,512,256]{2,1,0:T(8,128)} %add_bitcast_fusion.term_ref) | copy-start | bytes 12582916
Sparse Core Ops, SparseCore 0:
  58.7 55.3 reduce-scatter.1

commit v5 on v4

--- a/solution.py
+++ b/solution.py
@@ -149,24 +149,19 @@
     d_values = d_values.astype(jnp.bfloat16).reshape(num_rows, width)
     groups = lax.axis_size("head")
 
-    def by_block(weight):
-        return weight.reshape(groups, weight.shape[0] // groups, width)
-
-    head_terms = jnp.einsum("tk,bdk->btd", d_query, by_block(w_query), preferred_element_type=jnp.float32)
-    head_terms = head_terms + jnp.einsum(
-        "tk,bdk->btd", d_keys, by_block(w_key), preferred_element_type=jnp.float32
-    )
-    head_terms = head_terms + jnp.einsum(
-        "tk,bdk->btd", d_values, by_block(w_value), preferred_element_type=jnp.float32
-    )
+    grads = jnp.concatenate([d_query, d_keys, d_values], axis=1)
+    w_all = jnp.concatenate([w_query, w_key, w_value], axis=1)
     total_rows = lax.axis_size("seq") * lax.axis_size("dp") * num_rows
     grad_scale = jnp.float32(1.0) / jnp.sqrt(jnp.float32(total_rows))
-    grads = jnp.concatenate([d_query, d_keys, d_values], axis=1)
     term_qkv = jnp.einsum("td,tk->dk", in_rows, grads, preferred_element_type=jnp.float32)
     term_out = jnp.einsum("td,tk->dk", grad_rows, attention, preferred_element_type=jnp.float32)
     terms = jnp.concatenate([term_qkv, term_out], axis=1) * grad_scale
-    terms, head_terms = lax.optimization_barrier((terms, head_terms))
+    terms, grads, w_all = lax.optimization_barrier((terms, grads, w_all))
     summed = lax.psum_scatter(terms, "seq", scatter_dimension=0, tiled=True)
+    head_terms = jnp.einsum(
+        "tk,bdk->btd", grads, w_all.reshape(groups, w_all.shape[0] // groups, 3 * width),
+        preferred_element_type=jnp.float32,
+    )
     input_grad = ring_scatter(head_terms, "head", jnp.bfloat16, 0)[None]
     summed, input_grad = lax.optimization_barrier((summed, input_grad))
     shares = lax.axis_size("dp")

time: 143 us -> 150 us (1.049)
  other arithmetic: 6.39 us -> 10.9 us
  Pallas kernels: 71.3 us -> 75.7 us
  waiting for transfers between devices: 5.52 us -> 1.73 us
    pallas_call x2, Pallas kernels: 71.3 us -> 75.7 us  [ring_scatter(): pl.pallas_call(functools.partial(ring_scatter_kernel, n, axis), out_shape...]
    ppermute x6, waiting for transfers between devices: 5.48 us -> 1.7 us  [exclusive_scan(): arrived = lax.ppermute(span, axis, pairs)]
    concatenate x0 -> x2, other arithmetic: none -> 2.76 us  [the longest x1 1.82 us: local(): w_all = jnp.concatenate([w_query, w_key, w_value], axis=1)]
    dot_general x3 -> x1, matrix products: 5.56 us -> 3.71 us  [local(): jnp.einsum('tk,bdk->btd', grads, w_all.reshape(groups, w_all.shape[0] //...]
    dot_general x1, matrix products: 2.6 us -> 0.75 us  [local(): jnp.einsum('td,kd->tk', grad_rows, w_out, preferred_element_type=jnp.floa...]
    unnamed x15 -> x23, local copies, waits for them, and re-layouts: 4.9 us -> 4.14 us
  transfers between devices with their start and end apart: 7 -> 7, of which waited for: 3 -> 2; matrix products, arithmetic and copies ran while one was open for 6% -> 10% of each run, Pallas kernels for 39% -> 40%
where the time goes in v5:
time: 150 us; the launch traced here: 148 us
  Pallas kernels  75.7 us (50%)
  matrix products  20.5 us (14%)
  starting transfers between devices  18.3 us (12%)
  between operations  14.4 us (10%)
  other arithmetic  10.9 us (7%)
  local copies, waits for them, and re-layouts  6.79 us (5%)
  waiting for transfers between devices  1.73 us (1%)
    pallas_call x2, Pallas kernels, ring_scatter(): pl.pallas_call(functools.partial(ring_scatter_kernel, n, axis), out_shape...  75.7 us
    ppermute x6, starting transfers between devices, exclusive_scan(): arrived = lax.ppermute(span, axis, pairs)  18.3 us
    mul x1, other arithmetic, local(): terms = jnp.concatenate([term_qkv, term_out], axis=1) * grad_scale  6.2 us
    unnamed x23, local copies, waits for them, and re-layouts  4.14 us
    dot_general x1, matrix products, local(): jnp.einsum('tk,bdk->btd', grads, w_all.reshape(groups, w_all.shape[0] //...  3.71 us
    dot_general x3, matrix products, project(): jnp.dot(in_rows, weight, preferred_element_type=jnp.float32)  3.52 us
  transfers between devices with their start and end apart: 7, of which 2 were waited for; matrix products, arithmetic and copies ran while one was open for 10% of the time, Pallas kernels for 40%

profile of v5, /device:TPU:8, one launch (start us, length us, event | category | flops | bytes accessed | tf_op | source)
XLA Modules:
  0.0 148.3 jit_solution(8100436535588259777)
XLA Ops:
  7.3 1.5 %copy-done = bf16[1,512,2048]{2,1,0:T(8,128)(2,1)S(1)} copy-done((bf16[1,512,2048]{2,1,0:T(8,128)(2,1)S(1)}, bf16[1,512,2048]{2,1,0:T(8,128)(2,1)}, u32[]{:S(2)}) %copy-start) | copy-done | bytes 2097176
  8.8 2.0 %fusion.24 = bf16[512,256]{0,1:T(8,128)(2,1)S(1)} fusion(bf16[2048,256]{1,0:T(8,128)(2,1)} %param.7, bf16[1,512,2048]{2,1,0:T(8,128)(2,1)S(1)} %copy-done), kind=kOutput, calls=%fused_computation.27 | convolution fusion | flops 537001984 | bytes 3407872 | tf_op jit(solution)/shard_map/dot_general | solution.py:102
  11.8 1.4 collective-permute-start.3
  15.0 3.0 %collective-permute-start = (f32[2,128,128]{2,1,0:T(8,128)S(1)}, f32[2,128,128]{2,1,0:T(8,128)S(1)}, u32[]{:S(2)}, u32[]{:S(2)}) collective-permute-start(f32[2,128,128]{2,1,0:T(8,128)S(1)} %fusion.32), channel_id=1, source_target_pairs={{0,32},{32,64},{64,96},{96,128},{128,160},{160,192},{192,224},{1,3... | collective-permute-start | bytes 393224 | tf_op jit(solution)/shard_map/ppermute | solution.py:86
  19.4 1.8 %pad_maximum_fusion = bf16[2048,768]{1,0:T(8,128)(2,1)} fusion(bf16[2048,256]{1,0:T(8,128)(2,1)S(1)} %copy-done.4, bf16[2048,256]{1,0:T(8,128)(2,1)S(1)} %copy-done.5, bf16[2048,256]{1,0:T(8,128)(2,1)S(1)} %copy-done.6), kind=kLoop, calls=%fused_computation.2 | loop fusion | flops 9437184 | bytes 6291456 | tf_op jit(solution)/shard_map/concatenate | solution.py:153
  21.5 1.3 fusion.31
  22.8 1.3 collective-permute-start.4
  24.1 1.1 fusion.35
  25.2 4.6 %collective-permute-start.1 = (f32[2,128,128]{2,1,0:T(8,128)S(1)}, f32[2,128,128]{2,1,0:T(8,128)S(1)}, u32[]{:S(2)}, u32[]{:S(2)}) collective-permute-start(f32[2,128,128]{2,1,0:T(8,128)S(1)} %add.70), channel_id=1, source_target_pairs={{0,64},{32,96},{64,128},{96,160},{128,192},{160,224},{1,65},{33,97... | collective-permute-start | bytes 393224 | tf_op jit(solution)/shard_map/ppermute | solution.py:86
  29.8 1.1 collective-permute-done.4
  31.0 1.3 collective-permute-start.5
  32.3 1.3 fusion.36
  34.2 6.7 %collective-permute-start.2 = (f32[2,128,128]{2,1,0:T(8,128)}, f32[2,128,128]{2,1,0:T(8,128)}, u32[]{:S(2)}, u32[]{:S(2)}) collective-permute-start(f32[2,128,128]{2,1,0:T(8,128)} %add.72), channel_id=1, source_target_pairs={{0,128},{32,160},{64,192},{96,224},{1,129},{33,161},{65,193},{97,2... | collective-permute-start | bytes 393224 | tf_op jit(solution)/shard_map/ppermute | solution.py:86
  41.3 1.3 fusion.29
  43.3 1.1 add_convert_fusion.1
  44.4 1.2 fusion.27
  45.8 1.8 %convolution_bitcast_fusion = f32[2048,768]{0,1:T(8,128)S(1)} fusion(bf16[1,512,2048]{2,1,0:T(8,128)(2,1)S(1)} %copy-done, bf16[512,256]{1,0:T(8,128)(2,1)S(1)} %copy.23, bf16[512,256]{1,0:T(8,128)(2,1)S(1)} %copy.22, bf16[512,256]{1,0:T(8,128)(2,1)S(1)} %copy.21), kind=kOutput, calls=%fused_computation.1 | convolution fusion | flops 1612972032 | bytes 9175040 | tf_op jit(solution)/shard_map/td,tk->dk/dot_general | solution.py:156
  49.5 2.2 %convolution_bitcast_fusion.1 = f32[2048,256]{0,1:T(8,128)} fusion(bf16[512,256]{0,1:T(8,128)(2,1)S(1)} %bitcast.103, bf16[1,512,2048]{2,1,0:T(8,128)(2,1)S(1)} %copy-done.3), kind=kOutput, calls=%fused_computation.3 | convolution fusion | flops 536870912 | bytes 4456448 | tf_op jit(solution)/shard_map/td,tk->dk/dot_general | solution.py:157
  51.7 6.2 %maximum_multiply_fusion = f32[2048,1024]{0,1:T(8,128)} fusion(f32[2048,256]{0,1:T(8,128)} %convolution_bitcast_fusion.1, f32[2048,768]{0,1:T(8,128)S(1)} %convolution_bitcast_fusion), kind=kLoop, calls=%fused_computation | loop fusion | flops 4194304 | bytes 16777216 | tf_op jit(solution)/shard_map/mul | solution.py:158
  57.9 1.1 copy-done.7
  59.0 3.7 %convolution_bitcast_fusion.2.term_ref = f32[8,512,256]{2,1,0:T(8,128)S(1)} fusion(bf16[8,256,768]{2,1,0:T(8,128)(2,1)} %bitcast.86, bf16[512,768]{1,0:T(8,128)(2,1)S(1)} %copy-done.7), kind=kOutput, calls=%fused_computation.4 | convolution fusion | flops 1610612736 | bytes 8126464 | tf_op jit(solution)/shard_map/tk,bdk->btd/dot_general | solution.py:161
  62.7 59.8 %shard_map.101 = bf16[512,256]{1,0:T(8,128)(2,1)S(1)} custom-call(f32[8,512,256]{2,1,0:T(8,128)S(1)} %convolution_bitcast_fusion.2.term_ref), custom_call_target="tpu_custom_call" | custom-call | flops 2097152 | bytes 8388608 | tf_op jit(solution)/shard_map/pallas_call | solution.py:56
  122.5 1.6 %copy.27 = f32[256,1024]{1,0:T(8,128)S(1)} copy(f32[256,1024]{0,1:T(8,128)} %reduce-scatter.2.cloned.1.call-done) | data formatting | bytes 2097152 | tf_op jit(solution)/shard_map/optimization_barrier | solution.py:166
  124.1 16.0 %shard_map.102 = f32[64,1024]{1,0:T(8,128)S(1)} custom-call(f32[4,64,1024]{2,1,0:T(8,128)S(1)} %bitcast.84), custom_call_target="tpu_custom_call" | custom-call | flops 524288 | bytes 2097152 | tf_op jit(solution)/shard_map/pallas_call | solution.py:56
  (51 shorter events, 9.7 us)
Async XLA Ops:
  7.2 1.6 %copy-start = (bf16[1,512,2048]{2,1,0:T(8,128)(2,1)S(1)}, bf16[1,512,2048]{2,1,0:T(8,128)(2,1)}, u32[]{:S(2)}) copy-start(bf16[1,512,2048]{2,1,0:T(8,128)(2,1)} %param.6) | copy-start | bytes 6291460
  7.2 115.4 %reduce-scatter.2.cloned.1.call-start = ((), (), s32[]{:S(2)}) async-start(), calls=%async_computation.1 | async-start | bytes 9437184 | tf_op jit(solution)/shard_map/reduce_scatter | solution.py:160
  7.2 3.5 %copy-start.2 = (bf16[1,512,2048]{2,1,0:T(8,128)(2,1)S(1)}, bf16[1,512,2048]{2,1,0:T(8,128)(2,1)}, u32[]{:S(2)}) copy-start(bf16[1,512,2048]{2,1,0:T(8,128)(2,1)} %param.11) | copy-start | bytes 6291460
  7.2 3.5 %copy-start.10 = (bf16[256,2048]{1,0:T(8,128)(2,1)S(1)}, bf16[256,2048]{1,0:T(8,128)(2,1)}, u32[]{:S(2)}) copy-start(bf16[256,2048]{1,0:T(8,128)(2,1)} %param.10) | copy-start | bytes 3145732
  10.8 2.4 %copy-start.4 = (bf16[2048,256]{1,0:T(8,128)(2,1)S(1)}, bf16[2048,256]{1,0:T(8,128)(2,1)}, u32[]{:S(2)}) copy-start(bf16[2048,256]{1,0:T(8,128)(2,1)} %param.9) | copy-start | bytes 3145732
  11.5 2.5 %copy-start.5 = (bf16[2048,256]{1,0:T(8,128)(2,1)S(1)}, bf16[2048,256]{1,0:T(8,128)(2,1)}, u32[]{:S(2)}) copy-start(bf16[2048,256]{1,0:T(8,128)(2,1)} %param.8) | copy-start | bytes 3145732
  11.8 11.0 %collective-permute-start.3 = (f32[2,128,128]{2,1,0:T(8,128)S(1)}, f32[2,128,128]{2,1,0:T(8,128)S(1)}, u32[]{:S(2)}, u32[]{:S(2)}) collective-permute-start(f32[2,128,128]{2,1,0:T(8,128)S(1)} %fusion.34), channel_id=1, source_target_pairs={{32,0},{64,32},{96,64},{128,96},{160,128},{192,160},{224,192},{33,... | collective-permute-start | bytes 393224 | tf_op jit(solution)/shard_map/ppermute | solution.py:86
  15.0 10.2 %collective-permute-start = (f32[2,128,128]{2,1,0:T(8,128)S(1)}, f32[2,128,128]{2,1,0:T(8,128)S(1)}, u32[]{:S(2)}, u32[]{:S(2)}) collective-permute-start(f32[2,128,128]{2,1,0:T(8,128)S(1)} %fusion.32), channel_id=1, source_target_pairs={{0,32},{32,64},{64,96},{96,128},{128,160},{160,192},{192,224},{1,3... | collective-permute-start | bytes 393224 | tf_op jit(solution)/shard_map/ppermute | solution.py:86
  18.1 1.2 copy-start.6
  22.8 8.1 %collective-permute-start.4 = (f32[2,128,128]{2,1,0:T(8,128)S(1)}, f32[2,128,128]{2,1,0:T(8,128)S(1)}, u32[]{:S(2)}, u32[]{:S(2)}) collective-permute-start(f32[2,128,128]{2,1,0:T(8,128)S(1)} %add.75), channel_id=1, source_target_pairs={{64,0},{96,32},{128,64},{160,96},{192,128},{224,160},{65,1},{97,33... | collective-permute-start | bytes 393224 | tf_op jit(solution)/shard_map/ppermute | solution.py:86
  25.2 16.0 %copy-start.8 = (f32[2,128,128]{2,1,0:T(8,128)}, f32[2,128,128]{2,1,0:T(8,128)S(1)}, u32[]{:S(2)}) copy-start(f32[2,128,128]{2,1,0:T(8,128)S(1)} %collective-permute-done) | copy-start | bytes 393220
  25.2 8.3 %collective-permute-start.1 = (f32[2,128,128]{2,1,0:T(8,128)S(1)}, f32[2,128,128]{2,1,0:T(8,128)S(1)}, u32[]{:S(2)}, u32[]{:S(2)}) collective-permute-start(f32[2,128,128]{2,1,0:T(8,128)S(1)} %add.70), channel_id=1, source_target_pairs={{0,64},{32,96},{64,128},{96,160},{128,192},{160,224},{1,65},{33,97... | collective-permute-start | bytes 393224 | tf_op jit(solution)/shard_map/ppermute | solution.py:86
  31.0 10.0 %collective-permute-start.5 = (f32[2,128,128]{2,1,0:T(8,128)S(1)}, f32[2,128,128]{2,1,0:T(8,128)S(1)}, u32[]{:S(2)}, u32[]{:S(2)}) collective-permute-start(f32[2,128,128]{2,1,0:T(8,128)S(1)} %add.77), channel_id=1, source_target_pairs={{128,0},{160,32},{192,64},{224,96},{129,1},{161,33},{193,65},{225,... | collective-permute-start | bytes 393224 | tf_op jit(solution)/shard_map/ppermute | solution.py:86
  33.5 7.7 %copy-start.9 = (f32[2,128,128]{2,1,0:T(8,128)}, f32[2,128,128]{2,1,0:T(8,128)S(1)}, u32[]{:S(2)}) copy-start(f32[2,128,128]{2,1,0:T(8,128)S(1)} %collective-permute-done.1) | copy-start | bytes 393220
  34.2 9.1 %collective-permute-start.2 = (f32[2,128,128]{2,1,0:T(8,128)}, f32[2,128,128]{2,1,0:T(8,128)}, u32[]{:S(2)}, u32[]{:S(2)}) collective-permute-start(f32[2,128,128]{2,1,0:T(8,128)} %add.72), channel_id=1, source_target_pairs={{0,128},{32,160},{64,192},{96,224},{1,129},{33,161},{65,193},{97,2... | collective-permute-start | bytes 393224 | tf_op jit(solution)/shard_map/ppermute | solution.py:86
  45.8 2.8 %copy-start.1 = (f32[2,128,512]{2,1,0:T(8,128)S(1)}, f32[2,128,512]{2,1,0:T(8,128)}, u32[]{:S(2)}) copy-start(f32[2,128,512]{2,1,0:T(8,128)} %fusion.36) | copy-start | bytes 1572868
  47.6 1.9 %copy-start.3 = (bf16[1,512,2048]{2,1,0:T(8,128)(2,1)S(1)}, bf16[1,512,2048]{2,1,0:T(8,128)(2,1)}, u32[]{:S(2)}) copy-start(bf16[1,512,2048]{2,1,0:T(8,128)(2,1)} %param.11) | copy-start | bytes 6291460
  57.9 1.1 copy-start.7
Sparse Core Ops, SparseCore 0:
  58.0 59.4 reduce-scatter.1

commit v6 on v4

--- a/solution.py
+++ b/solution.py
@@ -73,22 +73,75 @@
     )(terms)
 
 
-def exclusive_scan(x, axis, reverse):
-    peers = lax.axis_size(axis)
-    span = x
-    total = None
-    reach = 1
-    while reach < peers:
-        if reverse:
-            pairs = [(j, j - reach) for j in range(reach, peers)]
-        else:
-            pairs = [(j, j + reach) for j in range(peers - reach)]
-        arrived = lax.ppermute(span, axis, pairs)
-        total = arrived if total is None else total + arrived
-        if reach * 2 < peers:
-            span = span + arrived
-        reach *= 2
-    return total
+def exchange_kernel(n, axis, kv_ref, qg_ref, prefix_ref, suffix_ref, kv_in, qg_in, send_sem, recv_sem):
+    me = lax.axis_index(axis)
+    barrier = pltpu.get_barrier_semaphore()
+    for offset in range(1, n):
+        pl.semaphore_signal(
+            barrier, inc=1, device_id={axis: lax.rem(me + offset, n)}, device_id_type=MESH
+        )
+    pl.semaphore_wait(barrier, n - 1)
+
+    def route(offset, later):
+        peer = lax.rem(me + offset, n)
+        kind = 0 if later else 1
+        return pltpu.make_async_remote_copy(
+            src_ref=kv_ref if later else qg_ref,
+            dst_ref=(kv_in if later else qg_in).at[me],
+            send_sem=send_sem.at[kind, offset],
+            recv_sem=recv_sem.at[kind, me],
+            device_id={axis: peer},
+            device_id_type=MESH,
+        )
+
+    for offset in range(1, n):
+        for later in (True, False):
+            @pl.when((me + offset < n) == later)
+            def _():
+                route(offset, later).start()
+
+    prefix_ref[...] = jnp.zeros_like(prefix_ref)
+    suffix_ref[...] = jnp.zeros_like(suffix_ref)
+    for peer in range(n):
+        @pl.when(peer < me)
+        def _():
+            pltpu.make_async_remote_copy(
+                src_ref=kv_ref, dst_ref=kv_in.at[peer], send_sem=send_sem.at[0, 0],
+                recv_sem=recv_sem.at[0, peer], device_id={axis: peer}, device_id_type=MESH,
+            ).wait_recv()
+            prefix_ref[...] += kv_in[peer]
+
+        @pl.when(peer > me)
+        def _():
+            pltpu.make_async_remote_copy(
+                src_ref=qg_ref, dst_ref=qg_in.at[peer], send_sem=send_sem.at[1, 0],
+                recv_sem=recv_sem.at[1, peer], device_id={axis: peer}, device_id_type=MESH,
+            ).wait_recv()
+            suffix_ref[...] += qg_in[peer]
+
+    for offset in range(1, n):
+        for later in (True, False):
+            @pl.when((me + offset < n) == later)
+            def _():
+                route(offset, later).wait_send()
+
+
+def exchange_states(kv_state, qg_state, axis):
+    n = lax.axis_size(axis)
+    shape = kv_state.shape
+    return pl.pallas_call(
+        functools.partial(exchange_kernel, n, axis),
+        out_shape=(jax.ShapeDtypeStruct(shape, jnp.float32),) * 2,
+        in_specs=[pl.BlockSpec(memory_space=pltpu.VMEM)] * 2,
+        out_specs=(pl.BlockSpec(memory_space=pltpu.VMEM),) * 2,
+        scratch_shapes=[
+            pltpu.VMEM((n,) + shape, jnp.float32),
+            pltpu.VMEM((n,) + shape, jnp.float32),
+            pltpu.SemaphoreType.DMA((2, n)),
+            pltpu.SemaphoreType.DMA((2, n)),
+        ],
+        compiler_params=pltpu.CompilerParams(collective_id=2, has_side_effects=True),
+    )(kv_state, qg_state)
 
 
 def local(layer_input, w_query, w_key, w_value, w_out, out_grad):
@@ -116,8 +169,9 @@
     )
     kv_state = jnp.einsum("thd,the->hde", key_rows, value_rows, preferred_element_type=jnp.float32)
     qg_state = jnp.einsum("thd,the->hde", queries, grad_in, preferred_element_type=jnp.float32)
-    prefix = exclusive_scan(kv_state, "seq", False).astype(jnp.bfloat16)
-    suffix = exclusive_scan(qg_state, "seq", True).astype(jnp.bfloat16)
+    prefix, suffix = exchange_states(kv_state, qg_state, "seq")
+    prefix = prefix.astype(jnp.bfloat16)
+    suffix = suffix.astype(jnp.bfloat16)
     causal = (jnp.arange(num_rows)[:, None] >= jnp.arange(num_rows)[None, :])[None]
     scores = jnp.einsum("thd,shd->hts", queries, key_rows, preferred_element_type=jnp.float32)
     scores_qk = jnp.where(causal, scores, 0.0).astype(jnp.bfloat16)

time: 143 us -> 144 us (level)
  Pallas kernels: 71.3 us -> 91.6 us
  starting transfers between devices: 17.5 us -> 0.04 us
  waiting for transfers between devices: 5.52 us -> 0.04 us
  matrix products: 19.7 us -> 22.7 us
    ppermute x6 -> x0, starting transfers between devices: 17.5 us -> none  [exclusive_scan(): arrived = lax.ppermute(span, axis, pairs)]
    pallas_call x0 -> x1, Pallas kernels: none -> 16.8 us  [exchange_states(): pl.pallas_call(functools.partial(exchange_kernel, n, axis), out_shape=(ja...]
    ppermute x6 -> x0, waiting for transfers between devices: 5.48 us -> none  [exclusive_scan(): arrived = lax.ppermute(span, axis, pairs)]
    pallas_call x2, Pallas kernels: 71.3 us -> 74.8 us  [ring_scatter(): pl.pallas_call(functools.partial(ring_scatter_kernel, n, axis), out_shape...]
    unnamed x15 -> x17, local copies, waits for them, and re-layouts: 4.9 us -> 5.84 us
  transfers between devices with their start and end apart: 7 -> 1, of which waited for: 3 -> 0; matrix products, arithmetic and copies ran while one was open for 6% -> 0% of each run, Pallas kernels for 39% -> 40%
where the time goes in v6:
time: 144 us; the launch traced here: 143 us
  Pallas kernels  91.6 us (64%)
  matrix products  22.7 us (16%)
  between operations  14.3 us (10%)
  local copies, waits for them, and re-layouts  8.09 us (6%)
  other arithmetic  6.28 us (4%)
    pallas_call x2, Pallas kernels, ring_scatter(): pl.pallas_call(functools.partial(ring_scatter_kernel, n, axis), out_shape...  74.8 us
    pallas_call x1, Pallas kernels, exchange_states(): pl.pallas_call(functools.partial(exchange_kernel, n, axis), out_shape=(ja...  16.8 us
    mul x1, other arithmetic, local(): terms = jnp.concatenate([term_qkv, term_out], axis=1) * grad_scale  6.19 us
    unnamed x17, local copies, waits for them, and re-layouts  5.84 us
    dot_general x3, matrix products, project(): jnp.dot(in_rows, weight, preferred_element_type=jnp.float32)  3.51 us
  transfers between devices with their start and end apart: 1, of which 0 were waited for; matrix products, arithmetic and copies ran while one was open for 0% of the time, Pallas kernels for 40%

profile of v6, /device:TPU:8, one launch (start us, length us, event | category | flops | bytes accessed | tf_op | source)
XLA Modules:
  0.0 143.0 jit_solution(3377149462261776496)
XLA Ops:
  7.3 1.4 %copy-done = bf16[1,512,2048]{2,1,0:T(8,128)(2,1)S(1)} copy-done((bf16[1,512,2048]{2,1,0:T(8,128)(2,1)S(1)}, bf16[1,512,2048]{2,1,0:T(8,128)(2,1)}, u32[]{:S(2)}) %copy-start) | copy-done | bytes 2097176
  8.8 2.0 %fusion.27 = bf16[512,256]{0,1:T(8,128)(2,1)S(1)} fusion(bf16[2048,256]{1,0:T(8,128)(2,1)} %param.7, bf16[1,512,2048]{2,1,0:T(8,128)(2,1)S(1)} %copy-done), kind=kOutput, calls=%fused_computation.29 | convolution fusion | flops 537001984 | bytes 3407872 | tf_op jit(solution)/shard_map/dot_general | solution.py:155
  10.8 0.8 fusion.21
  12.0 0.8 fusion.24
  12.8 0.9 fusion.44.kv_ref
  13.7 2.6 %fusion.17 = bf16[512,256]{0,1:T(8,128)(2,1)S(1)} fusion(bf16[256,2048]{1,0:T(8,128)(2,1)} %param.10, bf16[1,512,2048]{2,1,0:T(8,128)(2,1)} %param.11, f32[512]{0:T(512)S(1)} %multiply_rsqrt_fusion), kind=kOutput, calls=%fused_computation.25 | convolution fusion | flops 537133056 | bytes 3409920 | tf_op jit(solution)/shard_map/td,kd->tk/dot_general | solution.py:164
  16.3 0.9 fusion.45.qg_ref
  17.2 16.8 %shard_map.101 = (f32[2,128,128]{2,1,0:T(8,128)}, f32[2,128,128]{2,1,0:T(8,128)}) custom-call(f32[2,128,128]{2,1,0:T(8,128)} %fusion.44.kv_ref, f32[2,128,128]{2,1,0:T(8,128)} %fusion.45.qg_ref), custom_call_target="tpu_custom_call" | custom-call | tf_op jit(solution)/shard_map/pallas_call | solution.py:132
  33.9 1.2 fusion.35
  35.1 1.1 fusion.37
  36.2 0.5 select_convert_fusion
  38.3 0.6 copy-done.2
  38.9 2.1 %convolution_bitcast_fusion.1 = f32[2048,256]{0,1:T(8,128)} fusion(bf16[512,256]{0,1:T(8,128)(2,1)S(1)} %bitcast.114, bf16[1,512,2048]{2,1,0:T(8,128)(2,1)S(1)} %copy-done.2), kind=kOutput, calls=%fused_computation.3 | convolution fusion | flops 536870912 | bytes 4456448 | tf_op jit(solution)/shard_map/td,tk->dk/dot_general | solution.py:220
  42.1 1.8 %convolution_bitcast_fusion = f32[2048,768]{0,1:T(8,128)S(1)} fusion(bf16[1,512,2048]{2,1,0:T(8,128)(2,1)S(1)} %copy-done, bf16[512,256]{0,1:T(8,128)(2,1)S(1)} %bitcast.96, bf16[512,256]{0,1:T(8,128)(2,1)S(1)} %bitcast.110, bf16[512,256]{0,1:T(8,128)(2,1)S(1)} %bitcast.112), kind=kOutput, calls=%fused_computation.2 | convolution fusion | flops 1612972032 | bytes 9175040 | tf_op jit(solution)/shard_map/td,tk->dk/dot_general | solution.py:219
  43.9 6.2 %maximum_multiply_fusion = f32[2048,1024]{0,1:T(8,128)} fusion(f32[2048,256]{0,1:T(8,128)} %convolution_bitcast_fusion.1, f32[2048,768]{0,1:T(8,128)S(1)} %convolution_bitcast_fusion), kind=kLoop, calls=%fused_computation | loop fusion | flops 4194304 | bytes 16777216 | tf_op jit(solution)/shard_map/mul | solution.py:221
  50.1 2.1 %fusion.46 = f32[512,8,256]{2,0,1:T(8,128)S(1)} fusion(bf16[512,256,1]{0,1,2:T(8,128)(2,1)S(1)} %bitcast.113, bf16[8,256,256]{2,1,0:T(8,128)(2,1)} %bitcast.115), kind=kOutput, calls=%fused_computation.49 | convolution fusion | flops 536870912 | bytes 5505024 | tf_op jit(solution)/shard_map/tk,bdk->btd/dot_general | solution.py:209
  52.2 0.8 fusion.47
  53.4 2.7 %add_bitcast_fusion.term_ref = f32[8,512,256]{2,1,0:T(8,128)} fusion(f32[512,8,256]{2,0,1:T(8,128)S(1)} %fusion.46, f32[512,8,256]{2,0,1:T(8,128)S(1)} %fusion.47, bf16[512,256,1]{0,1,2:T(8,128)(2,1)S(1)} %bitcast.97, bf16[8,256,256]{2,1,0:T(8,128)(2,1)S(1)} %bitcast.117), kind=kOutput, calls=%fused_computation.1 | convolution fusion | flops 538968064 | bytes 13893632 | tf_op jit(solution)/shard_map/tk,bdk->btd/dot_general | solution.py:213
  56.2 2.2 %copy-done.1 = f32[8,512,256]{2,1,0:T(8,128)S(1)} copy-done((f32[8,512,256]{2,1,0:T(8,128)S(1)}, f32[8,512,256]{2,1,0:T(8,128)}, u32[]{:S(2)}) %copy-start.1) | copy-done | bytes 4194328
  58.3 57.8 %shard_map.102 = bf16[512,256]{1,0:T(8,128)(2,1)S(1)} custom-call(f32[8,512,256]{2,1,0:T(8,128)S(1)} %copy-done.1), custom_call_target="tpu_custom_call" | custom-call | flops 2097152 | bytes 8388608 | tf_op jit(solution)/shard_map/pallas_call | solution.py:56
  116.1 1.6 %copy.26 = f32[256,1024]{1,0:T(8,128)S(1)} copy(f32[256,1024]{0,1:T(8,128)} %reduce-scatter.2.cloned.1.call-done) | data formatting | bytes 2097152 | tf_op jit(solution)/shard_map/optimization_barrier | solution.py:225
  117.7 17.1 %shard_map.103 = f32[64,1024]{1,0:T(8,128)S(1)} custom-call(f32[4,64,1024]{2,1,0:T(8,128)S(1)} %bitcast.90), custom_call_target="tpu_custom_call" | custom-call | flops 524288 | bytes 2097152 | tf_op jit(solution)/shard_map/pallas_call | solution.py:56
  134.8 0.7 slice_bitcast_fusion
  135.5 0.7 copy.46
  (25 shorter events, 3.7 us)
Async XLA Ops:
  7.2 1.6 %copy-start = (bf16[1,512,2048]{2,1,0:T(8,128)(2,1)S(1)}, bf16[1,512,2048]{2,1,0:T(8,128)(2,1)}, u32[]{:S(2)}) copy-start(bf16[1,512,2048]{2,1,0:T(8,128)(2,1)} %param.6) | copy-start | bytes 6291460
  7.2 109.0 %reduce-scatter.2.cloned.1.call-start = ((), (), s32[]{:S(2)}) async-start(), calls=%async_computation.1 | async-start | bytes 9437184 | tf_op jit(solution)/shard_map/reduce_scatter | solution.py:223
  7.2 3.5 %copy-start.3 = (bf16[2048,256]{1,0:T(8,128)(2,1)S(1)}, bf16[2048,256]{1,0:T(8,128)(2,1)}, u32[]{:S(2)}) copy-start(bf16[2048,256]{1,0:T(8,128)(2,1)} %param.8) | copy-start | bytes 3145732
  10.8 1.2 copy-start.5
  36.2 1.1 copy-start.7
  37.3 1.6 %copy-start.2 = (bf16[1,512,2048]{2,1,0:T(8,128)(2,1)S(1)}, bf16[1,512,2048]{2,1,0:T(8,128)(2,1)}, u32[]{:S(2)}) copy-start(bf16[1,512,2048]{2,1,0:T(8,128)(2,1)} %param.11) | copy-start | bytes 6291460
  50.1 2.1 %copy-start.4 = (bf16[2048,256]{1,0:T(8,128)(2,1)S(1)}, bf16[2048,256]{1,0:T(8,128)(2,1)}, u32[]{:S(2)}) copy-start(bf16[2048,256]{1,0:T(8,128)(2,1)} %param.8) | copy-start | bytes 3145732
  52.2 1.2 copy-start.6
  56.1 2.2 %copy-start.1 = (f32[8,512,256]{2,1,0:T(8,128)S(1)}, f32[8,512,256]{2,1,0:T(8,128)}, u32[]{:S(2)}) copy-start(f32[8,512,256]{2,1,0:T(8,128)} %add_bitcast_fusion.term_ref) | copy-start | bytes 12582916
Sparse Core Ops, SparseCore 0:
  56.3 58.5 reduce-scatter.1

commit v7 on v6

--- a/solution.py
+++ b/solution.py
@@ -11,66 +11,85 @@
 MESH = pl.DeviceIdType.MESH
 
 
-def ring_scatter_kernel(n, axis, term_ref, out_ref, recv, sendbuf, send_sem, recv_sem):
-    me = lax.axis_index(axis)
-    right, left = lax.rem(me + 1, n), lax.rem(me + n - 1, n)
-    half = out_ref.shape[1] // 2
+def ring_scatter_kernel(jobs, *refs):
+    count = len(jobs)
+    terms, outs, scratch = refs[:count], refs[count:2 * count], refs[2 * count:]
     barrier = pltpu.get_barrier_semaphore()
-    for neighbour in (left, right):
-        pl.semaphore_signal(barrier, inc=1, device_id={axis: neighbour}, device_id_type=MESH)
-    pl.semaphore_wait(barrier, 2)
-    routes = ((right, -1), (left, 1))
-    copies = [[], []]
-    for step in range(n - 1):
-        for way, (dest, sign) in enumerate(routes):
-            block = lax.rem(me + n + sign * (step + 1), n)
+    places = []
+    for axis, n in jobs:
+        me = lax.axis_index(axis)
+        right, left = lax.rem(me + 1, n), lax.rem(me + n - 1, n)
+        places.append((me, right, left))
+        for neighbour in (left, right):
+            pl.semaphore_signal(barrier, inc=1, device_id={axis: neighbour}, device_id_type=MESH)
+    pl.semaphore_wait(barrier, 2 * count)
+    copies = [[[], []] for _ in jobs]
+    for step in range(max(n for _, n in jobs) - 1):
+        for job, (axis, n) in enumerate(jobs):
+            if step >= n - 1:
+                continue
+            me, right, left = places[job]
+            recv, sendbuf, send_sem, recv_sem = scratch[4 * job:4 * job + 4]
+            term_ref = terms[job]
+            half = outs[job].shape[1] // 2
+            for way, (dest, sign) in enumerate(((right, -1), (left, 1))):
+                block = lax.rem(me + n + sign * (step + 1), n)
+                cols = pl.ds(way * half, half)
+                if step == 0:
+                    src = term_ref.at[block, :, cols]
+                else:
+                    copies[job][way][step - 1].wait_recv()
+                    sendbuf[way, step] = recv[way, step - 1] + term_ref[block, :, cols]
+                    src = sendbuf.at[way, step]
+                copy = pltpu.make_async_remote_copy(
+                    src_ref=src,
+                    dst_ref=recv.at[way, step],
+                    send_sem=send_sem.at[way, step],
+                    recv_sem=recv_sem.at[way, step],
+                    device_id={axis: dest},
+                    device_id_type=MESH,
+                )
+                copy.start()
+                copies[job][way].append(copy)
+    for job, (axis, n) in enumerate(jobs):
+        me = places[job][0]
+        recv = scratch[4 * job]
+        half = outs[job].shape[1] // 2
+        for way in range(2):
             cols = pl.ds(way * half, half)
-            if step == 0:
-                src = term_ref.at[block, :, cols]
-            else:
-                copies[way][step - 1].wait_recv()
-                sendbuf[way, step] = recv[way, step - 1] + term_ref[block, :, cols]
-                src = sendbuf.at[way, step]
-            copy = pltpu.make_async_remote_copy(
-                src_ref=src,
-                dst_ref=recv.at[way, step],
-                send_sem=send_sem.at[way, step],
-                recv_sem=recv_sem.at[way, step],
-                device_id={axis: dest},
-                device_id_type=MESH,
-            )
-            copy.start()
-            copies[way].append(copy)
-    for way in range(2):
-        cols = pl.ds(way * half, half)
-        copies[way][n - 2].wait_recv()
-        out_ref[:, cols] = (recv[way, n - 2] + term_ref[me, :, cols]).astype(out_ref.dtype)
-    for way in range(2):
-        for copy in copies[way]:
-            copy.wait_send()
-
-
-def ring_scatter(terms, axis, out_dtype, channel):
-    n, rows, width = terms.shape
-    half = width // 2
-    return pl.pallas_call(
-        functools.partial(ring_scatter_kernel, n, axis),
-        out_shape=jax.ShapeDtypeStruct((rows, width), out_dtype),
-        in_specs=[pl.BlockSpec(memory_space=pltpu.VMEM)],
-        out_specs=pl.BlockSpec(memory_space=pltpu.VMEM),
-        scratch_shapes=[
-            pltpu.VMEM((2, n - 1, rows, half), jnp.float32),
-            pltpu.VMEM((2, n - 1, rows, half), jnp.float32),
+            copies[job][way][n - 2].wait_recv()
+            outs[job][:, cols] = (recv[way, n - 2] + terms[job][me, :, cols]).astype(outs[job].dtype)
+    for job in range(count):
+        for way in range(2):
+            for copy in copies[job][way]:
+                copy.wait_send()
+
+
+def ring_scatter(parts, channel):
+    jobs = tuple((axis, terms.shape[0]) for terms, axis, _ in parts)
+    scratch = []
+    for terms, _, _ in parts:
+        n, rows, width = terms.shape
+        scratch += [
+            pltpu.VMEM((2, n - 1, rows, width // 2), jnp.float32),
+            pltpu.VMEM((2, n - 1, rows, width // 2), jnp.float32),
             pltpu.SemaphoreType.DMA((2, n - 1)),
             pltpu.SemaphoreType.DMA((2, n - 1)),
-        ],
+        ]
+    size = sum(terms.size for terms, _, _ in parts)
+    return pl.pallas_call(
+        functools.partial(ring_scatter_kernel, jobs),
+        out_shape=tuple(
+            jax.ShapeDtypeStruct(terms.shape[1:], dtype) for terms, _, dtype in parts
+        ),
+        in_specs=[pl.BlockSpec(memory_space=pltpu.VMEM)] * len(parts),
+        out_specs=tuple(pl.BlockSpec(memory_space=pltpu.VMEM) for _ in parts),
+        scratch_shapes=scratch,
         compiler_params=pltpu.CompilerParams(
             collective_id=channel, has_side_effects=True, vmem_limit_bytes=48 * 1024 * 1024
         ),
-        cost_estimate=pl.CostEstimate(
-            flops=2 * n * rows * width, bytes_accessed=8 * n * rows * width, transcendentals=0
-        ),
-    )(terms)
+        cost_estimate=pl.CostEstimate(flops=2 * size, bytes_accessed=8 * size, transcendentals=0),
+    )(*(terms for terms, _, _ in parts))
 
 
 def exchange_kernel(n, axis, kv_ref, qg_ref, prefix_ref, suffix_ref, kv_in, qg_in, send_sem, recv_sem):
@@ -215,22 +234,32 @@
     )
     total_rows = lax.axis_size("seq") * lax.axis_size("dp") * num_rows
     grad_scale = jnp.float32(1.0) / jnp.sqrt(jnp.float32(total_rows))
+    seqs, shares = lax.axis_size("seq"), lax.axis_size("dp")
     grads = jnp.concatenate([d_query, d_keys, d_values], axis=1)
-    term_qkv = jnp.einsum("td,tk->dk", in_rows, grads, preferred_element_type=jnp.float32)
-    term_out = jnp.einsum("td,tk->dk", grad_rows, attention, preferred_element_type=jnp.float32)
-    terms = jnp.concatenate([term_qkv, term_out], axis=1) * grad_scale
-    terms, head_terms = lax.optimization_barrier((terms, head_terms))
-    summed = lax.psum_scatter(terms, "seq", scatter_dimension=0, tiled=True)
-    input_grad = ring_scatter(head_terms, "head", jnp.bfloat16, 0)[None]
-    summed, input_grad = lax.optimization_barrier((summed, input_grad))
-    shares = lax.axis_size("dp")
-    summed = ring_scatter(
-        summed.reshape(shares, summed.shape[0] // shares, summed.shape[1]), "dp", jnp.float32, 1
+    term_qkv = jnp.einsum("td,tk->dk", in_rows, grads, preferred_element_type=jnp.float32) * grad_scale
+    grad_blocks = grad_rows.reshape(num_rows, seqs, shares, -1)
+    term_out = jnp.einsum(
+        "tspr,tk->psrk", grad_blocks, attention, preferred_element_type=jnp.float32
+    ) * grad_scale
+    term_out = term_out.reshape(shares, -1, width)
+    term_qkv, head_terms, term_out = lax.optimization_barrier((term_qkv, head_terms, term_out))
+    summed = lax.psum_scatter(term_qkv, "seq", scatter_dimension=0, tiled=True)
+    input_grad, out_shared = ring_scatter(
+        [(head_terms, "head", jnp.bfloat16), (term_out, "dp", jnp.float32)], 0
+    )
+    input_grad = input_grad[None]
+    summed, input_grad, out_shared = lax.optimization_barrier((summed, input_grad, out_shared))
+    summed, out_summed = ring_scatter(
+        [
+            (summed.reshape(shares, -1, summed.shape[1]), "dp", jnp.float32),
+            (out_shared.reshape(seqs, -1, width), "seq", jnp.float32),
+        ],
+        1,
     )
     grad_query = summed[:, :width]
     grad_key = summed[:, width:2 * width]
-    grad_value = summed[:, 2 * width:3 * width]
-    grad_out = summed[:, 3 * width:].T
+    grad_value = summed[:, 2 * width:]
+    grad_out = out_summed.T
     return (input_grad, grad_query, grad_key, grad_value, grad_out)
 
 

time: 144 us -> 157 us (1.090)
  Pallas kernels: 91.6 us -> 98.8 us
  matrix products: 22.7 us -> 29.7 us
  other arithmetic: 6.28 us -> 0.24 us
  local copies, waits for them, and re-layouts: 8.09 us -> 12 us
    pallas_call x2, Pallas kernels: 74.8 us -> 82 us  [ring_scatter(): pl.pallas_call(functools.partial(ring_scatter_kernel, jobs), out_shape=tu...]
    mul x1, other arithmetic: 6.19 us -> 0.15 us  [local(): jnp.einsum('tspr,tk->psrk', grad_blocks, attention, preferred_element_typ...]
    dot_general x1, matrix products: 2.73 us -> 6.3 us  [local(): jnp.einsum('tk,bdk->btd', d_values, by_block(w_value), preferred_element_...]
    dot_general x1, matrix products: 1.8 us -> 4.46 us  [local(): jnp.einsum('td,tk->dk', in_rows, grads, preferred_element_type=jnp.float32)]
    unnamed x17 -> x26, local copies, waits for them, and re-layouts: 5.84 us -> 8.48 us
    dot_general x1 -> x0, matrix products: 2.07 us -> none  [local(): jnp.einsum('td,tk->dk', grad_rows, attention, preferred_element_type=jnp....]
    dot_general x1, matrix products: 0.76 us -> 2.79 us  [local(): jnp.einsum('tk,bdk->btd', d_keys, by_block(w_key), preferred_element_type...]
    dot_general x1, matrix products: 2.6 us -> 0.74 us  [local(): jnp.einsum('td,kd->tk', grad_rows, w_out, preferred_element_type=jnp.floa...]
  transfers between devices with their start and end apart: 1 -> 1, of which waited for: 0 -> 0; matrix products, arithmetic and copies ran while one was open for 0% -> 0% of each run, Pallas kernels for 40% -> 39%
where the time goes in v7:
time: 157 us; the launch traced here: 155 us
  Pallas kernels  98.8 us (63%)
  matrix products  29.7 us (19%)
  between operations  14.3 us (9%)
  local copies, waits for them, and re-layouts  12 us (8%)
    pallas_call x2, Pallas kernels, ring_scatter(): pl.pallas_call(functools.partial(ring_scatter_kernel, jobs), out_shape=tu...  82 us
    pallas_call x1, Pallas kernels, exchange_states(): pl.pallas_call(functools.partial(exchange_kernel, n, axis), out_shape=(ja...  16.8 us
    unnamed x26, local copies, waits for them, and re-layouts  8.48 us
    dot_general x1, matrix products, local(): jnp.einsum('tk,bdk->btd', d_values, by_block(w_value), preferred_element_...  6.3 us
    dot_general x1, matrix products, local(): jnp.einsum('td,tk->dk', in_rows, grads, preferred_element_type=jnp.float32)  4.46 us
    dot_general x3, matrix products, project(): jnp.dot(in_rows, weight, preferred_element_type=jnp.float32)  3.51 us
  transfers between devices with their start and end apart: 1, of which 0 were waited for; matrix products, arithmetic and copies ran while one was open for 0% of the time, Pallas kernels for 39%

profile of v7, /device:TPU:8, one launch (start us, length us, event | category | flops | bytes accessed | tf_op | source)
XLA Modules:
  0.0 155.0 jit_solution(11329882401249824376)
XLA Ops:
  7.3 1.4 copy-done
  8.8 2.0 %fusion.28 = bf16[512,256]{0,1:T(8,128)(2,1)S(1)} fusion(bf16[2048,256]{1,0:T(8,128)(2,1)} %param.7, bf16[1,512,2048]{2,1,0:T(8,128)(2,1)S(1)} %copy-done), kind=kOutput, calls=%fused_computation.29 | convolution fusion | flops 537001984 | bytes 3407872 | tf_op jit(solution)/shard_map/dot_general | solution.py:174
  10.8 0.8 fusion.22
  12.0 0.8 fusion.25
  12.8 0.8 copy-done.3
  13.8 0.7 fusion.18
  14.6 0.9 fusion.47.qg_ref
  15.5 0.9 fusion.46.kv_ref
  16.4 16.8 %shard_map.101 = (f32[2,128,128]{2,1,0:T(8,128)}, f32[2,128,128]{2,1,0:T(8,128)}) custom-call(f32[2,128,128]{2,1,0:T(8,128)} %fusion.46.kv_ref, f32[2,128,128]{2,1,0:T(8,128)} %fusion.47.qg_ref), custom_call_target="tpu_custom_call" | custom-call | tf_op jit(solution)/shard_map/pallas_call | solution.py:151
  33.2 1.2 fusion.40
  34.4 1.1 fusion.42
  35.5 1.2 fusion.36
  39.6 0.8 copy-done.4
  40.4 1.0 fusion
  41.5 1.4 copy.47
  43.1 2.8 %fusion.49 = f32[512,8,256]{2,0,1:T(8,128)} fusion(bf16[512,256,1]{0,1,2:T(8,128)(2,1)S(1)} %bitcast.120, bf16[8,256,256]{2,1,0:T(8,128)(2,1)S(1)} %bitcast.125), kind=kOutput, calls=%fused_computation.50 | convolution fusion | flops 536870912 | bytes 5505024 | tf_op jit(solution)/shard_map/tk,bdk->btd/dot_general | solution.py:229
  45.9 2.8 %fusion.48 = f32[512,8,256]{2,0,1:T(8,128)} fusion(bf16[512,256,1]{0,1,2:T(8,128)(2,1)S(1)} %bitcast.122, bf16[8,256,256]{2,1,0:T(8,128)(2,1)S(1)} %bitcast.126), kind=kOutput, calls=%fused_computation.49 | convolution fusion | flops 536870912 | bytes 5505024 | tf_op jit(solution)/shard_map/tk,bdk->btd/dot_general | solution.py:228
  48.7 4.5 %multiply_bitcast_fusion = f32[2048,768]{0,1:T(8,128)} fusion(bf16[1,512,2048]{2,1,0:T(8,128)(2,1)S(1)} %copy-done, bf16[512,256]{0,1:T(8,128)(2,1)S(1)} %bitcast.106, bf16[512,256]{0,1:T(8,128)(2,1)S(1)} %bitcast.121, bf16[512,256]{0,1:T(8,128)(2,1)S(1)} %bitcast.123), kind=kOutput, calls=%fused_computation | convolution fusion | flops 1614544896 | bytes 9175040 | tf_op jit(solution)/shard_map/td,tk->dk/dot_general | solution.py:239
  53.2 6.3 %add_bitcast_fusion.refs_0_ = f32[8,512,256]{2,1,0:T(8,128)} fusion(f32[512,8,256]{2,0,1:T(8,128)} %fusion.48, f32[512,8,256]{2,0,1:T(8,128)} %fusion.49, bf16[512,256,1]{0,1,2:T(8,128)(2,1)S(1)} %bitcast.107, bf16[8,256,256]{2,1,0:T(8,128)(2,1)S(1)} %bitcast.127), kind=kOutput, calls=%fused_computation.1 | convolution fusion | flops 538968064 | bytes 13893632 | tf_op jit(solution)/shard_map/tk,bdk->btd/dot_general | solution.py:232
  59.5 1.6 %copy-done.1 = f32[4,8,64,256]{3,2,1,0:T(8,128)S(1)} copy-done((f32[4,8,64,256]{3,2,1,0:T(8,128)S(1)}, f32[4,8,64,256]{3,2,1,0:T(8,128)}, u32[]{:S(2)}) %copy-start.1) | copy-done | bytes 2097176
  61.1 60.3 %shard_map.102 = (bf16[512,256]{1,0:T(8,128)(2,1)S(1)}, f32[512,256]{1,0:T(8,128)S(1)}) custom-call(f32[8,512,256]{2,1,0:T(8,128)} %add_bitcast_fusion.refs_0_, f32[4,512,256]{2,1,0:T(8,128)S(1)} %bitcast.96), custom_call_target="tpu_custom_call" | custom-call | flops 3145728 | bytes 12582912 | tf_op jit(solution)/shard_map/pallas_call | solution.py:80
  122.1 1.4 copy.48
  123.5 21.7 %shard_map.103 = (f32[64,768]{1,0:T(8,128)S(1)}, f32[64,256]{1,0:T(8,128)S(1)}) custom-call(f32[4,64,768]{2,1,0:T(8,128)S(1)} %bitcast.97, f32[8,64,256]{2,1,0:T(8,128)S(1)} %bitcast.98), custom_call_target="tpu_custom_call" | custom-call | flops 655360 | bytes 2621440 | tf_op jit(solution)/shard_map/pallas_call | solution.py:80
  145.9 1.7 %copy.70 = bf16[1,512,256]{2,1,0:T(8,128)(2,1)} copy(bf16[1,512,256]{2,1,0:T(8,128)(2,1)} %bitcast.99) | data formatting | bytes 524288
  (35 shorter events, 6.0 us)
Async XLA Ops:
  7.2 1.6 %copy-start = (bf16[1,512,2048]{2,1,0:T(8,128)(2,1)S(1)}, bf16[1,512,2048]{2,1,0:T(8,128)(2,1)}, u32[]{:S(2)}) copy-start(bf16[1,512,2048]{2,1,0:T(8,128)(2,1)} %param.6) | copy-start | bytes 6291460
  7.2 114.9 %reduce-scatter.2.cloned.1.call-start = ((), (), s32[]{:S(2)}) async-start(), calls=%async_computation.1 | async-start | bytes 7077888 | tf_op jit(solution)/shard_map/reduce_scatter | solution.py:246
  7.3 3.4 %copy-start.5 = (bf16[2048,256]{1,0:T(8,128)(2,1)S(1)}, bf16[2048,256]{1,0:T(8,128)(2,1)}, u32[]{:S(2)}) copy-start(bf16[2048,256]{1,0:T(8,128)(2,1)} %param.8) | copy-start | bytes 3145732
  10.8 1.2 copy-start.8
  12.0 1.6 %copy-start.3 = (bf16[1,512,2048]{2,1,0:T(8,128)(2,1)S(1)}, bf16[1,512,2048]{2,1,0:T(8,128)(2,1)}, u32[]{:S(2)}) copy-start(bf16[1,512,2048]{2,1,0:T(8,128)(2,1)} %param.11) | copy-start | bytes 6291460
  12.0 1.9 %copy-start.11 = (bf16[256,2048]{1,0:T(8,128)(2,1)S(1)}, bf16[256,2048]{1,0:T(8,128)(2,1)}, u32[]{:S(2)}) copy-start(bf16[256,2048]{1,0:T(8,128)(2,1)} %param.10) | copy-start | bytes 3145732
  33.1 3.5 %copy-start.10 = (f32[2,128,128]{2,1,0:T(8,128)S(1)}, f32[2,128,128]{2,1,0:T(8,128)}, u32[]{:S(2)}) copy-start(f32[2,128,128]{2,1,0:T(8,128)} %get-tuple-element.18) | copy-start | bytes 393220
  38.8 1.6 %copy-start.4 = (bf16[1,512,2048]{2,1,0:T(8,128)(2,1)S(1)}, bf16[1,512,2048]{2,1,0:T(8,128)(2,1)}, u32[]{:S(2)}) copy-start(bf16[1,512,2048]{2,1,0:T(8,128)(2,1)} %param.11) | copy-start | bytes 6291460
  41.5 1.6 %copy-start.6 = (bf16[2048,256]{1,0:T(8,128)(2,1)S(1)}, bf16[2048,256]{1,0:T(8,128)(2,1)}, u32[]{:S(2)}) copy-start(bf16[2048,256]{1,0:T(8,128)(2,1)} %param.8) | copy-start | bytes 3145732
  43.1 2.8 %copy-start.7 = (bf16[2048,256]{1,0:T(8,128)(2,1)S(1)}, bf16[2048,256]{1,0:T(8,128)(2,1)}, u32[]{:S(2)}) copy-start(bf16[2048,256]{1,0:T(8,128)(2,1)} %param.7) | copy-start | bytes 3145732
  48.7 4.5 %copy-start.9 = (bf16[2048,256]{1,0:T(8,128)(2,1)S(1)}, bf16[2048,256]{1,0:T(8,128)(2,1)}, u32[]{:S(2)}) copy-start(bf16[2048,256]{1,0:T(8,128)(2,1)} %param.9) | copy-start | bytes 3145732
  59.5 1.6 %copy-start.1 = (f32[4,8,64,256]{3,2,1,0:T(8,128)S(1)}, f32[4,8,64,256]{3,2,1,0:T(8,128)}, u32[]{:S(2)}) copy-start(f32[4,8,64,256]{3,2,1,0:T(8,128)} %copy.47) | copy-start | bytes 6291460
  121.4 0.7 copy-start.2
Sparse Core Ops, SparseCore 0:
  59.6 48.7 reduce-scatter.1

commit v8 on v7

--- a/solution.py
+++ b/solution.py
@@ -9,6 +9,7 @@
 
 HEAD_DIM = 128
 MESH = pl.DeviceIdType.MESH
+PIECES = 2
 
 
 def ring_scatter_kernel(jobs, *refs):
@@ -23,7 +24,8 @@
         for neighbour in (left, right):
             pl.semaphore_signal(barrier, inc=1, device_id={axis: neighbour}, device_id_type=MESH)
     pl.semaphore_wait(barrier, 2 * count)
-    copies = [[[], []] for _ in jobs]
+    ways = [(way, piece) for piece in range(PIECES) for way in range(2)]
+    copies = [[[] for _ in ways] for _ in jobs]
     for step in range(max(n for _, n in jobs) - 1):
         for job, (axis, n) in enumerate(jobs):
             if step >= n - 1:
@@ -31,37 +33,40 @@
             me, right, left = places[job]
             recv, sendbuf, send_sem, recv_sem = scratch[4 * job:4 * job + 4]
             term_ref = terms[job]
-            half = outs[job].shape[1] // 2
-            for way, (dest, sign) in enumerate(((right, -1), (left, 1))):
+            rows, half = outs[job].shape[0] // PIECES, outs[job].shape[1] // 2
+            for slot, (way, piece) in enumerate(ways):
+                dest, sign = ((right, -1), (left, 1))[way]
                 block = lax.rem(me + n + sign * (step + 1), n)
-                cols = pl.ds(way * half, half)
+                span = (pl.ds(piece * rows, rows), pl.ds(way * half, half))
                 if step == 0:
-                    src = term_ref.at[block, :, cols]
+                    src = term_ref.at[block, span[0], span[1]]
                 else:
-                    copies[job][way][step - 1].wait_recv()
-                    sendbuf[way, step] = recv[way, step - 1] + term_ref[block, :, cols]
-                    src = sendbuf.at[way, step]
+                    copies[job][slot][step - 1].wait_recv()
+                    sendbuf[slot, step] = recv[slot, step - 1] + term_ref[block, span[0], span[1]]
+                    src = sendbuf.at[slot, step]
                 copy = pltpu.make_async_remote_copy(
                     src_ref=src,
-                    dst_ref=recv.at[way, step],
-                    send_sem=send_sem.at[way, step],
-                    recv_sem=recv_sem.at[way, step],
+                    dst_ref=recv.at[slot, step],
+                    send_sem=send_sem.at[slot, step],
+                    recv_sem=recv_sem.at[slot, step],
                     device_id={axis: dest},
                     device_id_type=MESH,
                 )
                 copy.start()
-                copies[job][way].append(copy)
+                copies[job][slot].append(copy)
     for job, (axis, n) in enumerate(jobs):
         me = places[job][0]
         recv = scratch[4 * job]
-        half = outs[job].shape[1] // 2
-        for way in range(2):
-            cols = pl.ds(way * half, half)
-            copies[job][way][n - 2].wait_recv()
-            outs[job][:, cols] = (recv[way, n - 2] + terms[job][me, :, cols]).astype(outs[job].dtype)
+        rows, half = outs[job].shape[0] // PIECES, outs[job].shape[1] // 2
+        for slot, (way, piece) in enumerate(ways):
+            span = (pl.ds(piece * rows, rows), pl.ds(way * half, half))
+            copies[job][slot][n - 2].wait_recv()
+            outs[job][span[0], span[1]] = (
+                recv[slot, n - 2] + terms[job][me, span[0], span[1]]
+            ).astype(outs[job].dtype)
     for job in range(count):
-        for way in range(2):
-            for copy in copies[job][way]:
+        for slot in range(len(ways)):
+            for copy in copies[job][slot]:
                 copy.wait_send()
 
 
@@ -71,10 +76,10 @@
     for terms, _, _ in parts:
         n, rows, width = terms.shape
         scratch += [
-            pltpu.VMEM((2, n - 1, rows, width // 2), jnp.float32),
-            pltpu.VMEM((2, n - 1, rows, width // 2), jnp.float32),
-            pltpu.SemaphoreType.DMA((2, n - 1)),
-            pltpu.SemaphoreType.DMA((2, n - 1)),
+            pltpu.VMEM((2 * PIECES, n - 1, rows // PIECES, width // 2), jnp.float32),
+            pltpu.VMEM((2 * PIECES, n - 1, rows // PIECES, width // 2), jnp.float32),
+            pltpu.SemaphoreType.DMA((2 * PIECES, n - 1)),
+            pltpu.SemaphoreType.DMA((2 * PIECES, n - 1)),
         ]
     size = sum(terms.size for terms, _, _ in parts)
     return pl.pallas_call(
@@ -249,13 +254,8 @@
     )
     input_grad = input_grad[None]
     summed, input_grad, out_shared = lax.optimization_barrier((summed, input_grad, out_shared))
-    summed, out_summed = ring_scatter(
-        [
-            (summed.reshape(shares, -1, summed.shape[1]), "dp", jnp.float32),
-            (out_shared.reshape(seqs, -1, width), "seq", jnp.float32),
-        ],
-        1,
-    )
+    out_summed = lax.psum_scatter(out_shared, "seq", scatter_dimension=0, tiled=True)
+    (summed,) = ring_scatter([(summed.reshape(shares, -1, summed.shape[1]), "dp", jnp.float32)], 1)
     grad_query = summed[:, :width]
     grad_key = summed[:, width:2 * width]
     grad_value = summed[:, 2 * width:]

time: 157 us -> 152 us (0.968); the launches traced: 155 us -> 152 us
  Pallas kernels: 98.8 us -> 82.2 us
  waiting for transfers between devices: 0.02 us -> 15.9 us
  local copies, waits for them, and re-layouts: 12 us -> 9.71 us
    pallas_call x2, Pallas kernels: 82 us -> 65.4 us  [ring_scatter(): pl.pallas_call(functools.partial(ring_scatter_kernel, jobs), out_shape=tu...]
    reduce_scatter x0 -> x1, waiting for transfers between devices: none -> 15.9 us  [local(): lax.psum_scatter(out_shared, 'seq', scatter_dimension=0, tiled=True)]
    unnamed x26 -> x23, local copies, waits for them, and re-layouts: 8.48 us -> 6.2 us
  transfers between devices with their start and end apart: 1 -> 2, of which waited for: 0 -> 1; matrix products, arithmetic and copies ran while one was open for 0% -> 1% of each run, Pallas kernels for 39% -> 43%
where the time goes in v8:
time: 152 us
  Pallas kernels  82.2 us (54%)
  matrix products  29.6 us (19%)
  waiting for transfers between devices  15.9 us (10%)
  between operations  14.3 us (9%)
  local copies, waits for them, and re-layouts  9.71 us (6%)
    pallas_call x2, Pallas kernels, ring_scatter(): pl.pallas_call(functools.partial(ring_scatter_kernel, jobs), out_shape=tu...  65.4 us
    pallas_call x1, Pallas kernels, exchange_states(): pl.pallas_call(functools.partial(exchange_kernel, n, axis), out_shape=(ja...  16.8 us
    reduce_scatter x1, waiting for transfers between devices, local(): lax.psum_scatter(out_shared, 'seq', scatter_dimension=0, tiled=True)  15.9 us
    dot_general x1, matrix products, local(): jnp.einsum('tk,bdk->btd', d_values, by_block(w_value), preferred_element_...  6.29 us
    unnamed x23, local copies, waits for them, and re-layouts  6.2 us
    dot_general x1, matrix products, local(): jnp.einsum('td,tk->dk', in_rows, grads, preferred_element_type=jnp.float32)  4.44 us
    dot_general x3, matrix products, project(): jnp.dot(in_rows, weight, preferred_element_type=jnp.float32)  3.51 us
  transfers between devices with their start and end apart: 2, of which 1 were waited for; matrix products, arithmetic and copies ran while one was open for 1% of the time, Pallas kernels for 43%

profile of v8, /device:TPU:8, one launch (start us, length us, event | category | flops | bytes accessed | tf_op | source)
XLA Modules:
  0.0 152.1 jit_solution(272658878596166238)
XLA Ops:
  7.3 1.4 copy-done
  8.8 2.0 %fusion.28 = bf16[512,256]{0,1:T(8,128)(2,1)S(1)} fusion(bf16[2048,256]{1,0:T(8,128)(2,1)} %param.7, bf16[1,512,2048]{2,1,0:T(8,128)(2,1)S(1)} %copy-done), kind=kOutput, calls=%fused_computation.29 | convolution fusion | flops 537001984 | bytes 3407872 | tf_op jit(solution)/shard_map/dot_general | solution.py:179
  10.8 0.8 fusion.22
  12.0 0.8 fusion.25
  12.8 0.8 copy-done.2
  13.8 0.7 fusion.18
  14.6 0.9 fusion.47.qg_ref
  15.5 0.9 fusion.46.kv_ref
  16.4 16.8 %shard_map.101 = (f32[2,128,128]{2,1,0:T(8,128)}, f32[2,128,128]{2,1,0:T(8,128)}) custom-call(f32[2,128,128]{2,1,0:T(8,128)} %fusion.46.kv_ref, f32[2,128,128]{2,1,0:T(8,128)} %fusion.47.qg_ref), custom_call_target="tpu_custom_call" | custom-call | tf_op jit(solution)/shard_map/pallas_call | solution.py:156
  33.1 1.2 fusion.40
  34.3 1.1 fusion.42
  35.5 1.2 fusion.36
  39.6 0.8 copy-done.3
  40.3 1.0 fusion
  41.5 1.4 copy.47
  43.1 2.8 %fusion.49 = f32[512,8,256]{2,0,1:T(8,128)} fusion(bf16[512,256,1]{0,1,2:T(8,128)(2,1)S(1)} %bitcast.117, bf16[8,256,256]{2,1,0:T(8,128)(2,1)S(1)} %bitcast.122), kind=kOutput, calls=%fused_computation.50 | convolution fusion | flops 536870912 | bytes 5505024 | tf_op jit(solution)/shard_map/tk,bdk->btd/dot_general | solution.py:234
  45.9 2.8 %fusion.48 = f32[512,8,256]{2,0,1:T(8,128)} fusion(bf16[512,256,1]{0,1,2:T(8,128)(2,1)S(1)} %bitcast.119, bf16[8,256,256]{2,1,0:T(8,128)(2,1)S(1)} %bitcast.123), kind=kOutput, calls=%fused_computation.49 | convolution fusion | flops 536870912 | bytes 5505024 | tf_op jit(solution)/shard_map/tk,bdk->btd/dot_general | solution.py:233
  48.7 4.4 %multiply_bitcast_fusion = f32[2048,768]{0,1:T(8,128)} fusion(bf16[1,512,2048]{2,1,0:T(8,128)(2,1)S(1)} %copy-done, bf16[512,256]{0,1:T(8,128)(2,1)S(1)} %bitcast.103, bf16[512,256]{0,1:T(8,128)(2,1)S(1)} %bitcast.118, bf16[512,256]{0,1:T(8,128)(2,1)S(1)} %bitcast.120), kind=kOutput, calls=%fused_computation | convolution fusion | flops 1614544896 | bytes 9175040 | tf_op jit(solution)/shard_map/td,tk->dk/dot_general | solution.py:244
  53.1 6.3 %add_bitcast_fusion.refs_0_ = f32[8,512,256]{2,1,0:T(8,128)} fusion(f32[512,8,256]{2,0,1:T(8,128)} %fusion.48, f32[512,8,256]{2,0,1:T(8,128)} %fusion.49, bf16[512,256,1]{0,1,2:T(8,128)(2,1)S(1)} %bitcast.104, bf16[8,256,256]{2,1,0:T(8,128)(2,1)S(1)} %bitcast.124), kind=kOutput, calls=%fused_computation.1 | convolution fusion | flops 538968064 | bytes 13893632 | tf_op jit(solution)/shard_map/tk,bdk->btd/dot_general | solution.py:237
  59.5 1.6 %copy-done.1 = f32[4,8,64,256]{3,2,1,0:T(8,128)S(1)} copy-done((f32[4,8,64,256]{3,2,1,0:T(8,128)S(1)}, f32[4,8,64,256]{3,2,1,0:T(8,128)}, u32[]{:S(2)}) %copy-start.1) | copy-done | bytes 2097176
  61.1 52.1 %shard_map.102 = (bf16[512,256]{1,0:T(8,128)(2,1)S(1)}, f32[512,256]{1,0:T(8,128)}) custom-call(f32[8,512,256]{2,1,0:T(8,128)} %add_bitcast_fusion.refs_0_, f32[4,512,256]{2,1,0:T(8,128)S(1)} %bitcast.95), custom_call_target="tpu_custom_call" | custom-call | flops 3145728 | bytes 12582912 | tf_op jit(solution)/shard_map/pallas_call | solution.py:85
  113.3 1.4 copy.48
  114.7 13.3 %shard_map.103 = f32[64,768]{1,0:T(8,128)S(1)} custom-call(f32[4,64,768]{2,1,0:T(8,128)S(1)} %bitcast.96), custom_call_target="tpu_custom_call" | custom-call | flops 393216 | bytes 1572864 | tf_op jit(solution)/shard_map/pallas_call | solution.py:85
  128.7 15.9 %reduce-scatter.5.cloned.1.call-done = f32[64,256]{1,0:T(8,128)} async-done(((f32[512,256]{1,0:T(8,128)}), f32[64,256]{1,0:T(8,128)}) %reduce-scatter.5.cloned.1.call-update) | async-done | bytes 65552 | tf_op jit(solution)/shard_map/reduce_scatter | solution.py:257
  (35 shorter events, 5.5 us)
Async XLA Ops:
  7.2 1.6 %copy-start = (bf16[1,512,2048]{2,1,0:T(8,128)(2,1)S(1)}, bf16[1,512,2048]{2,1,0:T(8,128)(2,1)}, u32[]{:S(2)}) copy-start(bf16[1,512,2048]{2,1,0:T(8,128)(2,1)} %param.6) | copy-start | bytes 6291460
  7.2 106.1 %reduce-scatter.3.cloned.1.call-start = ((), (), s32[]{:S(2)}) async-start(), calls=%async_computation.2 | async-start | bytes 7077888 | tf_op jit(solution)/shard_map/reduce_scatter | solution.py:251
  7.3 3.4 %copy-start.4 = (bf16[2048,256]{1,0:T(8,128)(2,1)S(1)}, bf16[2048,256]{1,0:T(8,128)(2,1)}, u32[]{:S(2)}) copy-start(bf16[2048,256]{1,0:T(8,128)(2,1)} %param.8) | copy-start | bytes 3145732
  10.8 1.2 copy-start.7
  12.0 1.6 %copy-start.2 = (bf16[1,512,2048]{2,1,0:T(8,128)(2,1)S(1)}, bf16[1,512,2048]{2,1,0:T(8,128)(2,1)}, u32[]{:S(2)}) copy-start(bf16[1,512,2048]{2,1,0:T(8,128)(2,1)} %param.11) | copy-start | bytes 6291460
  12.0 1.9 %copy-start.10 = (bf16[256,2048]{1,0:T(8,128)(2,1)S(1)}, bf16[256,2048]{1,0:T(8,128)(2,1)}, u32[]{:S(2)}) copy-start(bf16[256,2048]{1,0:T(8,128)(2,1)} %param.10) | copy-start | bytes 3145732
  33.1 3.5 %copy-start.9 = (f32[2,128,128]{2,1,0:T(8,128)S(1)}, f32[2,128,128]{2,1,0:T(8,128)}, u32[]{:S(2)}) copy-start(f32[2,128,128]{2,1,0:T(8,128)} %get-tuple-element.16) | copy-start | bytes 393220
  38.8 1.6 %copy-start.3 = (bf16[1,512,2048]{2,1,0:T(8,128)(2,1)S(1)}, bf16[1,512,2048]{2,1,0:T(8,128)(2,1)}, u32[]{:S(2)}) copy-start(bf16[1,512,2048]{2,1,0:T(8,128)(2,1)} %param.11) | copy-start | bytes 6291460
  41.5 1.6 %copy-start.5 = (bf16[2048,256]{1,0:T(8,128)(2,1)S(1)}, bf16[2048,256]{1,0:T(8,128)(2,1)}, u32[]{:S(2)}) copy-start(bf16[2048,256]{1,0:T(8,128)(2,1)} %param.8) | copy-start | bytes 3145732
  43.1 2.8 %copy-start.6 = (bf16[2048,256]{1,0:T(8,128)(2,1)S(1)}, bf16[2048,256]{1,0:T(8,128)(2,1)}, u32[]{:S(2)}) copy-start(bf16[2048,256]{1,0:T(8,128)(2,1)} %param.7) | copy-start | bytes 3145732
  48.7 4.4 %copy-start.8 = (bf16[2048,256]{1,0:T(8,128)(2,1)S(1)}, bf16[2048,256]{1,0:T(8,128)(2,1)}, u32[]{:S(2)}) copy-start(bf16[2048,256]{1,0:T(8,128)(2,1)} %param.9) | copy-start | bytes 3145732
  59.5 85.1 %reduce-scatter.5.cloned.1.call-start = ((), (), s32[]{:S(2)}) async-start(), calls=%async_computation.3 | async-start | bytes 589824 | tf_op jit(solution)/shard_map/reduce_scatter | solution.py:257
  59.5 1.6 %copy-start.1 = (f32[4,8,64,256]{3,2,1,0:T(8,128)S(1)}, f32[4,8,64,256]{3,2,1,0:T(8,128)}, u32[]{:S(2)}) copy-start(f32[4,8,64,256]{3,2,1,0:T(8,128)} %copy.47) | copy-start | bytes 6291460
Sparse Core Ops, SparseCore 0:
  59.6 48.5 reduce-scatter.2
  113.4 31.0 reduce-scatter.4

commit v9 on v8

--- a/solution.py
+++ b/solution.py
@@ -9,32 +9,55 @@
 
 HEAD_DIM = 128
 MESH = pl.DeviceIdType.MESH
-PIECES = 2
 
 
 def ring_scatter_kernel(jobs, *refs):
     count = len(jobs)
     terms, outs, scratch = refs[:count], refs[count:2 * count], refs[2 * count:]
     barrier = pltpu.get_barrier_semaphore()
-    places = []
-    for axis, n in jobs:
+    places, greeted = [], 0
+    for axis, n, _, direct in jobs:
         me = lax.axis_index(axis)
         right, left = lax.rem(me + 1, n), lax.rem(me + n - 1, n)
         places.append((me, right, left))
-        for neighbour in (left, right):
-            pl.semaphore_signal(barrier, inc=1, device_id={axis: neighbour}, device_id_type=MESH)
-    pl.semaphore_wait(barrier, 2 * count)
-    ways = [(way, piece) for piece in range(PIECES) for way in range(2)]
-    copies = [[[] for _ in ways] for _ in jobs]
-    for step in range(max(n for _, n in jobs) - 1):
-        for job, (axis, n) in enumerate(jobs):
-            if step >= n - 1:
+        offsets = range(1, n) if direct else (n - 1, 1)
+        for offset in offsets:
+            pl.semaphore_signal(
+                barrier, inc=1, device_id={axis: lax.rem(me + offset, n)}, device_id_type=MESH
+            )
+        greeted += len(offsets)
+    pl.semaphore_wait(barrier, greeted)
+
+    def direct_copy(job, offset):
+        axis, n, _, _ = jobs[job]
+        me = places[job][0]
+        recv, send_sem, recv_sem = scratch[4 * job], scratch[4 * job + 2], scratch[4 * job + 3]
+        peer = lax.rem(me + offset, n)
+        return pltpu.make_async_remote_copy(
+            src_ref=terms[job].at[peer],
+            dst_ref=recv.at[me],
+            send_sem=send_sem.at[offset],
+            recv_sem=recv_sem.at[me],
+            device_id={axis: peer},
+            device_id_type=MESH,
+        )
+
+    for job, (axis, n, _, direct) in enumerate(jobs):
+        if direct:
+            for offset in range(1, n):
+                direct_copy(job, offset).start()
+
+    copies = [[[] for _ in range(2 * pieces)] for _, _, pieces, _ in jobs]
+    for step in range(max(n for _, n, _, _ in jobs) - 1):
+        for job, (axis, n, pieces, direct) in enumerate(jobs):
+            if direct or step >= n - 1:
                 continue
             me, right, left = places[job]
             recv, sendbuf, send_sem, recv_sem = scratch[4 * job:4 * job + 4]
             term_ref = terms[job]
-            rows, half = outs[job].shape[0] // PIECES, outs[job].shape[1] // 2
-            for slot, (way, piece) in enumerate(ways):
+            rows, half = outs[job].shape[0] // pieces, outs[job].shape[1] // 2
+            for slot in range(2 * pieces):
+                piece, way = divmod(slot, 2)
                 dest, sign = ((right, -1), (left, 1))[way]
                 block = lax.rem(me + n + sign * (step + 1), n)
                 span = (pl.ds(piece * rows, rows), pl.ds(way * half, half))
@@ -54,38 +77,65 @@
                 )
                 copy.start()
                 copies[job][slot].append(copy)
-    for job, (axis, n) in enumerate(jobs):
+    for job, (axis, n, pieces, direct) in enumerate(jobs):
         me = places[job][0]
         recv = scratch[4 * job]
-        rows, half = outs[job].shape[0] // PIECES, outs[job].shape[1] // 2
-        for slot, (way, piece) in enumerate(ways):
+        if direct:
+            outs[job][...] = terms[job][me]
+            for sender in range(n):
+                @pl.when(sender != me)
+                def _():
+                    pltpu.make_async_remote_copy(
+                        src_ref=terms[job].at[sender],
+                        dst_ref=recv.at[sender],
+                        send_sem=scratch[4 * job + 2].at[0],
+                        recv_sem=scratch[4 * job + 3].at[sender],
+                        device_id={axis: sender},
+                        device_id_type=MESH,
+                    ).wait_recv()
+                    outs[job][...] += recv[sender]
+            continue
+        rows, half = outs[job].shape[0] // pieces, outs[job].shape[1] // 2
+        for slot in range(2 * pieces):
+            piece, way = divmod(slot, 2)
             span = (pl.ds(piece * rows, rows), pl.ds(way * half, half))
             copies[job][slot][n - 2].wait_recv()
             outs[job][span[0], span[1]] = (
                 recv[slot, n - 2] + terms[job][me, span[0], span[1]]
             ).astype(outs[job].dtype)
-    for job in range(count):
-        for slot in range(len(ways)):
+    for job, (axis, n, pieces, direct) in enumerate(jobs):
+        if direct:
+            for offset in range(1, n):
+                direct_copy(job, offset).wait_send()
+        for slot in range(2 * pieces):
             for copy in copies[job][slot]:
                 copy.wait_send()
 
 
 def ring_scatter(parts, channel):
-    jobs = tuple((axis, terms.shape[0]) for terms, axis, _ in parts)
+    jobs = tuple((axis, terms.shape[0], pieces, direct) for terms, axis, _, pieces, direct in parts)
     scratch = []
-    for terms, _, _ in parts:
+    for terms, _, _, pieces, direct in parts:
         n, rows, width = terms.shape
+        if direct:
+            scratch += [
+                pltpu.VMEM((n, rows, width), jnp.float32),
+                pltpu.VMEM((8, 128), jnp.float32),
+                pltpu.SemaphoreType.DMA((n,)),
+                pltpu.SemaphoreType.DMA((n,)),
+            ]
+            continue
         scratch += [
-            pltpu.VMEM((2 * PIECES, n - 1, rows // PIECES, width // 2), jnp.float32),
-            pltpu.VMEM((2 * PIECES, n - 1, rows // PIECES, width // 2), jnp.float32),
-            pltpu.SemaphoreType.DMA((2 * PIECES, n - 1)),
-            pltpu.SemaphoreType.DMA((2 * PIECES, n - 1)),
+            pltpu.VMEM((2 * pieces, n - 1, rows // pieces, width // 2), jnp.float32),
+            pltpu.VMEM((2 * pieces, n - 1, rows // pieces, width // 2), jnp.float32),
+            pltpu.SemaphoreType.DMA((2 * pieces, n - 1)),
+            pltpu.SemaphoreType.DMA((2 * pieces, n - 1)),
         ]
-    size = sum(terms.size for terms, _, _ in parts)
+    size = sum(part[0].size for part in parts)
     return pl.pallas_call(
         functools.partial(ring_scatter_kernel, jobs),
         out_shape=tuple(
-            jax.ShapeDtypeStruct(terms.shape[1:], dtype) for terms, _, dtype in parts
+            jax.ShapeDtypeStruct(part[0].shape[1:], part[2]) for part in parts
         ),
         in_specs=[pl.BlockSpec(memory_space=pltpu.VMEM)] * len(parts),
         out_specs=tuple(pl.BlockSpec(memory_space=pltpu.VMEM) for _ in parts),
@@ -94,7 +144,7 @@
             collective_id=channel, has_side_effects=True, vmem_limit_bytes=48 * 1024 * 1024
         ),
         cost_estimate=pl.CostEstimate(flops=2 * size, bytes_accessed=8 * size, transcendentals=0),
-    )(*(terms for terms, _, _ in parts))
+    )(*(part[0] for part in parts))
 
 
 def exchange_kernel(n, axis, kv_ref, qg_ref, prefix_ref, suffix_ref, kv_in, qg_in, send_sem, recv_sem):
@@ -250,12 +300,17 @@
     term_qkv, head_terms, term_out = lax.optimization_barrier((term_qkv, head_terms, term_out))
     summed = lax.psum_scatter(term_qkv, "seq", scatter_dimension=0, tiled=True)
     input_grad, out_shared = ring_scatter(
-        [(head_terms, "head", jnp.bfloat16), (term_out, "dp", jnp.float32)], 0
+        [(head_terms, "head", jnp.bfloat16, 4, False), (term_out, "dp", jnp.float32, 2, False)], 0
     )
     input_grad = input_grad[None]
     summed, input_grad, out_shared = lax.optimization_barrier((summed, input_grad, out_shared))
-    out_summed = lax.psum_scatter(out_shared, "seq", scatter_dimension=0, tiled=True)
-    (summed,) = ring_scatter([(summed.reshape(shares, -1, summed.shape[1]), "dp", jnp.float32)], 1)
+    summed, out_summed = ring_scatter(
+        [
+            (summed.reshape(shares, -1, summed.shape[1]), "dp", jnp.float32, 2, False),
+            (out_shared.reshape(seqs, -1, width), "seq", jnp.float32, 1, True),
+        ],
+        1,
+    )
     grad_query = summed[:, :width]
     grad_key = summed[:, width:2 * width]
     grad_value = summed[:, 2 * width:]

time: 152 us -> 140 us (0.921)
  waiting for transfers between devices: 15.9 us -> 0.02 us
  local copies, waits for them, and re-layouts: 9.71 us -> 12 us
    reduce_scatter x1 -> x0, waiting for transfers between devices: 15.9 us -> none  [local(): lax.psum_scatter(out_shared, 'seq', scatter_dimension=0, tiled=True)]
    unnamed x23 -> x26, local copies, waits for them, and re-layouts: 6.2 us -> 8.48 us
  transfers between devices with their start and end apart: 2 -> 1, of which waited for: 1 -> 0; matrix products, arithmetic and copies ran while one was open for 1% -> 0% of each run, Pallas kernels for 43% -> 37%
where the time goes in v9:
time: 140 us; the launch traced here: 139 us
  Pallas kernels  82.6 us (59%)
  matrix products  29.7 us (21%)
  between operations  14.3 us (10%)
  local copies, waits for them, and re-layouts  12 us (9%)
    pallas_call x2, Pallas kernels, ring_scatter(): pl.pallas_call(functools.partial(ring_scatter_kernel, jobs), out_shape=tu...  65.9 us
    pallas_call x1, Pallas kernels, exchange_states(): pl.pallas_call(functools.partial(exchange_kernel, n, axis), out_shape=(ja...  16.8 us
    unnamed x26, local copies, waits for them, and re-layouts  8.48 us
    dot_general x1, matrix products, local(): jnp.einsum('tk,bdk->btd', d_values, by_block(w_value), preferred_element_...  6.3 us
    dot_general x1, matrix products, local(): jnp.einsum('td,tk->dk', in_rows, grads, preferred_element_type=jnp.float32)  4.46 us
    dot_general x3, matrix products, project(): jnp.dot(in_rows, weight, preferred_element_type=jnp.float32)  3.51 us
    dot_general x1, matrix products, local(): jnp.einsum('tk,bdk->btd', d_query, by_block(w_query), preferred_element_t...  2.83 us
  transfers between devices with their start and end apart: 1, of which 0 were waited for; matrix products, arithmetic and copies ran while one was open for 0% of the time, Pallas kernels for 37%

profile of v9, /device:TPU:8, one launch (start us, length us, event | category | flops | bytes accessed | tf_op | source)
XLA Modules:
  0.0 138.9 jit_solution(15415806678258595741)
XLA Ops:
  7.3 1.4 %copy-done = bf16[1,512,2048]{2,1,0:T(8,128)(2,1)S(1)} copy-done((bf16[1,512,2048]{2,1,0:T(8,128)(2,1)S(1)}, bf16[1,512,2048]{2,1,0:T(8,128)(2,1)}, u32[]{:S(2)}) %copy-start) | copy-done | bytes 2097176
  8.8 2.0 %fusion.28 = bf16[512,256]{0,1:T(8,128)(2,1)S(1)} fusion(bf16[2048,256]{1,0:T(8,128)(2,1)} %param.7, bf16[1,512,2048]{2,1,0:T(8,128)(2,1)S(1)} %copy-done), kind=kOutput, calls=%fused_computation.29 | convolution fusion | flops 537001984 | bytes 3407872 | tf_op jit(solution)/shard_map/dot_general | solution.py:229
  10.8 0.8 fusion.22
  12.0 0.8 fusion.25
  12.8 0.8 copy-done.3
  13.8 0.7 fusion.18
  14.6 0.9 fusion.47.qg_ref
  15.5 0.9 fusion.46.kv_ref
  16.4 16.8 %shard_map.101 = (f32[2,128,128]{2,1,0:T(8,128)}, f32[2,128,128]{2,1,0:T(8,128)}) custom-call(f32[2,128,128]{2,1,0:T(8,128)} %fusion.46.kv_ref, f32[2,128,128]{2,1,0:T(8,128)} %fusion.47.qg_ref), custom_call_target="tpu_custom_call" | custom-call | tf_op jit(solution)/shard_map/pallas_call | solution.py:206
  33.2 1.2 fusion.40
  34.4 1.1 fusion.42
  35.5 1.2 fusion.36
  39.6 0.8 copy-done.4
  40.4 1.0 fusion
  41.5 1.4 %copy.47 = f32[4,8,64,256]{3,2,1,0:T(8,128)} copy(f32[4,8,64,256]{3,2,0,1:T(8,128)S(1)} %multiply_bitcast_fusion.1) | data formatting | bytes 4194304 | tf_op jit(solution)/shard_map/mul | solution.py:296
  43.1 2.8 %fusion.49 = f32[512,8,256]{2,0,1:T(8,128)} fusion(bf16[512,256,1]{0,1,2:T(8,128)(2,1)S(1)} %bitcast.120, bf16[8,256,256]{2,1,0:T(8,128)(2,1)S(1)} %bitcast.125), kind=kOutput, calls=%fused_computation.50 | convolution fusion | flops 536870912 | bytes 5505024 | tf_op jit(solution)/shard_map/tk,bdk->btd/dot_general | solution.py:284
  45.9 2.8 %fusion.48 = f32[512,8,256]{2,0,1:T(8,128)} fusion(bf16[512,256,1]{0,1,2:T(8,128)(2,1)S(1)} %bitcast.122, bf16[8,256,256]{2,1,0:T(8,128)(2,1)S(1)} %bitcast.126), kind=kOutput, calls=%fused_computation.49 | convolution fusion | flops 536870912 | bytes 5505024 | tf_op jit(solution)/shard_map/tk,bdk->btd/dot_general | solution.py:283
  48.7 4.5 %multiply_bitcast_fusion = f32[2048,768]{0,1:T(8,128)} fusion(bf16[1,512,2048]{2,1,0:T(8,128)(2,1)S(1)} %copy-done, bf16[512,256]{0,1:T(8,128)(2,1)S(1)} %bitcast.106, bf16[512,256]{0,1:T(8,128)(2,1)S(1)} %bitcast.121, bf16[512,256]{0,1:T(8,128)(2,1)S(1)} %bitcast.123), kind=kOutput, calls=%fused_computation | convolution fusion | flops 1614544896 | bytes 9175040 | tf_op jit(solution)/shard_map/td,tk->dk/dot_general | solution.py:294
  53.2 6.3 %add_bitcast_fusion.refs_0_ = f32[8,512,256]{2,1,0:T(8,128)} fusion(f32[512,8,256]{2,0,1:T(8,128)} %fusion.48, f32[512,8,256]{2,0,1:T(8,128)} %fusion.49, bf16[512,256,1]{0,1,2:T(8,128)(2,1)S(1)} %bitcast.107, bf16[8,256,256]{2,1,0:T(8,128)(2,1)S(1)} %bitcast.127), kind=kOutput, calls=%fused_computation.1 | convolution fusion | flops 538968064 | bytes 13893632 | tf_op jit(solution)/shard_map/tk,bdk->btd/dot_general | solution.py:287
  59.5 1.6 %copy-done.1 = f32[4,8,64,256]{3,2,1,0:T(8,128)S(1)} copy-done((f32[4,8,64,256]{3,2,1,0:T(8,128)S(1)}, f32[4,8,64,256]{3,2,1,0:T(8,128)}, u32[]{:S(2)}) %copy-start.1) | copy-done | bytes 2097176
  61.1 51.2 %shard_map.102 = (bf16[512,256]{1,0:T(8,128)(2,1)S(1)}, f32[512,256]{1,0:T(8,128)S(1)}) custom-call(f32[8,512,256]{2,1,0:T(8,128)} %add_bitcast_fusion.refs_0_, f32[4,512,256]{2,1,0:T(8,128)S(1)} %bitcast.96), custom_call_target="tpu_custom_call" | custom-call | flops 3145728 | bytes 12582912 | tf_op jit(solution)/shard_map/pallas_call | solution.py:135
  113.0 1.4 %copy.48 = f32[256,768]{1,0:T(8,128)S(1)} copy(f32[256,768]{0,1:T(8,128)} %reduce-scatter.2.cloned.1.call-done) | data formatting | bytes 1572864 | tf_op jit(solution)/shard_map/optimization_barrier | solution.py:306
  114.4 14.7 %shard_map.103 = (f32[64,768]{1,0:T(8,128)S(1)}, f32[64,256]{1,0:T(8,128)S(1)}) custom-call(f32[4,64,768]{2,1,0:T(8,128)S(1)} %bitcast.97, f32[8,64,256]{2,1,0:T(8,128)S(1)} %bitcast.98), custom_call_target="tpu_custom_call" | custom-call | flops 655360 | bytes 2621440 | tf_op jit(solution)/shard_map/pallas_call | solution.py:135
  129.7 1.7 %copy.70 = bf16[1,512,256]{2,1,0:T(8,128)(2,1)} copy(bf16[1,512,256]{2,1,0:T(8,128)(2,1)} %bitcast.99) | data formatting | bytes 524288
  (35 shorter events, 6.0 us)
Async XLA Ops:
  7.2 1.6 %copy-start = (bf16[1,512,2048]{2,1,0:T(8,128)(2,1)S(1)}, bf16[1,512,2048]{2,1,0:T(8,128)(2,1)}, u32[]{:S(2)}) copy-start(bf16[1,512,2048]{2,1,0:T(8,128)(2,1)} %param.6) | copy-start | bytes 6291460
  7.2 105.8 %reduce-scatter.2.cloned.1.call-start = ((), (), s32[]{:S(2)}) async-start(), calls=%async_computation.1 | async-start | bytes 7077888 | tf_op jit(solution)/shard_map/reduce_scatter | solution.py:301
  7.3 3.4 %copy-start.5 = (bf16[2048,256]{1,0:T(8,128)(2,1)S(1)}, bf16[2048,256]{1,0:T(8,128)(2,1)}, u32[]{:S(2)}) copy-start(bf16[2048,256]{1,0:T(8,128)(2,1)} %param.8) | copy-start | bytes 3145732
  10.8 1.2 copy-start.8
  12.0 1.6 %copy-start.3 = (bf16[1,512,2048]{2,1,0:T(8,128)(2,1)S(1)}, bf16[1,512,2048]{2,1,0:T(8,128)(2,1)}, u32[]{:S(2)}) copy-start(bf16[1,512,2048]{2,1,0:T(8,128)(2,1)} %param.11) | copy-start | bytes 6291460
  12.0 1.9 %copy-start.11 = (bf16[256,2048]{1,0:T(8,128)(2,1)S(1)}, bf16[256,2048]{1,0:T(8,128)(2,1)}, u32[]{:S(2)}) copy-start(bf16[256,2048]{1,0:T(8,128)(2,1)} %param.10) | copy-start | bytes 3145732
  33.1 3.5 %copy-start.10 = (f32[2,128,128]{2,1,0:T(8,128)S(1)}, f32[2,128,128]{2,1,0:T(8,128)}, u32[]{:S(2)}) copy-start(f32[2,128,128]{2,1,0:T(8,128)} %get-tuple-element.18) | copy-start | bytes 393220
  38.8 1.6 %copy-start.4 = (bf16[1,512,2048]{2,1,0:T(8,128)(2,1)S(1)}, bf16[1,512,2048]{2,1,0:T(8,128)(2,1)}, u32[]{:S(2)}) copy-start(bf16[1,512,2048]{2,1,0:T(8,128)(2,1)} %param.11) | copy-start | bytes 6291460
  41.5 1.6 %copy-start.6 = (bf16[2048,256]{1,0:T(8,128)(2,1)S(1)}, bf16[2048,256]{1,0:T(8,128)(2,1)}, u32[]{:S(2)}) copy-start(bf16[2048,256]{1,0:T(8,128)(2,1)} %param.8) | copy-start | bytes 3145732
  43.1 2.8 %copy-start.7 = (bf16[2048,256]{1,0:T(8,128)(2,1)S(1)}, bf16[2048,256]{1,0:T(8,128)(2,1)}, u32[]{:S(2)}) copy-start(bf16[2048,256]{1,0:T(8,128)(2,1)} %param.7) | copy-start | bytes 3145732
  48.7 4.5 %copy-start.9 = (bf16[2048,256]{1,0:T(8,128)(2,1)S(1)}, bf16[2048,256]{1,0:T(8,128)(2,1)}, u32[]{:S(2)}) copy-start(bf16[2048,256]{1,0:T(8,128)(2,1)} %param.9) | copy-start | bytes 3145732
  59.5 1.6 %copy-start.1 = (f32[4,8,64,256]{3,2,1,0:T(8,128)S(1)}, f32[4,8,64,256]{3,2,1,0:T(8,128)}, u32[]{:S(2)}) copy-start(f32[4,8,64,256]{3,2,1,0:T(8,128)} %copy.47) | copy-start | bytes 6291460
  112.3 0.7 copy-start.2
Sparse Core Ops, SparseCore 0:
  59.6 48.7 reduce-scatter.1

commit v10 on v9

--- a/solution.py
+++ b/solution.py
@@ -276,21 +276,15 @@
     d_keys = d_keys.astype(jnp.bfloat16).reshape(num_rows, width)
     d_values = d_values.astype(jnp.bfloat16).reshape(num_rows, width)
     groups = lax.axis_size("head")
-
-    def by_block(weight):
-        return weight.reshape(groups, weight.shape[0] // groups, width)
-
-    head_terms = jnp.einsum("tk,bdk->btd", d_query, by_block(w_query), preferred_element_type=jnp.float32)
-    head_terms = head_terms + jnp.einsum(
-        "tk,bdk->btd", d_keys, by_block(w_key), preferred_element_type=jnp.float32
-    )
-    head_terms = head_terms + jnp.einsum(
-        "tk,bdk->btd", d_values, by_block(w_value), preferred_element_type=jnp.float32
+    grads = jnp.concatenate([d_query, d_keys, d_values], axis=1)
+    w_all = jnp.concatenate([w_query, w_key, w_value], axis=1)
+    head_terms = jnp.einsum(
+        "tk,bdk->btd", grads, w_all.reshape(groups, w_all.shape[0] // groups, 3 * width),
+        preferred_element_type=jnp.float32,
     )
     total_rows = lax.axis_size("seq") * lax.axis_size("dp") * num_rows
     grad_scale = jnp.float32(1.0) / jnp.sqrt(jnp.float32(total_rows))
     seqs, shares = lax.axis_size("seq"), lax.axis_size("dp")
-    grads = jnp.concatenate([d_query, d_keys, d_values], axis=1)
     term_qkv = jnp.einsum("td,tk->dk", in_rows, grads, preferred_element_type=jnp.float32) * grad_scale
     grad_blocks = grad_rows.reshape(num_rows, seqs, shares, -1)
     term_out = jnp.einsum(
@@ -300,9 +294,9 @@
     term_qkv, head_terms, term_out = lax.optimization_barrier((term_qkv, head_terms, term_out))
     summed = lax.psum_scatter(term_qkv, "seq", scatter_dimension=0, tiled=True)
     input_grad, out_shared = ring_scatter(
-        [(head_terms, "head", jnp.bfloat16, 4, False), (term_out, "dp", jnp.float32, 2, False)], 0
-    )
-    input_grad = input_grad[None]
+        [(head_terms, "head", jnp.float32, 4, False), (term_out, "dp", jnp.float32, 2, False)], 0
+    )
+    input_grad = input_grad.astype(jnp.bfloat16)[None]
     summed, input_grad, out_shared = lax.optimization_barrier((summed, input_grad, out_shared))
     summed, out_summed = ring_scatter(
         [

time: 140 us -> 147 us (1.050)
  other arithmetic: 0.24 us -> 2.95 us
  matrix products: 29.7 us -> 31.9 us
  local copies, waits for them, and re-layouts: 12 us -> 13.8 us
    dot_general x3 -> x1, matrix products: 11.9 us -> 5.79 us  [local(): jnp.einsum('tk,bdk->btd', grads, w_all.reshape(groups, w_all.shape[0] //...]
    reshape x0 -> x3, local copies, waits for them, and re-layouts: none -> 4.64 us  [the longest x1 1.78 us: local(): d_query = d_query.astype(jnp.bfloat16).reshape(num_rows, width)]
    unnamed x26 -> x43, local copies, waits for them, and re-layouts: 8.48 us -> 5.63 us
    concatenate x0 -> x1, other arithmetic: none -> 1.91 us  [local(): w_all = jnp.concatenate([w_query, w_key, w_value], axis=1)]
    dot_general x1, matrix products: 0.47 us -> 2.3 us  [local(): jnp.einsum('hts,she->the', scores_qk, value_rows, preferred_element_type=...]
    unnamed x1, matrix products: 0.96 us -> 2.55 us
  transfers between devices with their start and end apart: 1 -> 1, of which waited for: 0 -> 0; matrix products, arithmetic and copies ran while one was open for 0% -> 1% of each run, Pallas kernels for 37% -> 35%
where the time goes in v10:
time: 147 us; the launch traced here: 146 us
  Pallas kernels  82.7 us (56%)
  matrix products  31.9 us (22%)
  between operations  14.4 us (10%)
  local copies, waits for them, and re-layouts  13.8 us (9%)
  other arithmetic  2.95 us (2%)
    pallas_call x2, Pallas kernels, ring_scatter(): pl.pallas_call(functools.partial(ring_scatter_kernel, jobs), out_shape=tu...  65.9 us
    pallas_call x1, Pallas kernels, exchange_states(): pl.pallas_call(functools.partial(exchange_kernel, n, axis), out_shape=(ja...  16.8 us
    dot_general x1, matrix products, local(): jnp.einsum('tk,bdk->btd', grads, w_all.reshape(groups, w_all.shape[0] //...  5.79 us
    unnamed x43, local copies, waits for them, and re-layouts  5.63 us
    dot_general x1, matrix products, local(): jnp.einsum('td,tk->dk', in_rows, grads, preferred_element_type=jnp.float32)  4.48 us
    dot_general x3, matrix products, project(): jnp.dot(in_rows, weight, preferred_element_type=jnp.float32)  3.51 us
  transfers between devices with their start and end apart: 1, of which 0 were waited for; matrix products, arithmetic and copies ran while one was open for 1% of the time, Pallas kernels for 35%

profile of v10, /device:TPU:8, one launch (start us, length us, event | category | flops | bytes accessed | tf_op | source)
XLA Modules:
  0.0 145.8 jit_solution(15578014934628326737)
XLA Ops:
  7.4 1.5 %copy-done = bf16[1,512,2048]{2,1,0:T(8,128)(2,1)S(1)} copy-done((bf16[1,512,2048]{2,1,0:T(8,128)(2,1)S(1)}, bf16[1,512,2048]{2,1,0:T(8,128)(2,1)}, u32[]{:S(2)}) %copy-start) | copy-done | bytes 2097176
  8.9 2.0 %fusion.28 = bf16[512,256]{0,1:T(8,128)(2,1)S(1)} fusion(bf16[2048,256]{1,0:T(8,128)(2,1)} %param.7, bf16[1,512,2048]{2,1,0:T(8,128)(2,1)S(1)} %copy-done), kind=kOutput, calls=%fused_computation.30 | convolution fusion | flops 537001984 | bytes 3407872 | tf_op jit(solution)/shard_map/dot_general | solution.py:229
  13.0 0.9 copy-done.8
  16.7 16.8 %shard_map.101 = (f32[2,128,128]{2,1,0:T(8,128)}, f32[2,128,128]{2,1,0:T(8,128)}) custom-call(f32[2,128,128]{2,1,0:T(8,128)} %fusion.43.kv_ref, f32[2,128,128]{2,1,0:T(8,128)} %fusion.44.qg_ref), custom_call_target="tpu_custom_call" | custom-call | tf_op jit(solution)/shard_map/pallas_call | solution.py:206
  33.5 2.0 %fusion.36 = f32[2,128,512]{2,1,0:T(8,128)} fusion(bf16[512,2,128]{0,2,1:T(8,128)(2,1)S(1)} %bitcast.106, f32[2,128,128]{2,1,0:T(8,128)} %get-tuple-element.17), kind=kOutput, calls=%fused_computation.39 | convolution fusion | flops 33587200 | bytes 917504 | tf_op jit(solution)/shard_map/thd,hde->the/dot_general | solution.py:257
  35.5 1.1 fusion.38
  36.6 2.0 %fusion.32 = f32[2,128,512]{2,1,0:T(8,128)} fusion(bf16[512,2,128]{0,2,1:T(8,128)(2,1)S(1)} %bitcast.102, f32[2,128,128]{2,1,0:T(8,128)} %get-tuple-element.18), kind=kOutput, calls=%fused_computation.35 | convolution fusion | flops 33587200 | bytes 917504 | tf_op jit(solution)/shard_map/shd,hde->she/dot_general | solution.py:272
  39.6 1.7 %select_convert_fusion = bf16[2,512,512]{2,1,0:T(8,128)(2,1)S(1)} fusion(bf16[512,2,128]{0,2,1:T(8,128)(2,1)S(1)} %bitcast.107, bf16[512,2,128]{0,2,1:T(8,128)(2,1)S(1)} %bitcast.103, pred[512,512]{1,0:T(8,128)(4,1)} %copy-done.17), kind=kOutput, calls=%fused_computation.15 | convolution fusion | flops 135266304 | bytes 1835008 | tf_op jit(solution)/shard_map/thd,shd->hts/dot_general | solution.py:250
  41.3 1.9 %pad_maximum_fusion = bf16[2048,768]{1,0:T(8,128)(2,1)} fusion(bf16[2048,256]{1,0:T(8,128)(2,1)S(1)} %copy-done.12, bf16[2048,256]{1,0:T(8,128)(2,1)S(1)} %copy-done.14, bf16[2048,256]{1,0:T(8,128)(2,1)S(1)} %copy-done.15), kind=kLoop, calls=%fused_computation.1 | loop fusion | flops 9437184 | bytes 6291456 | tf_op jit(solution)/shard_map/concatenate | solution.py:280
  43.2 1.0 fusion.16
  44.3 1.2 fusion.15
  45.4 1.8 %copy.41 = bf16[512,256]{1,0:T(8,128)(2,1)} copy(bf16[512,256]{0,1:T(8,128)(2,1)} %bitcast.111) | data formatting | bytes 524288 | tf_op jit(solution)/shard_map/reshape | solution.py:275
  47.2 1.8 %copy.42 = bf16[512,256]{1,0:T(8,128)(2,1)} copy(bf16[512,256]{0,1:T(8,128)(2,1)} %bitcast.110) | data formatting | bytes 524288 | tf_op jit(solution)/shard_map/reshape | solution.py:276
  49.0 2.3 %fusion.21 = bf16[2,128,512]{2,1,0:T(8,128)(2,1)} fusion(f32[2,128,512]{2,1,0:T(8,128)} %fusion.36, bf16[512,2,128]{0,2,1:T(8,128)(2,1)S(1)} %bitcast.96, bf16[2,512,512]{2,1,0:T(8,128)(2,1)S(1)} %select_convert_fusion, f32[512]{0:T(512)S(1)} %multiply_rsqrt_fusion), kind=kOutput, calls=%fused_computation.27 | convolution fusion | flops 134610944 | bytes 2099200 | tf_op jit(solution)/shard_map/hts,she->the/dot_general | solution.py:254
  51.3 1.0 fusion.17
  52.3 1.1 copy.43
  53.4 2.5 %fusion = f32[256,2048]{0,1:S(1)} fusion(bf16[512,256]{0,1:T(8,128)(2,1)S(1)} %bitcast.109, bf16[1,512,2048]{2,1,0:T(8,128)(2,1)} %param.11), kind=kOutput, calls=%fused_computation.3 | convolution fusion | flops 536870912 | bytes 4456448
  56.2 1.5 %copy.49 = f32[4,8,64,256]{3,2,1,0:T(8,128)} copy(f32[4,8,64,256]{3,2,0,1:T(8,128)S(1)} %multiply_bitcast_fusion.1) | data formatting | bytes 4194304 | tf_op jit(solution)/shard_map/mul | solution.py:290
  57.7 4.5 %multiply_bitcast_fusion = f32[2048,768]{0,1:T(8,128)} fusion(bf16[1,512,2048]{2,1,0:T(8,128)(2,1)S(1)} %copy-done, bf16[512,256]{1,0:T(8,128)(2,1)S(1)} %copy.43, bf16[512,256]{1,0:T(8,128)(2,1)S(1)} %copy-done.19, bf16[512,256]{1,0:T(8,128)(2,1)S(1)} %copy-done.18), kind=kOutput, calls=%fused_computation | convolution fusion | flops 1614544896 | bytes 9175040 | tf_op jit(solution)/shard_map/td,tk->dk/dot_general | solution.py:288
  62.2 5.8 %convolution_bitcast_fusion.refs_0_ = f32[8,512,256]{2,1,0:T(8,128)} fusion(bf16[8,256,768]{2,1,0:T(8,128)(2,1)} %bitcast.92, bf16[512,256]{1,0:T(8,128)(2,1)S(1)} %copy.43, bf16[512,256]{1,0:T(8,128)(2,1)S(1)} %copy-done.19, bf16[512,256]{1,0:T(8,128)(2,1)S(1)} %copy-done.18), kind=kOutput, calls=%fused_computation.2 | convolution fusion | flops 1612972032 | bytes 8126464 | tf_op jit(solution)/shard_map/tk,bdk->btd/dot_general | solution.py:281
  68.0 1.6 %copy-done.1 = f32[4,8,64,256]{3,2,1,0:T(8,128)S(1)} copy-done((f32[4,8,64,256]{3,2,1,0:T(8,128)S(1)}, f32[4,8,64,256]{3,2,1,0:T(8,128)}, u32[]{:S(2)}) %copy-start.1) | copy-done | bytes 2097176
  69.6 51.1 %shard_map.102 = (f32[512,256]{1,0:T(8,128)S(1)}, f32[512,256]{1,0:T(8,128)S(1)}) custom-call(f32[8,512,256]{2,1,0:T(8,128)} %convolution_bitcast_fusion.refs_0_, f32[4,512,256]{2,1,0:T(8,128)S(1)} %bitcast.87), custom_call_target="tpu_custom_call" | custom-call | flops 3145728 | bytes 12582912 | tf_op jit(solution)/shard_map/pallas_call | solution.py:135
  121.5 1.4 copy.50
  122.9 14.7 %shard_map.103 = (f32[64,768]{1,0:T(8,128)S(1)}, f32[64,256]{1,0:T(8,128)S(1)}) custom-call(f32[4,64,768]{2,1,0:T(8,128)S(1)} %bitcast.88, f32[8,64,256]{2,1,0:T(8,128)S(1)} %bitcast.89), custom_call_target="tpu_custom_call" | custom-call | flops 655360 | bytes 2621440 | tf_op jit(solution)/shard_map/pallas_call | solution.py:135
  (55 shorter events, 8.2 us)
Async XLA Ops:
  7.2 1.7 %copy-start = (bf16[1,512,2048]{2,1,0:T(8,128)(2,1)S(1)}, bf16[1,512,2048]{2,1,0:T(8,128)(2,1)}, u32[]{:S(2)}) copy-start(bf16[1,512,2048]{2,1,0:T(8,128)(2,1)} %param.6) | copy-start | bytes 6291460
  7.2 114.3 %reduce-scatter.2.cloned.1.call-start = ((), (), s32[]{:S(2)}) async-start(), calls=%async_computation.1 | async-start | bytes 7077888 | tf_op jit(solution)/shard_map/reduce_scatter | solution.py:295
  7.3 31.5 %copy-start.17 = (pred[512,512]{1,0:T(8,128)(4,1)}, pred[512,512]{1,0:T(8,128)(4,1)S(1)}, u32[]{:S(2)}) copy-start(pred[512,512]{1,0:T(8,128)(4,1)S(1)} %iota_compare_fusion) | copy-start | bytes 786436
  7.3 3.5 %copy-start.13 = (bf16[2048,256]{1,0:T(8,128)(2,1)S(1)}, bf16[2048,256]{1,0:T(8,128)(2,1)}, u32[]{:S(2)}) copy-start(bf16[2048,256]{1,0:T(8,128)(2,1)} %param.8) | copy-start | bytes 3145732
  10.8 22.6 %copy-start.6 = (bf16[512,256]{0,1:T(8,128)(2,1)}, bf16[512,256]{0,1:T(8,128)(2,1)S(1)}, u32[]{:S(2)}) copy-start(bf16[512,256]{0,1:T(8,128)(2,1)S(1)} %fusion.28) | copy-start | bytes 786436
  10.9 1.3 copy-start.11
  12.2 24.4 %copy-start.4 = (bf16[512,256]{0,1:T(8,128)(2,1)}, bf16[512,256]{0,1:T(8,128)(2,1)S(1)}, u32[]{:S(2)}) copy-start(bf16[512,256]{0,1:T(8,128)(2,1)S(1)} %fusion.22) | copy-start | bytes 786436
  12.2 1.7 %copy-start.8 = (bf16[1,512,2048]{2,1,0:T(8,128)(2,1)S(1)}, bf16[1,512,2048]{2,1,0:T(8,128)(2,1)}, u32[]{:S(2)}) copy-start(bf16[1,512,2048]{2,1,0:T(8,128)(2,1)} %param.11) | copy-start | bytes 6291460
  12.2 1.9 %copy-start.20 = (bf16[256,2048]{1,0:T(8,128)(2,1)S(1)}, bf16[256,2048]{1,0:T(8,128)(2,1)}, u32[]{:S(2)}) copy-start(bf16[256,2048]{1,0:T(8,128)(2,1)} %param.10) | copy-start | bytes 3145732
  14.9 24.0 %copy-start.2 = (bf16[512,256]{0,1:T(8,128)(2,1)}, bf16[512,256]{0,1:T(8,128)(2,1)S(1)}, u32[]{:S(2)}) copy-start(bf16[512,256]{0,1:T(8,128)(2,1)S(1)} %fusion.18) | copy-start | bytes 786436
  33.5 5.2 %copy-start.16 = (f32[2,128,128]{2,1,0:T(8,128)S(1)}, f32[2,128,128]{2,1,0:T(8,128)}, u32[]{:S(2)}) copy-start(f32[2,128,128]{2,1,0:T(8,128)} %get-tuple-element.18) | copy-start | bytes 393220
  36.6 2.8 %copy-start.7 = (bf16[512,256]{0,1:T(8,128)(2,1)S(1)}, bf16[512,256]{0,1:T(8,128)(2,1)}, u32[]{:S(2)}) copy-start(bf16[512,256]{0,1:T(8,128)(2,1)} %copy-done.6) | copy-start | bytes 786436
  38.6 1.0 copy-start.5
  38.9 2.4 %copy-start.12 = (bf16[2048,256]{1,0:T(8,128)(2,1)S(1)}, bf16[2048,256]{1,0:T(8,128)(2,1)}, u32[]{:S(2)}) copy-start(bf16[2048,256]{1,0:T(8,128)(2,1)} %param.9) | copy-start | bytes 3145732
  38.9 2.4 %copy-start.14 = (bf16[2048,256]{1,0:T(8,128)(2,1)S(1)}, bf16[2048,256]{1,0:T(8,128)(2,1)}, u32[]{:S(2)}) copy-start(bf16[2048,256]{1,0:T(8,128)(2,1)} %param.8) | copy-start | bytes 3145732
  38.9 2.4 %copy-start.15 = (bf16[2048,256]{1,0:T(8,128)(2,1)S(1)}, bf16[2048,256]{1,0:T(8,128)(2,1)}, u32[]{:S(2)}) copy-start(bf16[2048,256]{1,0:T(8,128)(2,1)} %param.7) | copy-start | bytes 3145732
  49.0 2.3 %copy-start.3 = (bf16[512,256]{0,1:T(8,128)(2,1)S(1)}, bf16[512,256]{0,1:T(8,128)(2,1)}, u32[]{:S(2)}) copy-start(bf16[512,256]{0,1:T(8,128)(2,1)} %copy-done.2) | copy-start | bytes 786436
  49.0 2.3 %copy-start.9 = (f32[2,128,512]{2,1,0:T(8,128)S(1)}, f32[2,128,512]{2,1,0:T(8,128)}, u32[]{:S(2)}) copy-start(f32[2,128,512]{2,1,0:T(8,128)} %fusion.32) | copy-start | bytes 1572868
  51.3 2.1 %copy-start.10 = (bf16[2,128,512]{2,1,0:T(8,128)(2,1)S(1)}, bf16[2,128,512]{2,1,0:T(8,128)(2,1)}, u32[]{:S(2)}) copy-start(bf16[2,128,512]{2,1,0:T(8,128)(2,1)} %fusion.21) | copy-start | bytes 786436
  56.2 1.5 %copy-start.18 = (bf16[512,256]{1,0:T(8,128)(2,1)S(1)}, bf16[512,256]{1,0:T(8,128)(2,1)}, u32[]{:S(2)}) copy-start(bf16[512,256]{1,0:T(8,128)(2,1)} %copy.41) | copy-start | bytes 786436
  56.2 1.5 %copy-start.19 = (bf16[512,256]{1,0:T(8,128)(2,1)S(1)}, bf16[512,256]{1,0:T(8,128)(2,1)}, u32[]{:S(2)}) copy-start(bf16[512,256]{1,0:T(8,128)(2,1)} %copy.42) | copy-start | bytes 786436
  68.0 1.6 %copy-start.1 = (f32[4,8,64,256]{3,2,1,0:T(8,128)S(1)}, f32[4,8,64,256]{3,2,1,0:T(8,128)}, u32[]{:S(2)}) copy-start(f32[4,8,64,256]{3,2,1,0:T(8,128)} %copy.49) | copy-start | bytes 6291460
Sparse Core Ops, SparseCore 0:
  68.1 48.7 reduce-scatter.1

commit v11 on v9

--- a/solution.py
+++ b/solution.py
@@ -147,61 +147,83 @@
     )(*(part[0] for part in parts))
 
 
-def exchange_kernel(n, axis, kv_ref, qg_ref, prefix_ref, suffix_ref, kv_in, qg_in, send_sem, recv_sem):
+def exchange_kernel(n, axis, kv_ref, qg_ref, prefix_ref, suffix_ref,
+                    pair_in, chip_sum, kv_in, qg_in, pair_sem, send_sem, recv_sem):
     me = lax.axis_index(axis)
+    chips = n // 2
+    chip, core = me // 2, lax.rem(me, 2)
+    partner = me + 1 - 2 * core
     barrier = pltpu.get_barrier_semaphore()
-    for offset in range(1, n):
-        pl.semaphore_signal(
-            barrier, inc=1, device_id={axis: lax.rem(me + offset, n)}, device_id_type=MESH
+    pl.semaphore_signal(barrier, inc=1, device_id={axis: partner}, device_id_type=MESH)
+    for offset in range(1, chips):
+        peer = lax.rem(chip + offset, chips) * 2 + core
+        pl.semaphore_signal(barrier, inc=1, device_id={axis: peer}, device_id_type=MESH)
+    pl.semaphore_wait(barrier, chips)
+
+    swaps = []
+    for kind, ref in enumerate((kv_ref, qg_ref)):
+        swap = pltpu.make_async_remote_copy(
+            src_ref=ref, dst_ref=pair_in.at[kind], send_sem=pair_sem.at[0, kind],
+            recv_sem=pair_sem.at[1, kind], device_id={axis: partner}, device_id_type=MESH,
         )
-    pl.semaphore_wait(barrier, n - 1)
+        swap.start()
+        swaps.append(swap)
+    for swap in swaps:
+        swap.wait_recv()
+    chip_sum[0] = kv_ref[...] + pair_in[0]
+    chip_sum[1] = qg_ref[...] + pair_in[1]
 
     def route(offset, later):
-        peer = lax.rem(me + offset, n)
+        peer = lax.rem(chip + offset, chips) * 2 + core
         kind = 0 if later else 1
         return pltpu.make_async_remote_copy(
-            src_ref=kv_ref if later else qg_ref,
-            dst_ref=(kv_in if later else qg_in).at[me],
+            src_ref=chip_sum.at[kind],
+            dst_ref=(kv_in if later else qg_in).at[chip],
             send_sem=send_sem.at[kind, offset],
-            recv_sem=recv_sem.at[kind, me],
+            recv_sem=recv_sem.at[kind, chip],
             device_id={axis: peer},
             device_id_type=MESH,
         )
 
-    for offset in range(1, n):
+    for offset in range(1, chips):
         for later in (True, False):
-            @pl.when((me + offset < n) == later)
+            @pl.when((chip + offset < chips) == later)
             def _():
                 route(offset, later).start()
 
-    prefix_ref[...] = jnp.zeros_like(prefix_ref)
-    suffix_ref[...] = jnp.zeros_like(suffix_ref)
-    for peer in range(n):
-        @pl.when(peer < me)
+    prefix_ref[...] = jnp.where(core == 1, pair_in[0], 0.0)
+    suffix_ref[...] = jnp.where(core == 0, pair_in[1], 0.0)
+    for sender in range(chips):
+        @pl.when(sender < chip)
         def _():
             pltpu.make_async_remote_copy(
-                src_ref=kv_ref, dst_ref=kv_in.at[peer], send_sem=send_sem.at[0, 0],
-                recv_sem=recv_sem.at[0, peer], device_id={axis: peer}, device_id_type=MESH,
+                src_ref=chip_sum.at[0], dst_ref=kv_in.at[sender], send_sem=send_sem.at[0, 0],
+                recv_sem=recv_sem.at[0, sender], device_id={axis: sender * 2 + core},
+                device_id_type=MESH,
             ).wait_recv()
-            prefix_ref[...] += kv_in[peer]
-
-        @pl.when(peer > me)
+            prefix_ref[...] += kv_in[sender]
+
+        @pl.when(sender > chip)
         def _():
             pltpu.make_async_remote_copy(
-                src_ref=qg_ref, dst_ref=qg_in.at[peer], send_sem=send_sem.at[1, 0],
-                recv_sem=recv_sem.at[1, peer], device_id={axis: peer}, device_id_type=MESH,
+                src_ref=chip_sum.at[1], dst_ref=qg_in.at[sender], send_sem=send_sem.at[1, 0],
+                recv_sem=recv_sem.at[1, sender], device_id={axis: sender * 2 + core},
+                device_id_type=MESH,
             ).wait_recv()
-            suffix_ref[...] += qg_in[peer]
-
-    for offset in range(1, n):
+            suffix_ref[...] += qg_in[sender]
+
+    for swap in swaps:
+        swap.wait_send()
+    for offset in range(1, chips):
         for later in (True, False):
-            @pl.when((me + offset < n) == later)
+            @pl.when((chip + offset < chips) == later)
             def _():
                 route(offset, later).wait_send()
 
 
 def exchange_states(kv_state, qg_state, axis):
     n = lax.axis_size(axis)
+    chips = n // 2
     shape = kv_state.shape
     return pl.pallas_call(
         functools.partial(exchange_kernel, n, axis),
@@ -209,10 +231,13 @@
         in_specs=[pl.BlockSpec(memory_space=pltpu.VMEM)] * 2,
         out_specs=(pl.BlockSpec(memory_space=pltpu.VMEM),) * 2,
         scratch_shapes=[
-            pltpu.VMEM((n,) + shape, jnp.float32),
-            pltpu.VMEM((n,) + shape, jnp.float32),
-            pltpu.SemaphoreType.DMA((2, n)),
-            pltpu.SemaphoreType.DMA((2, n)),
+            pltpu.VMEM((2,) + shape, jnp.float32),
+            pltpu.VMEM((2,) + shape, jnp.float32),
+            pltpu.VMEM((chips,) + shape, jnp.float32),
+            pltpu.VMEM((chips,) + shape, jnp.float32),
+            pltpu.SemaphoreType.DMA((2, 2)),
+            pltpu.SemaphoreType.DMA((2, chips)),
+            pltpu.SemaphoreType.DMA((2, chips)),
         ],
         compiler_params=pltpu.CompilerParams(collective_id=2, has_side_effects=True),
     )(kv_state, qg_state)

time: 140 us -> 137 us (0.979)
  Pallas kernels: 82.6 us -> 80.2 us
    pallas_call x1, Pallas kernels: 16.8 us -> 13.8 us  [exchange_states(): pl.pallas_call(functools.partial(exchange_kernel, n, axis), out_shape=(ja...]
where the time goes in v11:
time: 137 us; the launch traced here: 136 us
  Pallas kernels  80.2 us (59%)
  matrix products  29.7 us (22%)
  between operations  14.3 us (10%)
  local copies, waits for them, and re-layouts  12 us (9%)
    pallas_call x2, Pallas kernels, ring_scatter(): pl.pallas_call(functools.partial(ring_scatter_kernel, jobs), out_shape=tu...  66.4 us
    pallas_call x1, Pallas kernels, exchange_states(): pl.pallas_call(functools.partial(exchange_kernel, n, axis), out_shape=(ja...  13.8 us
    unnamed x26, local copies, waits for them, and re-layouts  8.47 us
    dot_general x1, matrix products, local(): jnp.einsum('tk,bdk->btd', d_values, by_block(w_value), preferred_element_...  6.29 us
    dot_general x1, matrix products, local(): jnp.einsum('td,tk->dk', in_rows, grads, preferred_element_type=jnp.float32)  4.46 us
    dot_general x3, matrix products, project(): jnp.dot(in_rows, weight, preferred_element_type=jnp.float32)  3.51 us
    dot_general x1, matrix products, local(): jnp.einsum('tk,bdk->btd', d_query, by_block(w_query), preferred_element_t...  2.83 us
    dot_general x1, matrix products, local(): jnp.einsum('tk,bdk->btd', d_keys, by_block(w_key), preferred_element_type...  2.79 us
  transfers between devices with their start and end apart: 1, of which 0 were waited for; matrix products, arithmetic and copies ran while one was open for 0% of the time, Pallas kernels for 37%

profile of v11, /device:TPU:8, one launch (start us, length us, event | category | flops | bytes accessed | tf_op | source)
XLA Modules:
  0.0 136.5 jit_solution(610274849915415824)
XLA Ops:
  7.3 1.4 %copy-done = bf16[1,512,2048]{2,1,0:T(8,128)(2,1)S(1)} copy-done((bf16[1,512,2048]{2,1,0:T(8,128)(2,1)S(1)}, bf16[1,512,2048]{2,1,0:T(8,128)(2,1)}, u32[]{:S(2)}) %copy-start) | copy-done | bytes 2097176
  8.8 2.0 %fusion.28 = bf16[512,256]{0,1:T(8,128)(2,1)S(1)} fusion(bf16[2048,256]{1,0:T(8,128)(2,1)} %param.7, bf16[1,512,2048]{2,1,0:T(8,128)(2,1)S(1)} %copy-done), kind=kOutput, calls=%fused_computation.29 | convolution fusion | flops 537001984 | bytes 3407872 | tf_op jit(solution)/shard_map/dot_general | solution.py:254
  10.8 0.8 fusion.22
  12.0 0.8 fusion.25
  12.8 0.8 copy-done.3
  13.8 0.7 fusion.18
  14.6 0.9 fusion.47.qg_ref
  15.5 0.9 fusion.46.kv_ref
  16.4 13.8 %shard_map.101 = (f32[2,128,128]{2,1,0:T(8,128)}, f32[2,128,128]{2,1,0:T(8,128)}) custom-call(f32[2,128,128]{2,1,0:T(8,128)} %fusion.46.kv_ref, f32[2,128,128]{2,1,0:T(8,128)} %fusion.47.qg_ref), custom_call_target="tpu_custom_call" | custom-call | tf_op jit(solution)/shard_map/pallas_call | solution.py:228
  30.2 1.2 fusion.40
  31.4 1.1 fusion.42
  32.5 1.2 fusion.36
  36.6 0.8 copy-done.4
  37.4 1.0 fusion
  38.5 1.4 %copy.47 = f32[4,8,64,256]{3,2,1,0:T(8,128)} copy(f32[4,8,64,256]{3,2,0,1:T(8,128)S(1)} %multiply_bitcast_fusion.1) | data formatting | bytes 4194304 | tf_op jit(solution)/shard_map/mul | solution.py:321
  40.1 2.8 %fusion.49 = f32[512,8,256]{2,0,1:T(8,128)} fusion(bf16[512,256,1]{0,1,2:T(8,128)(2,1)S(1)} %bitcast.120, bf16[8,256,256]{2,1,0:T(8,128)(2,1)S(1)} %bitcast.125), kind=kOutput, calls=%fused_computation.50 | convolution fusion | flops 536870912 | bytes 5505024 | tf_op jit(solution)/shard_map/tk,bdk->btd/dot_general | solution.py:309
  42.9 2.8 %fusion.48 = f32[512,8,256]{2,0,1:T(8,128)} fusion(bf16[512,256,1]{0,1,2:T(8,128)(2,1)S(1)} %bitcast.122, bf16[8,256,256]{2,1,0:T(8,128)(2,1)S(1)} %bitcast.126), kind=kOutput, calls=%fused_computation.49 | convolution fusion | flops 536870912 | bytes 5505024 | tf_op jit(solution)/shard_map/tk,bdk->btd/dot_general | solution.py:308
  45.7 4.5 %multiply_bitcast_fusion = f32[2048,768]{0,1:T(8,128)} fusion(bf16[1,512,2048]{2,1,0:T(8,128)(2,1)S(1)} %copy-done, bf16[512,256]{0,1:T(8,128)(2,1)S(1)} %bitcast.106, bf16[512,256]{0,1:T(8,128)(2,1)S(1)} %bitcast.121, bf16[512,256]{0,1:T(8,128)(2,1)S(1)} %bitcast.123), kind=kOutput, calls=%fused_computation | convolution fusion | flops 1614544896 | bytes 9175040 | tf_op jit(solution)/shard_map/td,tk->dk/dot_general | solution.py:319
  50.2 6.3 %add_bitcast_fusion.refs_0_ = f32[8,512,256]{2,1,0:T(8,128)} fusion(f32[512,8,256]{2,0,1:T(8,128)} %fusion.48, f32[512,8,256]{2,0,1:T(8,128)} %fusion.49, bf16[512,256,1]{0,1,2:T(8,128)(2,1)S(1)} %bitcast.107, bf16[8,256,256]{2,1,0:T(8,128)(2,1)S(1)} %bitcast.127), kind=kOutput, calls=%fused_computation.1 | convolution fusion | flops 538968064 | bytes 13893632 | tf_op jit(solution)/shard_map/tk,bdk->btd/dot_general | solution.py:312
  56.5 1.6 %copy-done.1 = f32[4,8,64,256]{3,2,1,0:T(8,128)S(1)} copy-done((f32[4,8,64,256]{3,2,1,0:T(8,128)S(1)}, f32[4,8,64,256]{3,2,1,0:T(8,128)}, u32[]{:S(2)}) %copy-start.1) | copy-done | bytes 2097176
  58.1 51.0 %shard_map.102 = (bf16[512,256]{1,0:T(8,128)(2,1)S(1)}, f32[512,256]{1,0:T(8,128)S(1)}) custom-call(f32[8,512,256]{2,1,0:T(8,128)} %add_bitcast_fusion.refs_0_, f32[4,512,256]{2,1,0:T(8,128)S(1)} %bitcast.96), custom_call_target="tpu_custom_call" | custom-call | flops 3145728 | bytes 12582912 | tf_op jit(solution)/shard_map/pallas_call | solution.py:135
  109.9 1.4 %copy.48 = f32[256,768]{1,0:T(8,128)S(1)} copy(f32[256,768]{0,1:T(8,128)} %reduce-scatter.2.cloned.1.call-done) | data formatting | bytes 1572864 | tf_op jit(solution)/shard_map/optimization_barrier | solution.py:331
  111.3 15.4 %shard_map.103 = (f32[64,768]{1,0:T(8,128)S(1)}, f32[64,256]{1,0:T(8,128)S(1)}) custom-call(f32[4,64,768]{2,1,0:T(8,128)S(1)} %bitcast.97, f32[8,64,256]{2,1,0:T(8,128)S(1)} %bitcast.98), custom_call_target="tpu_custom_call" | custom-call | flops 655360 | bytes 2621440 | tf_op jit(solution)/shard_map/pallas_call | solution.py:135
  127.3 1.7 %copy.70 = bf16[1,512,256]{2,1,0:T(8,128)(2,1)} copy(bf16[1,512,256]{2,1,0:T(8,128)(2,1)} %bitcast.99) | data formatting | bytes 524288
  (35 shorter events, 6.0 us)
Async XLA Ops:
  7.2 1.6 %copy-start = (bf16[1,512,2048]{2,1,0:T(8,128)(2,1)S(1)}, bf16[1,512,2048]{2,1,0:T(8,128)(2,1)}, u32[]{:S(2)}) copy-start(bf16[1,512,2048]{2,1,0:T(8,128)(2,1)} %param.6) | copy-start | bytes 6291460
  7.2 102.7 %reduce-scatter.2.cloned.1.call-start = ((), (), s32[]{:S(2)}) async-start(), calls=%async_computation.1 | async-start | bytes 7077888 | tf_op jit(solution)/shard_map/reduce_scatter | solution.py:326
  7.3 3.4 %copy-start.5 = (bf16[2048,256]{1,0:T(8,128)(2,1)S(1)}, bf16[2048,256]{1,0:T(8,128)(2,1)}, u32[]{:S(2)}) copy-start(bf16[2048,256]{1,0:T(8,128)(2,1)} %param.8) | copy-start | bytes 3145732
  10.8 1.2 copy-start.8
  12.0 1.6 %copy-start.3 = (bf16[1,512,2048]{2,1,0:T(8,128)(2,1)S(1)}, bf16[1,512,2048]{2,1,0:T(8,128)(2,1)}, u32[]{:S(2)}) copy-start(bf16[1,512,2048]{2,1,0:T(8,128)(2,1)} %param.11) | copy-start | bytes 6291460
  12.0 1.9 %copy-start.11 = (bf16[256,2048]{1,0:T(8,128)(2,1)S(1)}, bf16[256,2048]{1,0:T(8,128)(2,1)}, u32[]{:S(2)}) copy-start(bf16[256,2048]{1,0:T(8,128)(2,1)} %param.10) | copy-start | bytes 3145732
  30.2 3.5 %copy-start.10 = (f32[2,128,128]{2,1,0:T(8,128)S(1)}, f32[2,128,128]{2,1,0:T(8,128)}, u32[]{:S(2)}) copy-start(f32[2,128,128]{2,1,0:T(8,128)} %get-tuple-element.18) | copy-start | bytes 393220
  35.8 1.6 %copy-start.4 = (bf16[1,512,2048]{2,1,0:T(8,128)(2,1)S(1)}, bf16[1,512,2048]{2,1,0:T(8,128)(2,1)}, u32[]{:S(2)}) copy-start(bf16[1,512,2048]{2,1,0:T(8,128)(2,1)} %param.11) | copy-start | bytes 6291460
  38.5 1.6 %copy-start.6 = (bf16[2048,256]{1,0:T(8,128)(2,1)S(1)}, bf16[2048,256]{1,0:T(8,128)(2,1)}, u32[]{:S(2)}) copy-start(bf16[2048,256]{1,0:T(8,128)(2,1)} %param.8) | copy-start | bytes 3145732
  40.1 2.8 %copy-start.7 = (bf16[2048,256]{1,0:T(8,128)(2,1)S(1)}, bf16[2048,256]{1,0:T(8,128)(2,1)}, u32[]{:S(2)}) copy-start(bf16[2048,256]{1,0:T(8,128)(2,1)} %param.7) | copy-start | bytes 3145732
  45.7 4.5 %copy-start.9 = (bf16[2048,256]{1,0:T(8,128)(2,1)S(1)}, bf16[2048,256]{1,0:T(8,128)(2,1)}, u32[]{:S(2)}) copy-start(bf16[2048,256]{1,0:T(8,128)(2,1)} %param.9) | copy-start | bytes 3145732
  56.5 1.6 %copy-start.1 = (f32[4,8,64,256]{3,2,1,0:T(8,128)S(1)}, f32[4,8,64,256]{3,2,1,0:T(8,128)}, u32[]{:S(2)}) copy-start(f32[4,8,64,256]{3,2,1,0:T(8,128)} %copy.47) | copy-start | bytes 6291460
  109.2 0.7 copy-start.2
Sparse Core Ops, SparseCore 0:
  56.6 47.3 reduce-scatter.1

commit v12 on v11

--- a/solution.py
+++ b/solution.py
@@ -1,4 +1,5 @@
 import functools
+import math
 
 import jax
 import jax.numpy as jnp
@@ -11,9 +12,27 @@
 MESH = pl.DeviceIdType.MESH
 
 
-def ring_scatter_kernel(jobs, *refs):
+def ring_scatter_kernel(jobs, produce, *refs):
     count = len(jobs)
-    terms, outs, scratch = refs[:count], refs[count:2 * count], refs[2 * count:]
+    if produce:
+        factors, refs = refs[:2 * produce], refs[2 * produce:]
+        made, refs = refs[-1], refs[:-1]
+        terms = (made,) + refs[:count - 1]
+        outs, scratch = refs[count - 1:2 * count - 1], refs[2 * count - 1:]
+        grads, weights = factors[:produce], factors[produce:]
+        block_rows = made.shape[2]
+        for block in range(made.shape[0]):
+            rows = pl.ds(block * block_rows, block_rows)
+            total = None
+            for grad, weight in zip(grads, weights):
+                part = lax.dot_general(
+                    grad[...], weight[rows, :], (((1,), (1,)), ((), ())),
+                    preferred_element_type=jnp.float32,
+                )
+                total = part if total is None else total + part
+            made[block] = total
+    else:
+        terms, outs, scratch = refs[:count], refs[count:2 * count], refs[2 * count:]
     barrier = pltpu.get_barrier_semaphore()
     places, greeted = [], 0
     for axis, n, _, direct in jobs:
@@ -112,8 +131,9 @@
                 copy.wait_send()
 
 
-def ring_scatter(parts, channel):
+def ring_scatter(parts, channel, factors=None):
     jobs = tuple((axis, terms.shape[0], pieces, direct) for terms, axis, _, pieces, direct in parts)
+    produce = len(factors[0]) if factors else 0
     scratch = []
     for terms, _, _, pieces, direct in parts:
         n, rows, width = terms.shape
@@ -131,20 +151,24 @@
             pltpu.SemaphoreType.DMA((2 * pieces, n - 1)),
             pltpu.SemaphoreType.DMA((2 * pieces, n - 1)),
         ]
-    size = sum(part[0].size for part in parts)
+    size = sum(math.prod(part[0].shape) for part in parts)
+    operands = [part[0] for part in parts]
+    if produce:
+        scratch.append(pltpu.VMEM(parts[0][0].shape, jnp.float32))
+        operands = list(factors[0]) + list(factors[1]) + operands[1:]
     return pl.pallas_call(
-        functools.partial(ring_scatter_kernel, jobs),
+        functools.partial(ring_scatter_kernel, jobs, produce),
         out_shape=tuple(
             jax.ShapeDtypeStruct(part[0].shape[1:], part[2]) for part in parts
         ),
-        in_specs=[pl.BlockSpec(memory_space=pltpu.VMEM)] * len(parts),
+        in_specs=[pl.BlockSpec(memory_space=pltpu.VMEM)] * len(operands),
         out_specs=tuple(pl.BlockSpec(memory_space=pltpu.VMEM) for _ in parts),
         scratch_shapes=scratch,
         compiler_params=pltpu.CompilerParams(
             collective_id=channel, has_side_effects=True, vmem_limit_bytes=48 * 1024 * 1024
         ),
         cost_estimate=pl.CostEstimate(flops=2 * size, bytes_accessed=8 * size, transcendentals=0),
-    )(*(part[0] for part in parts))
+    )(*operands)
 
 
 def exchange_kernel(n, axis, kv_ref, qg_ref, prefix_ref, suffix_ref,
@@ -301,17 +325,7 @@
     d_keys = d_keys.astype(jnp.bfloat16).reshape(num_rows, width)
     d_values = d_values.astype(jnp.bfloat16).reshape(num_rows, width)
     groups = lax.axis_size("head")
-
-    def by_block(weight):
-        return weight.reshape(groups, weight.shape[0] // groups, width)
-
-    head_terms = jnp.einsum("tk,bdk->btd", d_query, by_block(w_query), preferred_element_type=jnp.float32)
-    head_terms = head_terms + jnp.einsum(
-        "tk,bdk->btd", d_keys, by_block(w_key), preferred_element_type=jnp.float32
-    )
-    head_terms = head_terms + jnp.einsum(
-        "tk,bdk->btd", d_values, by_block(w_value), preferred_element_type=jnp.float32
-    )
+    head_terms = jax.ShapeDtypeStruct((groups, num_rows, w_query.shape[0] // groups), jnp.float32)
     total_rows = lax.axis_size("seq") * lax.axis_size("dp") * num_rows
     grad_scale = jnp.float32(1.0) / jnp.sqrt(jnp.float32(total_rows))
     seqs, shares = lax.axis_size("seq"), lax.axis_size("dp")
@@ -322,10 +336,12 @@
         "tspr,tk->psrk", grad_blocks, attention, preferred_element_type=jnp.float32
     ) * grad_scale
     term_out = term_out.reshape(shares, -1, width)
-    term_qkv, head_terms, term_out = lax.optimization_barrier((term_qkv, head_terms, term_out))
+    factors = ((d_query, d_keys, d_values), (w_query, w_key, w_value))
+    term_qkv, factors, term_out = lax.optimization_barrier((term_qkv, factors, term_out))
     summed = lax.psum_scatter(term_qkv, "seq", scatter_dimension=0, tiled=True)
     input_grad, out_shared = ring_scatter(
-        [(head_terms, "head", jnp.bfloat16, 4, False), (term_out, "dp", jnp.float32, 2, False)], 0
+        [(head_terms, "head", jnp.bfloat16, 4, False), (term_out, "dp", jnp.float32, 2, False)], 0,
+        factors,
     )
     input_grad = input_grad[None]
     summed, input_grad, out_shared = lax.optimization_barrier((summed, input_grad, out_shared))

time: 137 us -> 137 us (level)
  matrix products: 29.7 us -> 25 us
  local copies, waits for them, and re-layouts: 12 us -> 15 us
    dot_general x3 -> x0, matrix products: 11.9 us -> none  [the longest x1 6.29 us: local(): jnp.einsum('tk,bdk->btd', d_values, by_block(w_value), preferred_element_...]
    reshape x0 -> x3, local copies, waits for them, and re-layouts: none -> 2.3 us  [the longest x1 1.08 us: local(): d_keys = d_keys.astype(jnp.bfloat16).reshape(num_rows, width)]
    unnamed x1, matrix products: 0.96 us -> 2.55 us
    dot_general x1, matrix products: 0.48 us -> 1.95 us  [local(): jnp.einsum('hts,she->the', scores_qk, value_rows, preferred_element_type=...]
    unnamed x26 -> x32, local copies, waits for them, and re-layouts: 8.47 us -> 9.16 us
  transfers between devices with their start and end apart: 1 -> 1, of which waited for: 0 -> 0; matrix products, arithmetic and copies ran while one was open for 0% -> 0% of each run, Pallas kernels for 37% -> 38%
where the time goes in v12:
time: 137 us
  Pallas kernels  81.5 us (59%)
  matrix products  25 us (18%)
  local copies, waits for them, and re-layouts  15 us (11%)
  between operations  14.3 us (10%)
    pallas_call x2, Pallas kernels, ring_scatter(): pl.pallas_call(functools.partial(ring_scatter_kernel, jobs, produce), out...  67.7 us
    pallas_call x1, Pallas kernels, exchange_states(): pl.pallas_call(functools.partial(exchange_kernel, n, axis), out_shape=(ja...  13.8 us
    unnamed x32, local copies, waits for them, and re-layouts  9.16 us
    dot_general x1, matrix products, local(): jnp.einsum('td,tk->dk', in_rows, grads, preferred_element_type=jnp.float32)  4.5 us
    dot_general x3, matrix products, project(): jnp.dot(in_rows, weight, preferred_element_type=jnp.float32)  3.5 us
  transfers between devices with their start and end apart: 1, of which 0 were waited for; matrix products, arithmetic and copies ran while one was open for 0% of the time, Pallas kernels for 38%

profile of v12, /device:TPU:8, one launch (start us, length us, event | category | flops | bytes accessed | tf_op | source)
XLA Modules:
  0.0 136.9 jit_solution(7881816651229247496)
XLA Ops:
  8.0 0.8 copy-done
  8.9 2.0 %fusion.28 = bf16[512,256]{0,1:T(8,128)(2,1)S(1)} fusion(bf16[2048,256]{1,0:T(8,128)(2,1)} %refs_3_, bf16[1,512,2048]{2,1,0:T(8,128)(2,1)S(1)} %copy-done), kind=kOutput, calls=%fused_computation.28 | convolution fusion | flops 537001984 | bytes 3407872 | tf_op jit(solution)/shard_map/dot_general | solution.py:278
  14.8 0.9 fusion.47.qg_ref
  15.7 0.9 fusion.46.kv_ref
  16.6 13.8 %shard_map.101 = (f32[2,128,128]{2,1,0:T(8,128)}, f32[2,128,128]{2,1,0:T(8,128)}) custom-call(f32[2,128,128]{2,1,0:T(8,128)} %fusion.46.kv_ref, f32[2,128,128]{2,1,0:T(8,128)} %fusion.47.qg_ref), custom_call_target="tpu_custom_call" | custom-call | tf_op jit(solution)/shard_map/pallas_call | solution.py:252
  30.4 2.1 %fusion.40 = f32[2,128,512]{2,1,0:T(8,128)} fusion(bf16[512,2,128]{0,2,1:T(8,128)(2,1)} %bitcast.98, f32[2,128,128]{2,1,0:T(8,128)} %get-tuple-element.22), kind=kOutput, calls=%fused_computation.39 | convolution fusion | flops 33587200 | bytes 917504 | tf_op jit(solution)/shard_map/thd,hde->the/dot_general | solution.py:306
  32.6 1.1 fusion.42
  33.7 2.0 %fusion.36 = f32[2,128,512]{2,1,0:T(8,128)} fusion(bf16[512,2,128]{0,2,1:T(8,128)(2,1)S(1)} %bitcast.94, f32[2,128,128]{2,1,0:T(8,128)} %get-tuple-element.23), kind=kOutput, calls=%fused_computation.35 | convolution fusion | flops 33587200 | bytes 917504 | tf_op jit(solution)/shard_map/shd,hde->she/dot_general | solution.py:321
  36.5 1.5 %select_convert_fusion = bf16[2,512,512]{2,1,0:T(8,128)(2,1)} fusion(bf16[512,2,128]{0,2,1:T(8,128)(2,1)S(1)} %bitcast.99, bf16[512,2,128]{0,2,1:T(8,128)(2,1)S(1)} %bitcast.95, pred[512,512]{1,0:T(8,128)(4,1)S(1)} %copy-done.13), kind=kOutput, calls=%fused_computation.13 | convolution fusion | flops 135266304 | bytes 1835008 | tf_op jit(solution)/shard_map/thd,shd->hts/dot_general | solution.py:299
  38.0 1.0 fusion.16
  39.6 1.1 copy.63.refs_1_
  40.7 2.0 %fusion.21 = bf16[2,128,512]{2,1,0:T(8,128)(2,1)S(1)} fusion(f32[2,128,512]{2,1,0:T(8,128)} %fusion.40, bf16[512,2,128]{0,2,1:T(8,128)(2,1)S(1)} %bitcast.88, bf16[2,512,512]{2,1,0:T(8,128)(2,1)} %select_convert_fusion, f32[512]{0:T(512)S(1)} %multiply_rsqrt_fusion), kind=kOutput, calls=%fused_computation.25 | convolution fusion | flops 134610944 | bytes 2099200 | tf_op jit(solution)/shard_map/hts,she->the/dot_general | solution.py:303
  42.7 1.0 fusion.17
  43.7 1.1 copy.64.refs_2_
  44.8 2.5 %fusion = f32[256,2048]{0,1:S(1)} fusion(bf16[512,256]{0,1:T(8,128)(2,1)S(1)} %bitcast.101, bf16[1,512,2048]{2,1,0:T(8,128)(2,1)} %param.11), kind=kOutput, calls=%fused_computation.1 | convolution fusion | flops 536870912 | bytes 4456448
  47.6 1.5 %copy.47 = f32[4,8,64,256]{3,2,1,0:T(8,128)} copy(f32[4,8,64,256]{3,2,0,1:T(8,128)S(1)} %multiply_bitcast_fusion.1) | data formatting | bytes 4194304 | tf_op jit(solution)/shard_map/mul | solution.py:335
  49.1 4.5 %multiply_bitcast_fusion = f32[2048,768]{0,1:T(8,128)} fusion(bf16[1,512,2048]{2,1,0:T(8,128)(2,1)S(1)} %copy-done, bf16[512,256]{1,0:T(8,128)(2,1)S(1)} %copy.64.refs_2_, bf16[512,256]{1,0:T(8,128)(2,1)S(1)} %copy.63.refs_1_, bf16[512,256]{1,0:T(8,128)(2,1)S(1)} %copy.62.refs_0_), kind=kOutput, calls=%fused_computation | convolution fusion | flops 1614544896 | bytes 9175040 | tf_op jit(solution)/shard_map/td,tk->dk/dot_general | solution.py:333
  53.7 1.2 copy-done.2
  54.9 1.2 copy-done.4
  56.1 1.2 copy-done.5
  57.3 52.3 %shard_map.102 = (bf16[512,256]{1,0:T(8,128)(2,1)S(1)}, f32[512,256]{1,0:T(8,128)S(1)}) custom-call(bf16[512,256]{1,0:T(8,128)(2,1)S(1)} %copy.62.refs_0_, bf16[512,256]{1,0:T(8,128)(2,1)S(1)} %copy.63.refs_1_, bf16[512,256]{1,0:T(8,128)(2,1)S(1)} %copy.64.refs_2_, bf16[2048,256]{1,0:T(8,128)(2,1)S(1)} %copy-done.5, bf16[2048,256]{1,0:T(8,128)(2,1)S(1)} %copy-done.2, ...), custom_call_target="tpu_custom_call" | custom-call | flops 3145728 | bytes 12582912 | tf_op jit(solution)/shard_map/pallas_call | solution.py:159
  110.3 1.4 %copy.48 = f32[256,768]{1,0:T(8,128)S(1)} copy(f32[256,768]{0,1:T(8,128)} %reduce-scatter.2.cloned.1.call-done) | data formatting | bytes 1572864 | tf_op jit(solution)/shard_map/optimization_barrier | solution.py:347
  111.7 15.4 %shard_map.103 = (f32[64,768]{1,0:T(8,128)S(1)}, f32[64,256]{1,0:T(8,128)S(1)}) custom-call(f32[4,64,768]{2,1,0:T(8,128)S(1)} %bitcast.79, f32[8,64,256]{2,1,0:T(8,128)S(1)} %bitcast.80), custom_call_target="tpu_custom_call" | custom-call | flops 655360 | bytes 2621440 | tf_op jit(solution)/shard_map/pallas_call | solution.py:159
  127.8 1.7 %copy.67 = bf16[1,512,256]{2,1,0:T(8,128)(2,1)} copy(bf16[1,512,256]{2,1,0:T(8,128)(2,1)} %bitcast.81) | data formatting | bytes 524288
  (41 shorter events, 8.4 us)
Async XLA Ops:
  7.2 1.7 %copy-start = (bf16[1,512,2048]{2,1,0:T(8,128)(2,1)S(1)}, bf16[1,512,2048]{2,1,0:T(8,128)(2,1)}, u32[]{:S(2)}) copy-start(bf16[1,512,2048]{2,1,0:T(8,128)(2,1)} %param.6) | copy-start | bytes 6291460
  7.2 3.7 %copy-start.1 = (bf16[2048,256]{1,0:T(8,128)(2,1)S(1)}, bf16[2048,256]{1,0:T(8,128)(2,1)}, u32[]{:S(2)}) copy-start(bf16[2048,256]{1,0:T(8,128)(2,1)} %refs_4_) | copy-start | bytes 3145732
  7.2 103.1 %reduce-scatter.2.cloned.1.call-start = ((), (), s32[]{:S(2)}) async-start(), calls=%async_computation.1 | async-start | bytes 7077888 | tf_op jit(solution)/shard_map/reduce_scatter | solution.py:341
  10.8 3.9 %copy-start.8 = (bf16[512,256]{0,1:T(8,128)(2,1)}, bf16[512,256]{0,1:T(8,128)(2,1)S(1)}, u32[]{:S(2)}) copy-start(bf16[512,256]{0,1:T(8,128)(2,1)S(1)} %fusion.28) | copy-start | bytes 786436
  10.9 1.3 copy-start.3
  12.2 1.6 %copy-start.10 = (bf16[1,512,2048]{2,1,0:T(8,128)(2,1)S(1)}, bf16[1,512,2048]{2,1,0:T(8,128)(2,1)}, u32[]{:S(2)}) copy-start(bf16[1,512,2048]{2,1,0:T(8,128)(2,1)} %param.11) | copy-start | bytes 6291460
  12.2 1.9 %copy-start.14 = (bf16[256,2048]{1,0:T(8,128)(2,1)S(1)}, bf16[256,2048]{1,0:T(8,128)(2,1)}, u32[]{:S(2)}) copy-start(bf16[256,2048]{1,0:T(8,128)(2,1)} %param.10) | copy-start | bytes 3145732
  16.6 19.4 %copy-start.13 = (pred[512,512]{1,0:T(8,128)(4,1)S(1)}, pred[512,512]{1,0:T(8,128)(4,1)}, u32[]{:S(2)}) copy-start(pred[512,512]{1,0:T(8,128)(4,1)} %iota_compare_fusion) | copy-start | bytes 786436
  30.4 5.3 %copy-start.12 = (f32[2,128,128]{2,1,0:T(8,128)S(1)}, f32[2,128,128]{2,1,0:T(8,128)}, u32[]{:S(2)}) copy-start(f32[2,128,128]{2,1,0:T(8,128)} %get-tuple-element.23) | copy-start | bytes 393220
  33.7 2.8 %copy-start.9 = (bf16[512,256]{0,1:T(8,128)(2,1)S(1)}, bf16[512,256]{0,1:T(8,128)(2,1)}, u32[]{:S(2)}) copy-start(bf16[512,256]{0,1:T(8,128)(2,1)} %copy-done.8) | copy-start | bytes 786436
  40.7 2.0 %copy-start.7 = (bf16[2,512,512]{2,1,0:T(8,128)(2,1)S(1)}, bf16[2,512,512]{2,1,0:T(8,128)(2,1)}, u32[]{:S(2)}) copy-start(bf16[2,512,512]{2,1,0:T(8,128)(2,1)} %select_convert_fusion) | copy-start | bytes 3145732
  40.7 2.0 %copy-start.11 = (f32[2,128,512]{2,1,0:T(8,128)S(1)}, f32[2,128,512]{2,1,0:T(8,128)}, u32[]{:S(2)}) copy-start(f32[2,128,512]{2,1,0:T(8,128)} %fusion.36) | copy-start | bytes 1572868
  53.6 1.2 copy-start.2
  54.9 1.2 copy-start.4
  56.1 1.2 copy-start.5
  109.6 0.7 copy-start.6
Sparse Core Ops, SparseCore 0:
  53.8 47.3 reduce-scatter.1

commit v13 on v12

--- a/solution.py
+++ b/solution.py
@@ -340,7 +340,7 @@
     term_qkv, factors, term_out = lax.optimization_barrier((term_qkv, factors, term_out))
     summed = lax.psum_scatter(term_qkv, "seq", scatter_dimension=0, tiled=True)
     input_grad, out_shared = ring_scatter(
-        [(head_terms, "head", jnp.bfloat16, 4, False), (term_out, "dp", jnp.float32, 2, False)], 0,
+        [(head_terms, "head", jnp.bfloat16, 4, False), (term_out, "dp", jnp.float32, 1, True)], 0,
         factors,
     )
     input_grad = input_grad[None]

time: 137 us -> 137 us (level)
  transfers between devices with their start and end apart: 1 -> 1, of which waited for: 0 -> 0; matrix products, arithmetic and copies ran while one was open for 0% -> 0% of each run, Pallas kernels for 38% -> 39%
where the time goes in v13:
time: 137 us
  Pallas kernels  81.5 us (59%)
  matrix products  25 us (18%)
  local copies, waits for them, and re-layouts  15 us (11%)
  between operations  14.3 us (10%)
    pallas_call x2, Pallas kernels, ring_scatter(): pl.pallas_call(functools.partial(ring_scatter_kernel, jobs, produce), out...  67.9 us
    pallas_call x1, Pallas kernels, exchange_states(): pl.pallas_call(functools.partial(exchange_kernel, n, axis), out_shape=(ja...  13.6 us
    unnamed x32, local copies, waits for them, and re-layouts  9.17 us
    dot_general x1, matrix products, local(): jnp.einsum('td,tk->dk', in_rows, grads, preferred_element_type=jnp.float32)  4.5 us
    dot_general x3, matrix products, project(): jnp.dot(in_rows, weight, preferred_element_type=jnp.float32)  3.49 us
  transfers between devices with their start and end apart: 1, of which 0 were waited for; matrix products, arithmetic and copies ran while one was open for 0% of the time, Pallas kernels for 39%

profile of v13, /device:TPU:8, one launch (start us, length us, event | category | flops | bytes accessed | tf_op | source)
XLA Modules:
  0.0 136.9 jit_solution(9353799165661859879)
XLA Ops:
  8.0 0.8 copy-done
  8.9 2.0 %fusion.28 = bf16[512,256]{0,1:T(8,128)(2,1)S(1)} fusion(bf16[2048,256]{1,0:T(8,128)(2,1)} %refs_3_, bf16[1,512,2048]{2,1,0:T(8,128)(2,1)S(1)} %copy-done), kind=kOutput, calls=%fused_computation.28 | convolution fusion | flops 537001984 | bytes 3407872 | tf_op jit(solution)/shard_map/dot_general | solution.py:278
  14.8 0.9 fusion.47.qg_ref
  15.7 0.9 fusion.46.kv_ref
  16.6 13.6 %shard_map.101 = (f32[2,128,128]{2,1,0:T(8,128)}, f32[2,128,128]{2,1,0:T(8,128)}) custom-call(f32[2,128,128]{2,1,0:T(8,128)} %fusion.46.kv_ref, f32[2,128,128]{2,1,0:T(8,128)} %fusion.47.qg_ref), custom_call_target="tpu_custom_call" | custom-call | tf_op jit(solution)/shard_map/pallas_call | solution.py:252
  30.2 2.1 %fusion.40 = f32[2,128,512]{2,1,0:T(8,128)} fusion(bf16[512,2,128]{0,2,1:T(8,128)(2,1)} %bitcast.98, f32[2,128,128]{2,1,0:T(8,128)} %get-tuple-element.22), kind=kOutput, calls=%fused_computation.39 | convolution fusion | flops 33587200 | bytes 917504 | tf_op jit(solution)/shard_map/thd,hde->the/dot_general | solution.py:306
  32.4 1.1 fusion.42
  33.5 2.0 %fusion.36 = f32[2,128,512]{2,1,0:T(8,128)} fusion(bf16[512,2,128]{0,2,1:T(8,128)(2,1)S(1)} %bitcast.94, f32[2,128,128]{2,1,0:T(8,128)} %get-tuple-element.23), kind=kOutput, calls=%fused_computation.35 | convolution fusion | flops 33587200 | bytes 917504 | tf_op jit(solution)/shard_map/shd,hde->she/dot_general | solution.py:321
  36.3 1.5 %select_convert_fusion = bf16[2,512,512]{2,1,0:T(8,128)(2,1)} fusion(bf16[512,2,128]{0,2,1:T(8,128)(2,1)S(1)} %bitcast.99, bf16[512,2,128]{0,2,1:T(8,128)(2,1)S(1)} %bitcast.95, pred[512,512]{1,0:T(8,128)(4,1)S(1)} %copy-done.13), kind=kOutput, calls=%fused_computation.13 | convolution fusion | flops 135266304 | bytes 1835008 | tf_op jit(solution)/shard_map/thd,shd->hts/dot_general | solution.py:299
  37.8 1.0 fusion.16
  39.5 1.1 copy.63.refs_1_
  40.6 2.0 %fusion.21 = bf16[2,128,512]{2,1,0:T(8,128)(2,1)S(1)} fusion(f32[2,128,512]{2,1,0:T(8,128)} %fusion.40, bf16[512,2,128]{0,2,1:T(8,128)(2,1)S(1)} %bitcast.88, bf16[2,512,512]{2,1,0:T(8,128)(2,1)} %select_convert_fusion, f32[512]{0:T(512)S(1)} %multiply_rsqrt_fusion), kind=kOutput, calls=%fused_computation.25 | convolution fusion | flops 134610944 | bytes 2099200 | tf_op jit(solution)/shard_map/hts,she->the/dot_general | solution.py:303
  42.5 1.0 fusion.17
  43.6 1.1 copy.64.refs_2_
  44.6 2.5 %fusion = f32[256,2048]{0,1:S(1)} fusion(bf16[512,256]{0,1:T(8,128)(2,1)S(1)} %bitcast.101, bf16[1,512,2048]{2,1,0:T(8,128)(2,1)} %param.11), kind=kOutput, calls=%fused_computation.1 | convolution fusion | flops 536870912 | bytes 4456448
  47.4 1.5 %copy.47 = f32[4,8,64,256]{3,2,1,0:T(8,128)} copy(f32[4,8,64,256]{3,2,0,1:T(8,128)S(1)} %multiply_bitcast_fusion.1) | data formatting | bytes 4194304 | tf_op jit(solution)/shard_map/mul | solution.py:335
  48.9 4.5 %multiply_bitcast_fusion = f32[2048,768]{0,1:T(8,128)} fusion(bf16[1,512,2048]{2,1,0:T(8,128)(2,1)S(1)} %copy-done, bf16[512,256]{1,0:T(8,128)(2,1)S(1)} %copy.64.refs_2_, bf16[512,256]{1,0:T(8,128)(2,1)S(1)} %copy.63.refs_1_, bf16[512,256]{1,0:T(8,128)(2,1)S(1)} %copy.62.refs_0_), kind=kOutput, calls=%fused_computation | convolution fusion | flops 1614544896 | bytes 9175040 | tf_op jit(solution)/shard_map/td,tk->dk/dot_general | solution.py:333
  53.5 1.2 copy-done.2
  54.7 1.2 copy-done.4
  55.9 1.2 copy-done.5
  57.1 53.0 %shard_map.102 = (bf16[512,256]{1,0:T(8,128)(2,1)S(1)}, f32[512,256]{1,0:T(8,128)S(1)}) custom-call(bf16[512,256]{1,0:T(8,128)(2,1)S(1)} %copy.62.refs_0_, bf16[512,256]{1,0:T(8,128)(2,1)S(1)} %copy.63.refs_1_, bf16[512,256]{1,0:T(8,128)(2,1)S(1)} %copy.64.refs_2_, bf16[2048,256]{1,0:T(8,128)(2,1)S(1)} %copy-done.5, bf16[2048,256]{1,0:T(8,128)(2,1)S(1)} %copy-done.2, ...), custom_call_target="tpu_custom_call" | custom-call | flops 3145728 | bytes 12582912 | tf_op jit(solution)/shard_map/pallas_call | solution.py:159
  110.8 1.4 %copy.48 = f32[256,768]{1,0:T(8,128)S(1)} copy(f32[256,768]{0,1:T(8,128)} %reduce-scatter.2.cloned.1.call-done) | data formatting | bytes 1572864 | tf_op jit(solution)/shard_map/optimization_barrier | solution.py:347
  112.2 14.9 %shard_map.103 = (f32[64,768]{1,0:T(8,128)S(1)}, f32[64,256]{1,0:T(8,128)S(1)}) custom-call(f32[4,64,768]{2,1,0:T(8,128)S(1)} %bitcast.79, f32[8,64,256]{2,1,0:T(8,128)S(1)} %bitcast.80), custom_call_target="tpu_custom_call" | custom-call | flops 655360 | bytes 2621440 | tf_op jit(solution)/shard_map/pallas_call | solution.py:159
  127.8 1.7 %copy.67 = bf16[1,512,256]{2,1,0:T(8,128)(2,1)} copy(bf16[1,512,256]{2,1,0:T(8,128)(2,1)} %bitcast.81) | data formatting | bytes 524288
  (41 shorter events, 8.4 us)
Async XLA Ops:
  7.2 1.7 %copy-start = (bf16[1,512,2048]{2,1,0:T(8,128)(2,1)S(1)}, bf16[1,512,2048]{2,1,0:T(8,128)(2,1)}, u32[]{:S(2)}) copy-start(bf16[1,512,2048]{2,1,0:T(8,128)(2,1)} %param.6) | copy-start | bytes 6291460
  7.2 3.7 %copy-start.1 = (bf16[2048,256]{1,0:T(8,128)(2,1)S(1)}, bf16[2048,256]{1,0:T(8,128)(2,1)}, u32[]{:S(2)}) copy-start(bf16[2048,256]{1,0:T(8,128)(2,1)} %refs_4_) | copy-start | bytes 3145732
  7.2 103.6 %reduce-scatter.2.cloned.1.call-start = ((), (), s32[]{:S(2)}) async-start(), calls=%async_computation.1 | async-start | bytes 7077888 | tf_op jit(solution)/shard_map/reduce_scatter | solution.py:341
  10.8 3.9 %copy-start.8 = (bf16[512,256]{0,1:T(8,128)(2,1)}, bf16[512,256]{0,1:T(8,128)(2,1)S(1)}, u32[]{:S(2)}) copy-start(bf16[512,256]{0,1:T(8,128)(2,1)S(1)} %fusion.28) | copy-start | bytes 786436
  10.9 1.3 copy-start.3
  12.2 1.6 %copy-start.10 = (bf16[1,512,2048]{2,1,0:T(8,128)(2,1)S(1)}, bf16[1,512,2048]{2,1,0:T(8,128)(2,1)}, u32[]{:S(2)}) copy-start(bf16[1,512,2048]{2,1,0:T(8,128)(2,1)} %param.11) | copy-start | bytes 6291460
  12.2 1.9 %copy-start.14 = (bf16[256,2048]{1,0:T(8,128)(2,1)S(1)}, bf16[256,2048]{1,0:T(8,128)(2,1)}, u32[]{:S(2)}) copy-start(bf16[256,2048]{1,0:T(8,128)(2,1)} %param.10) | copy-start | bytes 3145732
  16.6 19.2 %copy-start.13 = (pred[512,512]{1,0:T(8,128)(4,1)S(1)}, pred[512,512]{1,0:T(8,128)(4,1)}, u32[]{:S(2)}) copy-start(pred[512,512]{1,0:T(8,128)(4,1)} %iota_compare_fusion) | copy-start | bytes 786436
  30.2 5.3 %copy-start.12 = (f32[2,128,128]{2,1,0:T(8,128)S(1)}, f32[2,128,128]{2,1,0:T(8,128)}, u32[]{:S(2)}) copy-start(f32[2,128,128]{2,1,0:T(8,128)} %get-tuple-element.23) | copy-start | bytes 393220
  33.5 2.8 %copy-start.9 = (bf16[512,256]{0,1:T(8,128)(2,1)S(1)}, bf16[512,256]{0,1:T(8,128)(2,1)}, u32[]{:S(2)}) copy-start(bf16[512,256]{0,1:T(8,128)(2,1)} %copy-done.8) | copy-start | bytes 786436
  40.5 2.0 %copy-start.7 = (bf16[2,512,512]{2,1,0:T(8,128)(2,1)S(1)}, bf16[2,512,512]{2,1,0:T(8,128)(2,1)}, u32[]{:S(2)}) copy-start(bf16[2,512,512]{2,1,0:T(8,128)(2,1)} %select_convert_fusion) | copy-start | bytes 3145732
  40.6 2.0 %copy-start.11 = (f32[2,128,512]{2,1,0:T(8,128)S(1)}, f32[2,128,512]{2,1,0:T(8,128)}, u32[]{:S(2)}) copy-start(f32[2,128,512]{2,1,0:T(8,128)} %fusion.36) | copy-start | bytes 1572868
  53.5 1.2 copy-start.2
  54.7 1.2 copy-start.4
  55.9 1.2 copy-start.5
  110.1 0.7 copy-start.6
Sparse Core Ops, SparseCore 0:
  53.6 47.3 reduce-scatter.1

commit v14 on v13

--- a/solution.py
+++ b/solution.py
@@ -340,10 +340,10 @@
     term_qkv, factors, term_out = lax.optimization_barrier((term_qkv, factors, term_out))
     summed = lax.psum_scatter(term_qkv, "seq", scatter_dimension=0, tiled=True)
     input_grad, out_shared = ring_scatter(
-        [(head_terms, "head", jnp.bfloat16, 4, False), (term_out, "dp", jnp.float32, 1, True)], 0,
+        [(head_terms, "head", jnp.float32, 4, False), (term_out, "dp", jnp.float32, 2, False)], 0,
         factors,
     )
-    input_grad = input_grad[None]
+    input_grad = input_grad.astype(jnp.bfloat16)[None]
     summed, input_grad, out_shared = lax.optimization_barrier((summed, input_grad, out_shared))
     summed, out_summed = ring_scatter(
         [

time: 137 us -> 136 us (level)
  local copies, waits for them, and re-layouts: 15 us -> 12.7 us
    unnamed x32 -> x29, local copies, waits for them, and re-layouts: 9.17 us -> 6.79 us
  transfers between devices with their start and end apart: 1 -> 1, of which waited for: 0 -> 0; matrix products, arithmetic and copies ran while one was open for 0% -> 1% of each run, Pallas kernels for 39% -> 39%
where the time goes in v14:
time: 136 us; the launch traced here: 135 us
  Pallas kernels  81.5 us (60%)
  matrix products  25 us (18%)
  between operations  14.3 us (11%)
  local copies, waits for them, and re-layouts  12.7 us (9%)
  other arithmetic  1.74 us (1%)
    pallas_call x2, Pallas kernels, ring_scatter(): pl.pallas_call(functools.partial(ring_scatter_kernel, jobs, produce), out...  67.6 us
    pallas_call x1, Pallas kernels, exchange_states(): pl.pallas_call(functools.partial(exchange_kernel, n, axis), out_shape=(ja...  13.8 us
    unnamed x29, local copies, waits for them, and re-layouts  6.79 us
    dot_general x1, matrix products, local(): jnp.einsum('td,tk->dk', in_rows, grads, preferred_element_type=jnp.float32)  4.48 us
    dot_general x3, matrix products, project(): jnp.dot(in_rows, weight, preferred_element_type=jnp.float32)  3.5 us
  transfers between devices with their start and end apart: 1, of which 0 were waited for; matrix products, arithmetic and copies ran while one was open for 1% of the time, Pallas kernels for 39%

profile of v14, /device:TPU:8, one launch (start us, length us, event | category | flops | bytes accessed | tf_op | source)
XLA Modules:
  0.0 135.3 jit_solution(12166882440568128274)
XLA Ops:
  8.0 0.8 copy-done
  8.9 2.0 %fusion.28 = bf16[512,256]{0,1:T(8,128)(2,1)S(1)} fusion(bf16[2048,256]{1,0:T(8,128)(2,1)} %refs_3_, bf16[1,512,2048]{2,1,0:T(8,128)(2,1)S(1)} %copy-done), kind=kOutput, calls=%fused_computation.28 | convolution fusion | flops 537001984 | bytes 3407872 | tf_op jit(solution)/shard_map/dot_general | solution.py:278
  13.0 0.8 copy-done.9
  14.8 0.9 fusion.47.qg_ref
  15.7 0.9 fusion.46.kv_ref
  16.6 13.8 %shard_map.101 = (f32[2,128,128]{2,1,0:T(8,128)}, f32[2,128,128]{2,1,0:T(8,128)}) custom-call(f32[2,128,128]{2,1,0:T(8,128)} %fusion.46.kv_ref, f32[2,128,128]{2,1,0:T(8,128)} %fusion.47.qg_ref), custom_call_target="tpu_custom_call" | custom-call | tf_op jit(solution)/shard_map/pallas_call | solution.py:252
  30.4 2.1 %fusion.40 = f32[2,128,512]{2,1,0:T(8,128)} fusion(bf16[512,2,128]{0,2,1:T(8,128)(2,1)} %bitcast.98, f32[2,128,128]{2,1,0:T(8,128)} %get-tuple-element.22), kind=kOutput, calls=%fused_computation.40 | convolution fusion | flops 33587200 | bytes 917504 | tf_op jit(solution)/shard_map/thd,hde->the/dot_general | solution.py:306
  32.6 1.1 fusion.42
  33.7 2.0 %fusion.36 = f32[2,128,512]{2,1,0:T(8,128)} fusion(bf16[512,2,128]{0,2,1:T(8,128)(2,1)S(1)} %bitcast.94, f32[2,128,128]{2,1,0:T(8,128)} %get-tuple-element.23), kind=kOutput, calls=%fused_computation.36 | convolution fusion | flops 33587200 | bytes 917504 | tf_op jit(solution)/shard_map/shd,hde->she/dot_general | solution.py:321
  36.5 1.5 %select_convert_fusion = bf16[2,512,512]{2,1,0:T(8,128)(2,1)} fusion(bf16[512,2,128]{0,2,1:T(8,128)(2,1)S(1)} %bitcast.99, bf16[512,2,128]{0,2,1:T(8,128)(2,1)S(1)} %bitcast.95, pred[512,512]{1,0:T(8,128)(4,1)S(1)} %copy-done.12), kind=kOutput, calls=%fused_computation.13 | convolution fusion | flops 135266304 | bytes 1835008 | tf_op jit(solution)/shard_map/thd,shd->hts/dot_general | solution.py:299
  38.0 1.0 fusion.16
  39.7 1.1 copy.63.refs_1_
  40.8 2.0 %fusion.21 = bf16[2,128,512]{2,1,0:T(8,128)(2,1)S(1)} fusion(f32[2,128,512]{2,1,0:T(8,128)} %fusion.40, bf16[512,2,128]{0,2,1:T(8,128)(2,1)S(1)} %bitcast.88, bf16[2,512,512]{2,1,0:T(8,128)(2,1)} %select_convert_fusion, f32[512]{0:T(512)S(1)} %multiply_rsqrt_fusion), kind=kOutput, calls=%fused_computation.25 | convolution fusion | flops 134610944 | bytes 2099200 | tf_op jit(solution)/shard_map/hts,she->the/dot_general | solution.py:303
  42.7 1.0 fusion.17
  43.8 1.1 copy.64.refs_2_
  44.8 2.5 %fusion = f32[256,2048]{0,1:S(1)} fusion(bf16[512,256]{0,1:T(8,128)(2,1)S(1)} %bitcast.101, bf16[1,512,2048]{2,1,0:T(8,128)(2,1)} %param.11), kind=kOutput, calls=%fused_computation.1 | convolution fusion | flops 536870912 | bytes 4456448
  47.6 1.5 %copy.47 = f32[4,8,64,256]{3,2,1,0:T(8,128)} copy(f32[4,8,64,256]{3,2,0,1:T(8,128)S(1)} %multiply_bitcast_fusion.1) | data formatting | bytes 4194304 | tf_op jit(solution)/shard_map/mul | solution.py:335
  49.1 4.5 %multiply_bitcast_fusion = f32[2048,768]{0,1:T(8,128)} fusion(bf16[1,512,2048]{2,1,0:T(8,128)(2,1)S(1)} %copy-done, bf16[512,256]{1,0:T(8,128)(2,1)S(1)} %copy.64.refs_2_, bf16[512,256]{1,0:T(8,128)(2,1)S(1)} %copy.63.refs_1_, bf16[512,256]{1,0:T(8,128)(2,1)S(1)} %copy.62.refs_0_), kind=kOutput, calls=%fused_computation | convolution fusion | flops 1614544896 | bytes 9175040 | tf_op jit(solution)/shard_map/td,tk->dk/dot_general | solution.py:333
  53.7 1.2 copy-done.2
  54.9 1.2 copy-done.4
  56.1 1.2 copy-done.5
  57.3 52.3 %shard_map.102 = (f32[512,256]{1,0:T(8,128)S(1)}, f32[512,256]{1,0:T(8,128)S(1)}) custom-call(bf16[512,256]{1,0:T(8,128)(2,1)S(1)} %copy.62.refs_0_, bf16[512,256]{1,0:T(8,128)(2,1)S(1)} %copy.63.refs_1_, bf16[512,256]{1,0:T(8,128)(2,1)S(1)} %copy.64.refs_2_, bf16[2048,256]{1,0:T(8,128)(2,1)S(1)} %copy-done.5, bf16[2048,256]{1,0:T(8,128)(2,1)S(1)} %copy-done.2, ...), custom_call_target="tpu_custom_call" | custom-call | flops 3145728 | bytes 12582912 | tf_op jit(solution)/shard_map/pallas_call | solution.py:159
  110.3 1.4 %copy.48 = f32[256,768]{1,0:T(8,128)S(1)} copy(f32[256,768]{0,1:T(8,128)} %reduce-scatter.2.cloned.1.call-done) | data formatting | bytes 1572864 | tf_op jit(solution)/shard_map/optimization_barrier | solution.py:347
  111.7 15.4 %shard_map.103 = (f32[64,768]{1,0:T(8,128)S(1)}, f32[64,256]{1,0:T(8,128)S(1)}) custom-call(f32[4,64,768]{2,1,0:T(8,128)S(1)} %bitcast.80, f32[8,64,256]{2,1,0:T(8,128)S(1)} %bitcast.81), custom_call_target="tpu_custom_call" | custom-call | flops 655360 | bytes 2621440 | tf_op jit(solution)/shard_map/pallas_call | solution.py:159
  (39 shorter events, 7.6 us)
Async XLA Ops:
  7.2 1.7 %copy-start = (bf16[1,512,2048]{2,1,0:T(8,128)(2,1)S(1)}, bf16[1,512,2048]{2,1,0:T(8,128)(2,1)}, u32[]{:S(2)}) copy-start(bf16[1,512,2048]{2,1,0:T(8,128)(2,1)} %param.6) | copy-start | bytes 6291460
  7.2 3.7 %copy-start.1 = (bf16[2048,256]{1,0:T(8,128)(2,1)S(1)}, bf16[2048,256]{1,0:T(8,128)(2,1)}, u32[]{:S(2)}) copy-start(bf16[2048,256]{1,0:T(8,128)(2,1)} %refs_4_) | copy-start | bytes 3145732
  7.2 103.1 %reduce-scatter.2.cloned.1.call-start = ((), (), s32[]{:S(2)}) async-start(), calls=%async_computation.1 | async-start | bytes 7077888 | tf_op jit(solution)/shard_map/reduce_scatter | solution.py:341
  10.8 3.9 %copy-start.7 = (bf16[512,256]{0,1:T(8,128)(2,1)}, bf16[512,256]{0,1:T(8,128)(2,1)S(1)}, u32[]{:S(2)}) copy-start(bf16[512,256]{0,1:T(8,128)(2,1)S(1)} %fusion.28) | copy-start | bytes 786436
  10.9 1.3 copy-start.3
  12.2 1.6 %copy-start.9 = (bf16[1,512,2048]{2,1,0:T(8,128)(2,1)S(1)}, bf16[1,512,2048]{2,1,0:T(8,128)(2,1)}, u32[]{:S(2)}) copy-start(bf16[1,512,2048]{2,1,0:T(8,128)(2,1)} %param.11) | copy-start | bytes 6291460
  12.2 1.9 %copy-start.13 = (bf16[256,2048]{1,0:T(8,128)(2,1)S(1)}, bf16[256,2048]{1,0:T(8,128)(2,1)}, u32[]{:S(2)}) copy-start(bf16[256,2048]{1,0:T(8,128)(2,1)} %param.10) | copy-start | bytes 3145732
  16.6 19.4 %copy-start.12 = (pred[512,512]{1,0:T(8,128)(4,1)S(1)}, pred[512,512]{1,0:T(8,128)(4,1)}, u32[]{:S(2)}) copy-start(pred[512,512]{1,0:T(8,128)(4,1)} %iota_compare_fusion) | copy-start | bytes 786436
  30.4 5.3 %copy-start.11 = (f32[2,128,128]{2,1,0:T(8,128)S(1)}, f32[2,128,128]{2,1,0:T(8,128)}, u32[]{:S(2)}) copy-start(f32[2,128,128]{2,1,0:T(8,128)} %get-tuple-element.23) | copy-start | bytes 393220
  33.7 2.8 %copy-start.8 = (bf16[512,256]{0,1:T(8,128)(2,1)S(1)}, bf16[512,256]{0,1:T(8,128)(2,1)}, u32[]{:S(2)}) copy-start(bf16[512,256]{0,1:T(8,128)(2,1)} %copy-done.7) | copy-start | bytes 786436
  40.7 2.0 %copy-start.6 = (bf16[2,512,512]{2,1,0:T(8,128)(2,1)S(1)}, bf16[2,512,512]{2,1,0:T(8,128)(2,1)}, u32[]{:S(2)}) copy-start(bf16[2,512,512]{2,1,0:T(8,128)(2,1)} %select_convert_fusion) | copy-start | bytes 3145732
  40.8 2.0 %copy-start.10 = (f32[2,128,512]{2,1,0:T(8,128)S(1)}, f32[2,128,512]{2,1,0:T(8,128)}, u32[]{:S(2)}) copy-start(f32[2,128,512]{2,1,0:T(8,128)} %fusion.36) | copy-start | bytes 1572868
  53.6 1.2 copy-start.2
  54.9 1.2 copy-start.4
  56.1 1.2 copy-start.5
Sparse Core Ops, SparseCore 0:
  53.8 47.3 reduce-scatter.1

commit v15 on v14

--- a/solution.py
+++ b/solution.py
@@ -14,25 +14,20 @@
 
 def ring_scatter_kernel(jobs, produce, *refs):
     count = len(jobs)
+    terms, outs, scratch = refs[:count], refs[count:2 * count], refs[2 * count:]
     if produce:
         factors, refs = refs[:2 * produce], refs[2 * produce:]
-        made, refs = refs[-1], refs[:-1]
+        made, held, held_sem = refs[-2 - produce], refs[-1 - produce:-1], refs[-1]
+        refs = refs[:-2 - produce]
         terms = (made,) + refs[:count - 1]
         outs, scratch = refs[count - 1:2 * count - 1], refs[2 * count - 1:]
-        grads, weights = factors[:produce], factors[produce:]
-        block_rows = made.shape[2]
-        for block in range(made.shape[0]):
-            rows = pl.ds(block * block_rows, block_rows)
-            total = None
-            for grad, weight in zip(grads, weights):
-                part = lax.dot_general(
-                    grad[...], weight[rows, :], (((1,), (1,)), ((), ())),
-                    preferred_element_type=jnp.float32,
-                )
-                total = part if total is None else total + part
-            made[block] = total
-    else:
-        terms, outs, scratch = refs[:count], refs[count:2 * count], refs[2 * count:]
+        grads, weights = factors[:produce], held
+        loads = [
+            pltpu.make_async_copy(source, target, held_sem.at[index])
+            for index, (source, target) in enumerate(zip(factors[produce:], held))
+        ]
+        for load in loads:
+            load.start()
     barrier = pltpu.get_barrier_semaphore()
     places, greeted = [], 0
     for axis, n, _, direct in jobs:
@@ -46,6 +41,20 @@
             )
         greeted += len(offsets)
     pl.semaphore_wait(barrier, greeted)
+    if produce:
+        for load in loads:
+            load.wait()
+        block_rows = made.shape[2]
+        for block in range(made.shape[0]):
+            rows = pl.ds(block * block_rows, block_rows)
+            total = None
+            for grad, weight in zip(grads, weights):
+                part = lax.dot_general(
+                    grad[...], weight[rows, :], (((1,), (1,)), ((), ())),
+                    preferred_element_type=jnp.float32,
+                )
+                total = part if total is None else total + part
+            made[block] = total
 
     def direct_copy(job, offset):
         axis, n, _, _ = jobs[job]
@@ -153,19 +162,27 @@
         ]
     size = sum(math.prod(part[0].shape) for part in parts)
     operands = [part[0] for part in parts]
+    in_specs = [pl.BlockSpec(memory_space=pltpu.VMEM)] * len(operands)
     if produce:
         scratch.append(pltpu.VMEM(parts[0][0].shape, jnp.float32))
+        scratch += [pltpu.VMEM(weight.shape, weight.dtype) for weight in factors[1]]
+        scratch.append(pltpu.SemaphoreType.DMA((produce,)))
         operands = list(factors[0]) + list(factors[1]) + operands[1:]
+        in_specs = (
+            [pl.BlockSpec(memory_space=pltpu.VMEM)] * produce
+            + [pl.BlockSpec(memory_space=pl.ANY)] * produce
+            + [pl.BlockSpec(memory_space=pltpu.VMEM)] * (len(parts) - 1)
+        )
     return pl.pallas_call(
         functools.partial(ring_scatter_kernel, jobs, produce),
         out_shape=tuple(
             jax.ShapeDtypeStruct(part[0].shape[1:], part[2]) for part in parts
         ),
-        in_specs=[pl.BlockSpec(memory_space=pltpu.VMEM)] * len(operands),
+        in_specs=in_specs,
         out_specs=tuple(pl.BlockSpec(memory_space=pltpu.VMEM) for _ in parts),
         scratch_shapes=scratch,
         compiler_params=pltpu.CompilerParams(
-            collective_id=channel, has_side_effects=True, vmem_limit_bytes=48 * 1024 * 1024
+            collective_id=channel, has_side_effects=True
         ),
         cost_estimate=pl.CostEstimate(flops=2 * size, bytes_accessed=8 * size, transcendentals=0),
     )(*operands)

time: 136 us -> 143 us (1.051)
  Pallas kernels: 81.5 us -> 84.8 us
  local copies, waits for them, and re-layouts: 12.7 us -> 14.9 us
    pallas_call x2, Pallas kernels: 67.6 us -> 71.1 us  [ring_scatter(): pl.pallas_call(functools.partial(ring_scatter_kernel, jobs, produce), out...]
    unnamed x29 -> x37, local copies, waits for them, and re-layouts: 6.79 us -> 4.91 us
    reshape x1, local copies, waits for them, and re-layouts: 0.13 us -> 1.79 us  [local(): d_query = d_query.astype(jnp.bfloat16).reshape(num_rows, width)]
  transfers between devices with their start and end apart: 1 -> 1, of which waited for: 0 -> 0; matrix products, arithmetic and copies ran while one was open for 1% -> 1% of each run, Pallas kernels for 39% -> 38%
where the time goes in v15:
time: 143 us; the launch traced here: 142 us
  Pallas kernels  84.8 us (59%)
  matrix products  26 us (18%)
  local copies, waits for them, and re-layouts  14.9 us (10%)
  between operations  14.3 us (10%)
  other arithmetic  2.08 us (1%)
    pallas_call x2, Pallas kernels, ring_scatter(): pl.pallas_call(functools.partial(ring_scatter_kernel, jobs, produce), out...  71.1 us
    pallas_call x1, Pallas kernels, exchange_states(): pl.pallas_call(functools.partial(exchange_kernel, n, axis), out_shape=(ja...  13.8 us
    unnamed x37, local copies, waits for them, and re-layouts  4.91 us
    dot_general x1, matrix products, local(): jnp.einsum('td,tk->dk', in_rows, grads, preferred_element_type=jnp.float32)  4.48 us
    dot_general x3, matrix products, project(): jnp.dot(in_rows, weight, preferred_element_type=jnp.float32)  3.51 us
  transfers between devices with their start and end apart: 1, of which 0 were waited for; matrix products, arithmetic and copies ran while one was open for 1% of the time, Pallas kernels for 38%

profile of v15, /device:TPU:8, one launch (start us, length us, event | category | flops | bytes accessed | tf_op | source)
XLA Modules:
  0.0 142.2 jit_solution(13150203953592793367)
XLA Ops:
  7.4 1.5 %copy-done = bf16[1,512,2048]{2,1,0:T(8,128)(2,1)S(1)} copy-done((bf16[1,512,2048]{2,1,0:T(8,128)(2,1)S(1)}, bf16[1,512,2048]{2,1,0:T(8,128)(2,1)}, u32[]{:S(2)}) %copy-start) | copy-done | bytes 2097176
  8.9 2.0 %fusion.28 = bf16[512,256]{0,1:T(8,128)(2,1)S(1)} fusion(bf16[2048,256]{1,0:T(8,128)(2,1)} %refs_3_, bf16[1,512,2048]{2,1,0:T(8,128)(2,1)S(1)} %copy-done), kind=kOutput, calls=%fused_computation.28 | convolution fusion | flops 537001984 | bytes 3407872 | tf_op jit(solution)/shard_map/dot_general | solution.py:295
  13.0 0.9 copy-done.7
  16.7 13.8 %shard_map.101 = (f32[2,128,128]{2,1,0:T(8,128)}, f32[2,128,128]{2,1,0:T(8,128)}) custom-call(f32[2,128,128]{2,1,0:T(8,128)} %fusion.46.kv_ref, f32[2,128,128]{2,1,0:T(8,128)} %fusion.47.qg_ref), custom_call_target="tpu_custom_call" | custom-call | tf_op jit(solution)/shard_map/pallas_call | solution.py:269
  30.5 2.0 %fusion.40 = f32[2,128,512]{2,1,0:T(8,128)} fusion(bf16[512,2,128]{0,2,1:T(8,128)(2,1)S(1)} %bitcast.96, f32[2,128,128]{2,1,0:T(8,128)} %get-tuple-element.22), kind=kOutput, calls=%fused_computation.40 | convolution fusion | flops 33587200 | bytes 917504 | tf_op jit(solution)/shard_map/thd,hde->the/dot_general | solution.py:323
  32.5 1.1 fusion.42
  33.6 2.0 %fusion.36 = f32[2,128,512]{2,1,0:T(8,128)} fusion(bf16[512,2,128]{0,2,1:T(8,128)(2,1)S(1)} %bitcast.92, f32[2,128,128]{2,1,0:T(8,128)} %get-tuple-element.23), kind=kOutput, calls=%fused_computation.36 | convolution fusion | flops 33587200 | bytes 917504 | tf_op jit(solution)/shard_map/shd,hde->she/dot_general | solution.py:338
  36.6 1.5 %select_convert_fusion = bf16[2,512,512]{2,1,0:T(8,128)(2,1)S(1)} fusion(bf16[512,2,128]{0,2,1:T(8,128)(2,1)S(1)} %bitcast.97, bf16[512,2,128]{0,2,1:T(8,128)(2,1)S(1)} %bitcast.93, pred[512,512]{1,0:T(8,128)(4,1)} %copy-done.16), kind=kOutput, calls=%fused_computation.13 | convolution fusion | flops 135266304 | bytes 1835008 | tf_op jit(solution)/shard_map/thd,shd->hts/dot_general | solution.py:316
  38.1 1.0 fusion.16
  39.1 1.2 fusion.15
  40.3 1.8 %copy.62.refs_0_ = bf16[512,256]{1,0:T(8,128)(2,1)} copy(bf16[512,256]{0,1:T(8,128)(2,1)} %bitcast.101) | data formatting | bytes 524288 | tf_op jit(solution)/shard_map/reshape | solution.py:341
  42.0 1.8 %copy.63.refs_1_ = bf16[512,256]{1,0:T(8,128)(2,1)} copy(bf16[512,256]{0,1:T(8,128)(2,1)} %bitcast.100) | data formatting | bytes 524288 | tf_op jit(solution)/shard_map/reshape | solution.py:342
  43.8 2.3 %fusion.21 = bf16[2,128,512]{2,1,0:T(8,128)(2,1)} fusion(f32[2,128,512]{2,1,0:T(8,128)} %fusion.40, bf16[512,2,128]{0,2,1:T(8,128)(2,1)S(1)} %bitcast.86, bf16[2,512,512]{2,1,0:T(8,128)(2,1)S(1)} %select_convert_fusion, f32[512]{0:T(512)S(1)} %multiply_rsqrt_fusion), kind=kOutput, calls=%fused_computation.25 | convolution fusion | flops 134610944 | bytes 2099200 | tf_op jit(solution)/shard_map/hts,she->the/dot_general | solution.py:320
  46.1 1.0 fusion.17
  47.1 1.1 copy.64.refs_2_
  48.2 2.6 %fusion = f32[256,2048]{0,1:S(1)} fusion(bf16[512,256]{0,1:T(8,128)(2,1)S(1)} %bitcast.99, bf16[1,512,2048]{2,1,0:T(8,128)(2,1)} %param.11), kind=kOutput, calls=%fused_computation.1 | convolution fusion | flops 536870912 | bytes 4456448
  51.2 1.5 %copy.47 = f32[4,8,64,256]{3,2,1,0:T(8,128)} copy(f32[4,8,64,256]{3,2,0,1:T(8,128)S(1)} %multiply_bitcast_fusion.1) | data formatting | bytes 4194304 | tf_op jit(solution)/shard_map/mul | solution.py:352
  52.7 4.5 %multiply_bitcast_fusion = f32[2048,768]{0,1:T(8,128)} fusion(bf16[1,512,2048]{2,1,0:T(8,128)(2,1)S(1)} %copy-done, bf16[512,256]{1,0:T(8,128)(2,1)S(1)} %copy.64.refs_2_, bf16[512,256]{1,0:T(8,128)(2,1)S(1)} %copy-done.11, bf16[512,256]{1,0:T(8,128)(2,1)S(1)} %copy-done.10), kind=kOutput, calls=%fused_computation | convolution fusion | flops 1614544896 | bytes 9175040 | tf_op jit(solution)/shard_map/td,tk->dk/dot_general | solution.py:350
  57.2 54.2 %shard_map.102 = (f32[512,256]{1,0:T(8,128)}, f32[512,256]{1,0:T(8,128)}) custom-call(bf16[512,256]{1,0:T(8,128)(2,1)} %copy.62.refs_0_, bf16[512,256]{1,0:T(8,128)(2,1)} %copy.63.refs_1_, bf16[512,256]{1,0:T(8,128)(2,1)} %copy-done.12, bf16[2048,256]{1,0:T(8,128)(2,1)} %refs_3_, bf16[2048,256]{1,0:T(8,128)(2,1)} %refs_4_, bf16[2048,256]{1,0:T(8,128)(2,1)} %refs_5_, ...), custom_call_target="tpu_custom_call" | custom-call | flops 3145728 | bytes 12582912 | tf_op jit(solution)/shard_map/pallas_call | solution.py:176
  111.4 1.8 %convert_bitcast_fusion = bf16[1,512,256]{2,1,0:T(8,128)(2,1)} fusion(f32[512,256]{1,0:T(8,128)} %get-tuple-element.32), kind=kLoop, calls=%fused_computation.35 | loop fusion | flops 131072 | bytes 786432 | tf_op jit(solution)/shard_map/broadcast_in_dim | solution.py:363
  113.2 2.3 %copy.48 = f32[256,768]{1,0:T(8,128)} copy(f32[256,768]{0,1:T(8,128)} %reduce-scatter.2.cloned.1.call-done) | data formatting | bytes 1572864 | tf_op jit(solution)/shard_map/optimization_barrier | solution.py:364
  115.5 16.8 %shard_map.103 = (f32[64,768]{1,0:T(8,128)}, f32[64,256]{1,0:T(8,128)}) custom-call(f32[4,64,768]{2,1,0:T(8,128)} %bitcast.82, f32[8,64,256]{2,1,0:T(8,128)} %bitcast.103), custom_call_target="tpu_custom_call" | custom-call | flops 655360 | bytes 2621440 | tf_op jit(solution)/shard_map/pallas_call | solution.py:176
  132.3 1.6 %fusion.45 = (f32[64,256]{1,0:T(8,128)}, f32[64,256]{1,0:T(8,128)}, f32[64,256]{1,0:T(8,128)}) fusion(f32[64,768]{1,0:T(8,128)} %get-tuple-element.37), kind=kLoop, calls=%fused_computation.46 | loop fusion | bytes 393216 | tf_op jit(solution)/shard_map/slice | solution.py:374
  133.9 1.5 %copy.66 = f32[256,64]{0,1:T(8,128)} copy(f32[256,64]{0,1:T(8,128)} %bitcast.104) | data formatting | bytes 131072
  (47 shorter events, 6.2 us)
Async XLA Ops:
  7.2 1.7 %copy-start = (bf16[1,512,2048]{2,1,0:T(8,128)(2,1)S(1)}, bf16[1,512,2048]{2,1,0:T(8,128)(2,1)}, u32[]{:S(2)}) copy-start(bf16[1,512,2048]{2,1,0:T(8,128)(2,1)} %param.6) | copy-start | bytes 6291460
  7.2 106.0 %reduce-scatter.2.cloned.1.call-start = ((), (), s32[]{:S(2)}) async-start(), calls=%async_computation.1 | async-start | bytes 7077888 | tf_op jit(solution)/shard_map/reduce_scatter | solution.py:358
  7.3 28.5 %copy-start.16 = (pred[512,512]{1,0:T(8,128)(4,1)}, pred[512,512]{1,0:T(8,128)(4,1)S(1)}, u32[]{:S(2)}) copy-start(pred[512,512]{1,0:T(8,128)(4,1)S(1)} %iota_compare_fusion) | copy-start | bytes 786436
  7.3 3.5 %copy-start.13 = (bf16[2048,256]{1,0:T(8,128)(2,1)S(1)}, bf16[2048,256]{1,0:T(8,128)(2,1)}, u32[]{:S(2)}) copy-start(bf16[2048,256]{1,0:T(8,128)(2,1)} %refs_4_) | copy-start | bytes 3145732
  10.8 19.6 %copy-start.5 = (bf16[512,256]{0,1:T(8,128)(2,1)}, bf16[512,256]{0,1:T(8,128)(2,1)S(1)}, u32[]{:S(2)}) copy-start(bf16[512,256]{0,1:T(8,128)(2,1)S(1)} %fusion.28) | copy-start | bytes 786436
  10.9 1.3 copy-start.14
  12.2 21.4 %copy-start.3 = (bf16[512,256]{0,1:T(8,128)(2,1)}, bf16[512,256]{0,1:T(8,128)(2,1)S(1)}, u32[]{:S(2)}) copy-start(bf16[512,256]{0,1:T(8,128)(2,1)S(1)} %fusion.22) | copy-start | bytes 786436
  12.2 1.7 %copy-start.7 = (bf16[1,512,2048]{2,1,0:T(8,128)(2,1)S(1)}, bf16[1,512,2048]{2,1,0:T(8,128)(2,1)}, u32[]{:S(2)}) copy-start(bf16[1,512,2048]{2,1,0:T(8,128)(2,1)} %param.11) | copy-start | bytes 6291460
  12.2 1.9 %copy-start.17 = (bf16[256,2048]{1,0:T(8,128)(2,1)S(1)}, bf16[256,2048]{1,0:T(8,128)(2,1)}, u32[]{:S(2)}) copy-start(bf16[256,2048]{1,0:T(8,128)(2,1)} %param.10) | copy-start | bytes 3145732
  14.9 21.0 %copy-start.1 = (bf16[512,256]{0,1:T(8,128)(2,1)}, bf16[512,256]{0,1:T(8,128)(2,1)S(1)}, u32[]{:S(2)}) copy-start(bf16[512,256]{0,1:T(8,128)(2,1)S(1)} %fusion.18) | copy-start | bytes 786436
  30.4 5.2 %copy-start.15 = (f32[2,128,128]{2,1,0:T(8,128)S(1)}, f32[2,128,128]{2,1,0:T(8,128)}, u32[]{:S(2)}) copy-start(f32[2,128,128]{2,1,0:T(8,128)} %get-tuple-element.23) | copy-start | bytes 393220
  33.6 2.8 %copy-start.6 = (bf16[512,256]{0,1:T(8,128)(2,1)S(1)}, bf16[512,256]{0,1:T(8,128)(2,1)}, u32[]{:S(2)}) copy-start(bf16[512,256]{0,1:T(8,128)(2,1)} %copy-done.5) | copy-start | bytes 786436
  35.6 1.0 copy-start.4
  43.8 2.3 %copy-start.2 = (bf16[512,256]{0,1:T(8,128)(2,1)S(1)}, bf16[512,256]{0,1:T(8,128)(2,1)}, u32[]{:S(2)}) copy-start(bf16[512,256]{0,1:T(8,128)(2,1)} %copy-done.1) | copy-start | bytes 786436
  43.8 2.3 %copy-start.8 = (f32[2,128,512]{2,1,0:T(8,128)S(1)}, f32[2,128,512]{2,1,0:T(8,128)}, u32[]{:S(2)}) copy-start(f32[2,128,512]{2,1,0:T(8,128)} %fusion.36) | copy-start | bytes 1572868
  46.1 2.1 %copy-start.9 = (bf16[2,128,512]{2,1,0:T(8,128)(2,1)S(1)}, bf16[2,128,512]{2,1,0:T(8,128)(2,1)}, u32[]{:S(2)}) copy-start(bf16[2,128,512]{2,1,0:T(8,128)(2,1)} %fusion.21) | copy-start | bytes 786436
  48.2 4.4 %copy-start.12 = (bf16[512,256]{1,0:T(8,128)(2,1)}, bf16[512,256]{1,0:T(8,128)(2,1)S(1)}, u32[]{:S(2)}) copy-start(bf16[512,256]{1,0:T(8,128)(2,1)S(1)} %copy.64.refs_2_) | copy-start | bytes 786436
  51.1 1.5 %copy-start.10 = (bf16[512,256]{1,0:T(8,128)(2,1)S(1)}, bf16[512,256]{1,0:T(8,128)(2,1)}, u32[]{:S(2)}) copy-start(bf16[512,256]{1,0:T(8,128)(2,1)} %copy.62.refs_0_) | copy-start | bytes 786436
  51.1 1.5 %copy-start.11 = (bf16[512,256]{1,0:T(8,128)(2,1)S(1)}, bf16[512,256]{1,0:T(8,128)(2,1)}, u32[]{:S(2)}) copy-start(bf16[512,256]{1,0:T(8,128)(2,1)} %copy.63.refs_1_) | copy-start | bytes 786436
Sparse Core Ops, SparseCore 0:
  57.3 47.3 reduce-scatter.1

commit v16 on v14

--- a/solution.py
+++ b/solution.py
@@ -347,7 +347,7 @@
     summed, input_grad, out_shared = lax.optimization_barrier((summed, input_grad, out_shared))
     summed, out_summed = ring_scatter(
         [
-            (summed.reshape(shares, -1, summed.shape[1]), "dp", jnp.float32, 2, False),
+            (summed.reshape(shares, -1, summed.shape[1]), "dp", jnp.float32, 1, True),
             (out_shared.reshape(seqs, -1, width), "seq", jnp.float32, 1, True),
         ],
         1,

time: 136 us -> 136 us (level)
  the two profiles are of different devices: /device:TPU:8 before, /device:TPU:1 now
where the time goes in v16:
time: 136 us
  Pallas kernels  82 us (60%)
  matrix products  25 us (18%)
  between operations  14.3 us (11%)
  local copies, waits for them, and re-layouts  12.7 us (9%)
  other arithmetic  1.74 us (1%)
    pallas_call x2, Pallas kernels, ring_scatter(): pl.pallas_call(functools.partial(ring_scatter_kernel, jobs, produce), out...  66.6 us
    pallas_call x1, Pallas kernels, exchange_states(): pl.pallas_call(functools.partial(exchange_kernel, n, axis), out_shape=(ja...  15.4 us
    unnamed x29, local copies, waits for them, and re-layouts  6.79 us
    dot_general x1, matrix products, local(): jnp.einsum('td,tk->dk', in_rows, grads, preferred_element_type=jnp.float32)  4.48 us
    dot_general x3, matrix products, project(): jnp.dot(in_rows, weight, preferred_element_type=jnp.float32)  3.49 us
  transfers between devices with their start and end apart: 1, of which 0 were waited for; matrix products, arithmetic and copies ran while one was open for 1% of the time, Pallas kernels for 39%

profile of v16, /device:TPU:1, one launch (start us, length us, event | category | flops | bytes accessed | tf_op | source)
XLA Modules:
  0.0 135.8 jit_solution(2638537288031914587)
XLA Ops:
  8.0 0.8 copy-done
  8.9 2.0 %fusion.28 = bf16[512,256]{0,1:T(8,128)(2,1)S(1)} fusion(bf16[2048,256]{1,0:T(8,128)(2,1)} %refs_3_, bf16[1,512,2048]{2,1,0:T(8,128)(2,1)S(1)} %copy-done), kind=kOutput, calls=%fused_computation.28 | convolution fusion | flops 537001984 | bytes 3407872 | tf_op jit(solution)/shard_map/dot_general | solution.py:278
  13.0 0.8 copy-done.9
  14.8 0.9 fusion.47.qg_ref
  15.7 0.9 fusion.46.kv_ref
  16.6 15.4 %shard_map.101 = (f32[2,128,128]{2,1,0:T(8,128)}, f32[2,128,128]{2,1,0:T(8,128)}) custom-call(f32[2,128,128]{2,1,0:T(8,128)} %fusion.46.kv_ref, f32[2,128,128]{2,1,0:T(8,128)} %fusion.47.qg_ref), custom_call_target="tpu_custom_call" | custom-call | tf_op jit(solution)/shard_map/pallas_call | solution.py:252
  32.0 2.1 %fusion.40 = f32[2,128,512]{2,1,0:T(8,128)} fusion(bf16[512,2,128]{0,2,1:T(8,128)(2,1)} %bitcast.98, f32[2,128,128]{2,1,0:T(8,128)} %get-tuple-element.22), kind=kOutput, calls=%fused_computation.40 | convolution fusion | flops 33587200 | bytes 917504 | tf_op jit(solution)/shard_map/thd,hde->the/dot_general | solution.py:306
  34.1 1.1 fusion.42
  35.2 2.0 %fusion.36 = f32[2,128,512]{2,1,0:T(8,128)} fusion(bf16[512,2,128]{0,2,1:T(8,128)(2,1)S(1)} %bitcast.94, f32[2,128,128]{2,1,0:T(8,128)} %get-tuple-element.23), kind=kOutput, calls=%fused_computation.36 | convolution fusion | flops 33587200 | bytes 917504 | tf_op jit(solution)/shard_map/shd,hde->she/dot_general | solution.py:321
  38.0 1.5 %select_convert_fusion = bf16[2,512,512]{2,1,0:T(8,128)(2,1)} fusion(bf16[512,2,128]{0,2,1:T(8,128)(2,1)S(1)} %bitcast.99, bf16[512,2,128]{0,2,1:T(8,128)(2,1)S(1)} %bitcast.95, pred[512,512]{1,0:T(8,128)(4,1)S(1)} %copy-done.12), kind=kOutput, calls=%fused_computation.13 | convolution fusion | flops 135266304 | bytes 1835008 | tf_op jit(solution)/shard_map/thd,shd->hts/dot_general | solution.py:299
  39.6 1.0 fusion.16
  41.2 1.1 copy.63.refs_1_
  42.3 2.0 %fusion.21 = bf16[2,128,512]{2,1,0:T(8,128)(2,1)S(1)} fusion(f32[2,128,512]{2,1,0:T(8,128)} %fusion.40, bf16[512,2,128]{0,2,1:T(8,128)(2,1)S(1)} %bitcast.88, bf16[2,512,512]{2,1,0:T(8,128)(2,1)} %select_convert_fusion, f32[512]{0:T(512)S(1)} %multiply_rsqrt_fusion), kind=kOutput, calls=%fused_computation.25 | convolution fusion | flops 134610944 | bytes 2099200 | tf_op jit(solution)/shard_map/hts,she->the/dot_general | solution.py:303
  44.3 1.0 fusion.17
  45.3 1.1 copy.64.refs_2_
  46.4 2.5 %fusion = f32[256,2048]{0,1:S(1)} fusion(bf16[512,256]{0,1:T(8,128)(2,1)S(1)} %bitcast.101, bf16[1,512,2048]{2,1,0:T(8,128)(2,1)} %param.11), kind=kOutput, calls=%fused_computation.1 | convolution fusion | flops 536870912 | bytes 4456448
  49.2 1.5 %copy.47 = f32[4,8,64,256]{3,2,1,0:T(8,128)} copy(f32[4,8,64,256]{3,2,0,1:T(8,128)S(1)} %multiply_bitcast_fusion.1) | data formatting | bytes 4194304 | tf_op jit(solution)/shard_map/mul | solution.py:335
  50.7 4.5 %multiply_bitcast_fusion = f32[2048,768]{0,1:T(8,128)} fusion(bf16[1,512,2048]{2,1,0:T(8,128)(2,1)S(1)} %copy-done, bf16[512,256]{1,0:T(8,128)(2,1)S(1)} %copy.64.refs_2_, bf16[512,256]{1,0:T(8,128)(2,1)S(1)} %copy.63.refs_1_, bf16[512,256]{1,0:T(8,128)(2,1)S(1)} %copy.62.refs_0_), kind=kOutput, calls=%fused_computation | convolution fusion | flops 1614544896 | bytes 9175040 | tf_op jit(solution)/shard_map/td,tk->dk/dot_general | solution.py:333
  55.2 1.2 copy-done.2
  56.4 1.2 copy-done.4
  57.6 1.2 copy-done.5
  58.9 52.4 %shard_map.102 = (f32[512,256]{1,0:T(8,128)S(1)}, f32[512,256]{1,0:T(8,128)S(1)}) custom-call(bf16[512,256]{1,0:T(8,128)(2,1)S(1)} %copy.62.refs_0_, bf16[512,256]{1,0:T(8,128)(2,1)S(1)} %copy.63.refs_1_, bf16[512,256]{1,0:T(8,128)(2,1)S(1)} %copy.64.refs_2_, bf16[2048,256]{1,0:T(8,128)(2,1)S(1)} %copy-done.5, bf16[2048,256]{1,0:T(8,128)(2,1)S(1)} %copy-done.2, ...), custom_call_target="tpu_custom_call" | custom-call | flops 3145728 | bytes 12582912 | tf_op jit(solution)/shard_map/pallas_call | solution.py:159
  112.1 1.4 %copy.48 = f32[256,768]{1,0:T(8,128)S(1)} copy(f32[256,768]{0,1:T(8,128)} %reduce-scatter.2.cloned.1.call-done) | data formatting | bytes 1572864 | tf_op jit(solution)/shard_map/optimization_barrier | solution.py:347
  113.5 14.2 %shard_map.103 = (f32[64,768]{1,0:T(8,128)S(1)}, f32[64,256]{1,0:T(8,128)S(1)}) custom-call(f32[4,64,768]{2,1,0:T(8,128)S(1)} %bitcast.80, f32[8,64,256]{2,1,0:T(8,128)S(1)} %bitcast.81), custom_call_target="tpu_custom_call" | custom-call | flops 655360 | bytes 2621440 | tf_op jit(solution)/shard_map/pallas_call | solution.py:159
  (39 shorter events, 7.6 us)
Async XLA Ops:
  7.2 1.7 %copy-start = (bf16[1,512,2048]{2,1,0:T(8,128)(2,1)S(1)}, bf16[1,512,2048]{2,1,0:T(8,128)(2,1)}, u32[]{:S(2)}) copy-start(bf16[1,512,2048]{2,1,0:T(8,128)(2,1)} %param.6) | copy-start | bytes 6291460
  7.2 3.7 %copy-start.1 = (bf16[2048,256]{1,0:T(8,128)(2,1)S(1)}, bf16[2048,256]{1,0:T(8,128)(2,1)}, u32[]{:S(2)}) copy-start(bf16[2048,256]{1,0:T(8,128)(2,1)} %refs_4_) | copy-start | bytes 3145732
  7.2 104.9 %reduce-scatter.2.cloned.1.call-start = ((), (), s32[]{:S(2)}) async-start(), calls=%async_computation.1 | async-start | bytes 7077888 | tf_op jit(solution)/shard_map/reduce_scatter | solution.py:341
  10.8 3.9 %copy-start.7 = (bf16[512,256]{0,1:T(8,128)(2,1)}, bf16[512,256]{0,1:T(8,128)(2,1)S(1)}, u32[]{:S(2)}) copy-start(bf16[512,256]{0,1:T(8,128)(2,1)S(1)} %fusion.28) | copy-start | bytes 786436
  10.9 1.3 copy-start.3
  12.2 1.6 %copy-start.9 = (bf16[1,512,2048]{2,1,0:T(8,128)(2,1)S(1)}, bf16[1,512,2048]{2,1,0:T(8,128)(2,1)}, u32[]{:S(2)}) copy-start(bf16[1,512,2048]{2,1,0:T(8,128)(2,1)} %param.11) | copy-start | bytes 6291460
  12.2 1.9 %copy-start.13 = (bf16[256,2048]{1,0:T(8,128)(2,1)S(1)}, bf16[256,2048]{1,0:T(8,128)(2,1)}, u32[]{:S(2)}) copy-start(bf16[256,2048]{1,0:T(8,128)(2,1)} %param.10) | copy-start | bytes 3145732
  16.6 20.9 %copy-start.12 = (pred[512,512]{1,0:T(8,128)(4,1)S(1)}, pred[512,512]{1,0:T(8,128)(4,1)}, u32[]{:S(2)}) copy-start(pred[512,512]{1,0:T(8,128)(4,1)} %iota_compare_fusion) | copy-start | bytes 786436
  32.0 5.3 %copy-start.11 = (f32[2,128,128]{2,1,0:T(8,128)S(1)}, f32[2,128,128]{2,1,0:T(8,128)}, u32[]{:S(2)}) copy-start(f32[2,128,128]{2,1,0:T(8,128)} %get-tuple-element.23) | copy-start | bytes 393220
  35.2 2.8 %copy-start.8 = (bf16[512,256]{0,1:T(8,128)(2,1)S(1)}, bf16[512,256]{0,1:T(8,128)(2,1)}, u32[]{:S(2)}) copy-start(bf16[512,256]{0,1:T(8,128)(2,1)} %copy-done.7) | copy-start | bytes 786436
  42.3 2.0 %copy-start.6 = (bf16[2,512,512]{2,1,0:T(8,128)(2,1)S(1)}, bf16[2,512,512]{2,1,0:T(8,128)(2,1)}, u32[]{:S(2)}) copy-start(bf16[2,512,512]{2,1,0:T(8,128)(2,1)} %select_convert_fusion) | copy-start | bytes 3145732
  42.3 2.0 %copy-start.10 = (f32[2,128,512]{2,1,0:T(8,128)S(1)}, f32[2,128,512]{2,1,0:T(8,128)}, u32[]{:S(2)}) copy-start(f32[2,128,512]{2,1,0:T(8,128)} %fusion.36) | copy-start | bytes 1572868
  55.2 1.2 copy-start.2
  56.4 1.2 copy-start.4
  57.6 1.2 copy-start.5
Sparse Core Ops, SparseCore 0:
  55.3 46.0 reduce-scatter.1

commit v17 on v14

--- a/solution.py
+++ b/solution.py
@@ -340,7 +340,7 @@
     term_qkv, factors, term_out = lax.optimization_barrier((term_qkv, factors, term_out))
     summed = lax.psum_scatter(term_qkv, "seq", scatter_dimension=0, tiled=True)
     input_grad, out_shared = ring_scatter(
-        [(head_terms, "head", jnp.float32, 4, False), (term_out, "dp", jnp.float32, 2, False)], 0,
+        [(head_terms, "head", jnp.float32, 8, False), (term_out, "dp", jnp.float32, 2, False)], 0,
         factors,
     )
     input_grad = input_grad.astype(jnp.bfloat16)[None]

time: 136 us -> 137 us (level)
  no operation moved by 1% of the time
where the time goes in v17:
time: 137 us; the launch traced here: 136 us
  Pallas kernels  82.6 us (60%)
  matrix products  25 us (18%)
  between operations  14.3 us (10%)
  local copies, waits for them, and re-layouts  12.7 us (9%)
  other arithmetic  1.74 us (1%)
    pallas_call x2, Pallas kernels, ring_scatter(): pl.pallas_call(functools.partial(ring_scatter_kernel, jobs, produce), out...  68.7 us
    pallas_call x1, Pallas kernels, exchange_states(): pl.pallas_call(functools.partial(exchange_kernel, n, axis), out_shape=(ja...  13.8 us
    unnamed x29, local copies, waits for them, and re-layouts  6.79 us
    dot_general x1, matrix products, local(): jnp.einsum('td,tk->dk', in_rows, grads, preferred_element_type=jnp.float32)  4.48 us
    dot_general x3, matrix products, project(): jnp.dot(in_rows, weight, preferred_element_type=jnp.float32)  3.5 us
  transfers between devices with their start and end apart: 1, of which 0 were waited for; matrix products, arithmetic and copies ran while one was open for 1% of the time, Pallas kernels for 39%

profile of v17, /device:TPU:8, one launch (start us, length us, event | category | flops | bytes accessed | tf_op | source)
XLA Modules:
  0.0 136.4 jit_solution(17218069472254656405)
XLA Ops:
  8.0 0.8 copy-done
  8.9 2.0 %fusion.28 = bf16[512,256]{0,1:T(8,128)(2,1)S(1)} fusion(bf16[2048,256]{1,0:T(8,128)(2,1)} %refs_3_, bf16[1,512,2048]{2,1,0:T(8,128)(2,1)S(1)} %copy-done), kind=kOutput, calls=%fused_computation.28 | convolution fusion | flops 537001984 | bytes 3407872 | tf_op jit(solution)/shard_map/dot_general | solution.py:278
  13.0 0.8 copy-done.9
  14.8 0.9 fusion.47.qg_ref
  15.7 0.9 fusion.46.kv_ref
  16.6 13.8 %shard_map.101 = (f32[2,128,128]{2,1,0:T(8,128)}, f32[2,128,128]{2,1,0:T(8,128)}) custom-call(f32[2,128,128]{2,1,0:T(8,128)} %fusion.46.kv_ref, f32[2,128,128]{2,1,0:T(8,128)} %fusion.47.qg_ref), custom_call_target="tpu_custom_call" | custom-call | tf_op jit(solution)/shard_map/pallas_call | solution.py:252
  30.4 2.1 %fusion.40 = f32[2,128,512]{2,1,0:T(8,128)} fusion(bf16[512,2,128]{0,2,1:T(8,128)(2,1)} %bitcast.98, f32[2,128,128]{2,1,0:T(8,128)} %get-tuple-element.22), kind=kOutput, calls=%fused_computation.40 | convolution fusion | flops 33587200 | bytes 917504 | tf_op jit(solution)/shard_map/thd,hde->the/dot_general | solution.py:306
  32.6 1.1 fusion.42
  33.7 2.0 %fusion.36 = f32[2,128,512]{2,1,0:T(8,128)} fusion(bf16[512,2,128]{0,2,1:T(8,128)(2,1)S(1)} %bitcast.94, f32[2,128,128]{2,1,0:T(8,128)} %get-tuple-element.23), kind=kOutput, calls=%fused_computation.36 | convolution fusion | flops 33587200 | bytes 917504 | tf_op jit(solution)/shard_map/shd,hde->she/dot_general | solution.py:321
  36.5 1.5 %select_convert_fusion = bf16[2,512,512]{2,1,0:T(8,128)(2,1)} fusion(bf16[512,2,128]{0,2,1:T(8,128)(2,1)S(1)} %bitcast.99, bf16[512,2,128]{0,2,1:T(8,128)(2,1)S(1)} %bitcast.95, pred[512,512]{1,0:T(8,128)(4,1)S(1)} %copy-done.12), kind=kOutput, calls=%fused_computation.13 | convolution fusion | flops 135266304 | bytes 1835008 | tf_op jit(solution)/shard_map/thd,shd->hts/dot_general | solution.py:299
  38.0 1.0 fusion.16
  39.7 1.1 copy.63.refs_1_
  40.8 2.0 %fusion.21 = bf16[2,128,512]{2,1,0:T(8,128)(2,1)S(1)} fusion(f32[2,128,512]{2,1,0:T(8,128)} %fusion.40, bf16[512,2,128]{0,2,1:T(8,128)(2,1)S(1)} %bitcast.88, bf16[2,512,512]{2,1,0:T(8,128)(2,1)} %select_convert_fusion, f32[512]{0:T(512)S(1)} %multiply_rsqrt_fusion), kind=kOutput, calls=%fused_computation.25 | convolution fusion | flops 134610944 | bytes 2099200 | tf_op jit(solution)/shard_map/hts,she->the/dot_general | solution.py:303
  42.7 1.0 fusion.17
  43.8 1.1 copy.64.refs_2_
  44.8 2.5 %fusion = f32[256,2048]{0,1:S(1)} fusion(bf16[512,256]{0,1:T(8,128)(2,1)S(1)} %bitcast.101, bf16[1,512,2048]{2,1,0:T(8,128)(2,1)} %param.11), kind=kOutput, calls=%fused_computation.1 | convolution fusion | flops 536870912 | bytes 4456448
  47.6 1.5 %copy.47 = f32[4,8,64,256]{3,2,1,0:T(8,128)} copy(f32[4,8,64,256]{3,2,0,1:T(8,128)S(1)} %multiply_bitcast_fusion.1) | data formatting | bytes 4194304 | tf_op jit(solution)/shard_map/mul | solution.py:335
  49.1 4.5 %multiply_bitcast_fusion = f32[2048,768]{0,1:T(8,128)} fusion(bf16[1,512,2048]{2,1,0:T(8,128)(2,1)S(1)} %copy-done, bf16[512,256]{1,0:T(8,128)(2,1)S(1)} %copy.64.refs_2_, bf16[512,256]{1,0:T(8,128)(2,1)S(1)} %copy.63.refs_1_, bf16[512,256]{1,0:T(8,128)(2,1)S(1)} %copy.62.refs_0_), kind=kOutput, calls=%fused_computation | convolution fusion | flops 1614544896 | bytes 9175040 | tf_op jit(solution)/shard_map/td,tk->dk/dot_general | solution.py:333
  53.7 1.2 copy-done.2
  54.9 1.2 copy-done.4
  56.1 1.2 copy-done.5
  57.3 53.4 %shard_map.102 = (f32[512,256]{1,0:T(8,128)S(1)}, f32[512,256]{1,0:T(8,128)S(1)}) custom-call(bf16[512,256]{1,0:T(8,128)(2,1)S(1)} %copy.62.refs_0_, bf16[512,256]{1,0:T(8,128)(2,1)S(1)} %copy.63.refs_1_, bf16[512,256]{1,0:T(8,128)(2,1)S(1)} %copy.64.refs_2_, bf16[2048,256]{1,0:T(8,128)(2,1)S(1)} %copy-done.5, bf16[2048,256]{1,0:T(8,128)(2,1)S(1)} %copy-done.2, ...), custom_call_target="tpu_custom_call" | custom-call | flops 3145728 | bytes 12582912 | tf_op jit(solution)/shard_map/pallas_call | solution.py:159
  111.4 1.4 %copy.48 = f32[256,768]{1,0:T(8,128)S(1)} copy(f32[256,768]{0,1:T(8,128)} %reduce-scatter.2.cloned.1.call-done) | data formatting | bytes 1572864 | tf_op jit(solution)/shard_map/optimization_barrier | solution.py:347
  112.8 15.4 %shard_map.103 = (f32[64,768]{1,0:T(8,128)S(1)}, f32[64,256]{1,0:T(8,128)S(1)}) custom-call(f32[4,64,768]{2,1,0:T(8,128)S(1)} %bitcast.80, f32[8,64,256]{2,1,0:T(8,128)S(1)} %bitcast.81), custom_call_target="tpu_custom_call" | custom-call | flops 655360 | bytes 2621440 | tf_op jit(solution)/shard_map/pallas_call | solution.py:159
  (39 shorter events, 7.6 us)
Async XLA Ops:
  7.2 1.7 %copy-start = (bf16[1,512,2048]{2,1,0:T(8,128)(2,1)S(1)}, bf16[1,512,2048]{2,1,0:T(8,128)(2,1)}, u32[]{:S(2)}) copy-start(bf16[1,512,2048]{2,1,0:T(8,128)(2,1)} %param.6) | copy-start | bytes 6291460
  7.2 3.7 %copy-start.1 = (bf16[2048,256]{1,0:T(8,128)(2,1)S(1)}, bf16[2048,256]{1,0:T(8,128)(2,1)}, u32[]{:S(2)}) copy-start(bf16[2048,256]{1,0:T(8,128)(2,1)} %refs_4_) | copy-start | bytes 3145732
  7.2 104.2 %reduce-scatter.2.cloned.1.call-start = ((), (), s32[]{:S(2)}) async-start(), calls=%async_computation.1 | async-start | bytes 7077888 | tf_op jit(solution)/shard_map/reduce_scatter | solution.py:341
  10.8 3.9 %copy-start.7 = (bf16[512,256]{0,1:T(8,128)(2,1)}, bf16[512,256]{0,1:T(8,128)(2,1)S(1)}, u32[]{:S(2)}) copy-start(bf16[512,256]{0,1:T(8,128)(2,1)S(1)} %fusion.28) | copy-start | bytes 786436
  10.9 1.3 copy-start.3
  12.2 1.6 %copy-start.9 = (bf16[1,512,2048]{2,1,0:T(8,128)(2,1)S(1)}, bf16[1,512,2048]{2,1,0:T(8,128)(2,1)}, u32[]{:S(2)}) copy-start(bf16[1,512,2048]{2,1,0:T(8,128)(2,1)} %param.11) | copy-start | bytes 6291460
  12.2 1.9 %copy-start.13 = (bf16[256,2048]{1,0:T(8,128)(2,1)S(1)}, bf16[256,2048]{1,0:T(8,128)(2,1)}, u32[]{:S(2)}) copy-start(bf16[256,2048]{1,0:T(8,128)(2,1)} %param.10) | copy-start | bytes 3145732
  16.6 19.4 %copy-start.12 = (pred[512,512]{1,0:T(8,128)(4,1)S(1)}, pred[512,512]{1,0:T(8,128)(4,1)}, u32[]{:S(2)}) copy-start(pred[512,512]{1,0:T(8,128)(4,1)} %iota_compare_fusion) | copy-start | bytes 786436
  30.4 5.3 %copy-start.11 = (f32[2,128,128]{2,1,0:T(8,128)S(1)}, f32[2,128,128]{2,1,0:T(8,128)}, u32[]{:S(2)}) copy-start(f32[2,128,128]{2,1,0:T(8,128)} %get-tuple-element.23) | copy-start | bytes 393220
  33.7 2.8 %copy-start.8 = (bf16[512,256]{0,1:T(8,128)(2,1)S(1)}, bf16[512,256]{0,1:T(8,128)(2,1)}, u32[]{:S(2)}) copy-start(bf16[512,256]{0,1:T(8,128)(2,1)} %copy-done.7) | copy-start | bytes 786436
  40.7 2.0 %copy-start.6 = (bf16[2,512,512]{2,1,0:T(8,128)(2,1)S(1)}, bf16[2,512,512]{2,1,0:T(8,128)(2,1)}, u32[]{:S(2)}) copy-start(bf16[2,512,512]{2,1,0:T(8,128)(2,1)} %select_convert_fusion) | copy-start | bytes 3145732
  40.8 2.0 %copy-start.10 = (f32[2,128,512]{2,1,0:T(8,128)S(1)}, f32[2,128,512]{2,1,0:T(8,128)}, u32[]{:S(2)}) copy-start(f32[2,128,512]{2,1,0:T(8,128)} %fusion.36) | copy-start | bytes 1572868
  53.6 1.2 copy-start.2
  54.9 1.2 copy-start.4
  56.1 1.2 copy-start.5
Sparse Core Ops, SparseCore 0:
  53.8 47.3 reduce-scatter.1

commit v18 on v14

--- a/solution.py
+++ b/solution.py
@@ -20,17 +20,6 @@
         terms = (made,) + refs[:count - 1]
         outs, scratch = refs[count - 1:2 * count - 1], refs[2 * count - 1:]
         grads, weights = factors[:produce], factors[produce:]
-        block_rows = made.shape[2]
-        for block in range(made.shape[0]):
-            rows = pl.ds(block * block_rows, block_rows)
-            total = None
-            for grad, weight in zip(grads, weights):
-                part = lax.dot_general(
-                    grad[...], weight[rows, :], (((1,), (1,)), ((), ())),
-                    preferred_element_type=jnp.float32,
-                )
-                total = part if total is None else total + part
-            made[block] = total
     else:
         terms, outs, scratch = refs[:count], refs[count:2 * count], refs[2 * count:]
     barrier = pltpu.get_barrier_semaphore()
@@ -47,6 +36,18 @@
         greeted += len(offsets)
     pl.semaphore_wait(barrier, greeted)
 
+    def make_block(block):
+        block_rows = made.shape[2]
+        rows = pl.ds(pl.multiple_of(block * block_rows, block_rows), block_rows)
+        total = None
+        for grad, weight in zip(grads, weights):
+            part = lax.dot_general(
+                grad[...], weight[rows, :], (((1,), (1,)), ((), ())),
+                preferred_element_type=jnp.float32,
+            )
+            total = part if total is None else total + part
+        made[block] = total
+
     def direct_copy(job, offset):
         axis, n, _, _ = jobs[job]
         me = places[job][0]
@@ -72,6 +73,10 @@
             if direct or step >= n - 1:
                 continue
             me, right, left = places[job]
+            if produce and job == 0 and 2 * (step + 1) <= n:
+                make_block(lax.rem(me + n - (step + 1), n))
+                if 2 * (step + 1) != n:
+                    make_block(lax.rem(me + step + 1, n))
             recv, sendbuf, send_sem, recv_sem = scratch[4 * job:4 * job + 4]
             term_ref = terms[job]
             rows, half = outs[job].shape[0] // pieces, outs[job].shape[1] // 2
@@ -114,6 +119,8 @@
                     ).wait_recv()
                     outs[job][...] += recv[sender]
             continue
+        if produce and job == 0:
+            make_block(me)
         rows, half = outs[job].shape[0] // pieces, outs[job].shape[1] // 2
         for slot in range(2 * pieces):
             piece, way = divmod(slot, 2)

time: 136 us -> 135 us (level)
  transfers between devices with their start and end apart: 1 -> 1, of which waited for: 0 -> 0; matrix products, arithmetic and copies ran while one was open for 1% -> 1% of each run, Pallas kernels for 39% -> 38%
where the time goes in v18:
time: 135 us; the launch traced here: 134 us
  Pallas kernels  80.2 us (59%)
  matrix products  25 us (19%)
  between operations  14.3 us (11%)
  local copies, waits for them, and re-layouts  12.7 us (9%)
  other arithmetic  1.74 us (1%)
    pallas_call x2, Pallas kernels, ring_scatter(): pl.pallas_call(functools.partial(ring_scatter_kernel, jobs, produce), out...  66.4 us
    pallas_call x1, Pallas kernels, exchange_states(): pl.pallas_call(functools.partial(exchange_kernel, n, axis), out_shape=(ja...  13.8 us
    unnamed x29, local copies, waits for them, and re-layouts  6.79 us
    dot_general x1, matrix products, local(): jnp.einsum('td,tk->dk', in_rows, grads, preferred_element_type=jnp.float32)  4.48 us
    dot_general x3, matrix products, project(): jnp.dot(in_rows, weight, preferred_element_type=jnp.float32)  3.5 us
  transfers between devices with their start and end apart: 1, of which 0 were waited for; matrix products, arithmetic and copies ran while one was open for 1% of the time, Pallas kernels for 38%

profile of v18, /device:TPU:8, one launch (start us, length us, event | category | flops | bytes accessed | tf_op | source)
XLA Modules:
  0.0 134.0 jit_solution(16962700752436225021)
XLA Ops:
  8.0 0.8 copy-done
  8.9 2.0 %fusion.28 = bf16[512,256]{0,1:T(8,128)(2,1)S(1)} fusion(bf16[2048,256]{1,0:T(8,128)(2,1)} %refs_3_, bf16[1,512,2048]{2,1,0:T(8,128)(2,1)S(1)} %copy-done), kind=kOutput, calls=%fused_computation.28 | convolution fusion | flops 537001984 | bytes 3407872 | tf_op jit(solution)/shard_map/dot_general | solution.py:285
  13.0 0.8 copy-done.9
  14.8 0.9 fusion.47.qg_ref
  15.7 0.9 fusion.46.kv_ref
  16.6 13.8 %shard_map.101 = (f32[2,128,128]{2,1,0:T(8,128)}, f32[2,128,128]{2,1,0:T(8,128)}) custom-call(f32[2,128,128]{2,1,0:T(8,128)} %fusion.46.kv_ref, f32[2,128,128]{2,1,0:T(8,128)} %fusion.47.qg_ref), custom_call_target="tpu_custom_call" | custom-call | tf_op jit(solution)/shard_map/pallas_call | solution.py:259
  30.4 2.1 %fusion.40 = f32[2,128,512]{2,1,0:T(8,128)} fusion(bf16[512,2,128]{0,2,1:T(8,128)(2,1)} %bitcast.98, f32[2,128,128]{2,1,0:T(8,128)} %get-tuple-element.22), kind=kOutput, calls=%fused_computation.40 | convolution fusion | flops 33587200 | bytes 917504 | tf_op jit(solution)/shard_map/thd,hde->the/dot_general | solution.py:313
  32.6 1.1 fusion.42
  33.7 2.0 %fusion.36 = f32[2,128,512]{2,1,0:T(8,128)} fusion(bf16[512,2,128]{0,2,1:T(8,128)(2,1)S(1)} %bitcast.94, f32[2,128,128]{2,1,0:T(8,128)} %get-tuple-element.23), kind=kOutput, calls=%fused_computation.36 | convolution fusion | flops 33587200 | bytes 917504 | tf_op jit(solution)/shard_map/shd,hde->she/dot_general | solution.py:328
  36.5 1.5 %select_convert_fusion = bf16[2,512,512]{2,1,0:T(8,128)(2,1)} fusion(bf16[512,2,128]{0,2,1:T(8,128)(2,1)S(1)} %bitcast.99, bf16[512,2,128]{0,2,1:T(8,128)(2,1)S(1)} %bitcast.95, pred[512,512]{1,0:T(8,128)(4,1)S(1)} %copy-done.12), kind=kOutput, calls=%fused_computation.13 | convolution fusion | flops 135266304 | bytes 1835008 | tf_op jit(solution)/shard_map/thd,shd->hts/dot_general | solution.py:306
  38.0 1.0 fusion.16
  39.7 1.1 copy.63.refs_1_
  40.8 2.0 %fusion.21 = bf16[2,128,512]{2,1,0:T(8,128)(2,1)S(1)} fusion(f32[2,128,512]{2,1,0:T(8,128)} %fusion.40, bf16[512,2,128]{0,2,1:T(8,128)(2,1)S(1)} %bitcast.88, bf16[2,512,512]{2,1,0:T(8,128)(2,1)} %select_convert_fusion, f32[512]{0:T(512)S(1)} %multiply_rsqrt_fusion), kind=kOutput, calls=%fused_computation.25 | convolution fusion | flops 134610944 | bytes 2099200 | tf_op jit(solution)/shard_map/hts,she->the/dot_general | solution.py:310
  42.7 1.0 fusion.17
  43.8 1.1 copy.64.refs_2_
  44.8 2.5 %fusion = f32[256,2048]{0,1:S(1)} fusion(bf16[512,256]{0,1:T(8,128)(2,1)S(1)} %bitcast.101, bf16[1,512,2048]{2,1,0:T(8,128)(2,1)} %param.11), kind=kOutput, calls=%fused_computation.1 | convolution fusion | flops 536870912 | bytes 4456448
  47.6 1.5 %copy.47 = f32[4,8,64,256]{3,2,1,0:T(8,128)} copy(f32[4,8,64,256]{3,2,0,1:T(8,128)S(1)} %multiply_bitcast_fusion.1) | data formatting | bytes 4194304 | tf_op jit(solution)/shard_map/mul | solution.py:342
  49.1 4.5 %multiply_bitcast_fusion = f32[2048,768]{0,1:T(8,128)} fusion(bf16[1,512,2048]{2,1,0:T(8,128)(2,1)S(1)} %copy-done, bf16[512,256]{1,0:T(8,128)(2,1)S(1)} %copy.64.refs_2_, bf16[512,256]{1,0:T(8,128)(2,1)S(1)} %copy.63.refs_1_, bf16[512,256]{1,0:T(8,128)(2,1)S(1)} %copy.62.refs_0_), kind=kOutput, calls=%fused_computation | convolution fusion | flops 1614544896 | bytes 9175040 | tf_op jit(solution)/shard_map/td,tk->dk/dot_general | solution.py:340
  53.7 1.2 copy-done.2
  54.9 1.2 copy-done.4
  56.1 1.2 copy-done.5
  57.3 51.1 %shard_map.102 = (f32[512,256]{1,0:T(8,128)S(1)}, f32[512,256]{1,0:T(8,128)S(1)}) custom-call(bf16[512,256]{1,0:T(8,128)(2,1)S(1)} %copy.62.refs_0_, bf16[512,256]{1,0:T(8,128)(2,1)S(1)} %copy.63.refs_1_, bf16[512,256]{1,0:T(8,128)(2,1)S(1)} %copy.64.refs_2_, bf16[2048,256]{1,0:T(8,128)(2,1)S(1)} %copy-done.5, bf16[2048,256]{1,0:T(8,128)(2,1)S(1)} %copy-done.2, ...), custom_call_target="tpu_custom_call" | custom-call | flops 3145728 | bytes 12582912 | tf_op jit(solution)/shard_map/pallas_call | solution.py:166
  109.1 1.4 %copy.48 = f32[256,768]{1,0:T(8,128)S(1)} copy(f32[256,768]{0,1:T(8,128)} %reduce-scatter.2.cloned.1.call-done) | data formatting | bytes 1572864 | tf_op jit(solution)/shard_map/optimization_barrier | solution.py:354
  110.5 15.3 %shard_map.103 = (f32[64,768]{1,0:T(8,128)S(1)}, f32[64,256]{1,0:T(8,128)S(1)}) custom-call(f32[4,64,768]{2,1,0:T(8,128)S(1)} %bitcast.80, f32[8,64,256]{2,1,0:T(8,128)S(1)} %bitcast.81), custom_call_target="tpu_custom_call" | custom-call | flops 655360 | bytes 2621440 | tf_op jit(solution)/shard_map/pallas_call | solution.py:166
  (39 shorter events, 7.6 us)
Async XLA Ops:
  7.2 1.7 %copy-start = (bf16[1,512,2048]{2,1,0:T(8,128)(2,1)S(1)}, bf16[1,512,2048]{2,1,0:T(8,128)(2,1)}, u32[]{:S(2)}) copy-start(bf16[1,512,2048]{2,1,0:T(8,128)(2,1)} %param.6) | copy-start | bytes 6291460
  7.2 3.7 %copy-start.1 = (bf16[2048,256]{1,0:T(8,128)(2,1)S(1)}, bf16[2048,256]{1,0:T(8,128)(2,1)}, u32[]{:S(2)}) copy-start(bf16[2048,256]{1,0:T(8,128)(2,1)} %refs_4_) | copy-start | bytes 3145732
  7.2 101.9 %reduce-scatter.2.cloned.1.call-start = ((), (), s32[]{:S(2)}) async-start(), calls=%async_computation.1 | async-start | bytes 7077888 | tf_op jit(solution)/shard_map/reduce_scatter | solution.py:348
  10.8 3.9 %copy-start.7 = (bf16[512,256]{0,1:T(8,128)(2,1)}, bf16[512,256]{0,1:T(8,128)(2,1)S(1)}, u32[]{:S(2)}) copy-start(bf16[512,256]{0,1:T(8,128)(2,1)S(1)} %fusion.28) | copy-start | bytes 786436
  10.9 1.3 copy-start.3
  12.2 1.6 %copy-start.9 = (bf16[1,512,2048]{2,1,0:T(8,128)(2,1)S(1)}, bf16[1,512,2048]{2,1,0:T(8,128)(2,1)}, u32[]{:S(2)}) copy-start(bf16[1,512,2048]{2,1,0:T(8,128)(2,1)} %param.11) | copy-start | bytes 6291460
  12.2 1.9 %copy-start.13 = (bf16[256,2048]{1,0:T(8,128)(2,1)S(1)}, bf16[256,2048]{1,0:T(8,128)(2,1)}, u32[]{:S(2)}) copy-start(bf16[256,2048]{1,0:T(8,128)(2,1)} %param.10) | copy-start | bytes 3145732
  16.6 19.4 %copy-start.12 = (pred[512,512]{1,0:T(8,128)(4,1)S(1)}, pred[512,512]{1,0:T(8,128)(4,1)}, u32[]{:S(2)}) copy-start(pred[512,512]{1,0:T(8,128)(4,1)} %iota_compare_fusion) | copy-start | bytes 786436
  30.4 5.3 %copy-start.11 = (f32[2,128,128]{2,1,0:T(8,128)S(1)}, f32[2,128,128]{2,1,0:T(8,128)}, u32[]{:S(2)}) copy-start(f32[2,128,128]{2,1,0:T(8,128)} %get-tuple-element.23) | copy-start | bytes 393220
  33.7 2.8 %copy-start.8 = (bf16[512,256]{0,1:T(8,128)(2,1)S(1)}, bf16[512,256]{0,1:T(8,128)(2,1)}, u32[]{:S(2)}) copy-start(bf16[512,256]{0,1:T(8,128)(2,1)} %copy-done.7) | copy-start | bytes 786436
  40.7 2.0 %copy-start.6 = (bf16[2,512,512]{2,1,0:T(8,128)(2,1)S(1)}, bf16[2,512,512]{2,1,0:T(8,128)(2,1)}, u32[]{:S(2)}) copy-start(bf16[2,512,512]{2,1,0:T(8,128)(2,1)} %select_convert_fusion) | copy-start | bytes 3145732
  40.8 2.0 %copy-start.10 = (f32[2,128,512]{2,1,0:T(8,128)S(1)}, f32[2,128,512]{2,1,0:T(8,128)}, u32[]{:S(2)}) copy-start(f32[2,128,512]{2,1,0:T(8,128)} %fusion.36) | copy-start | bytes 1572868
  53.6 1.2 copy-start.2
  54.9 1.2 copy-start.4
  56.1 1.2 copy-start.5
Sparse Core Ops, SparseCore 0:
  53.8 47.3 reduce-scatter.1

commit v19 on v18

--- a/solution.py
+++ b/solution.py
@@ -34,7 +34,6 @@
                 barrier, inc=1, device_id={axis: lax.rem(me + offset, n)}, device_id_type=MESH
             )
         greeted += len(offsets)
-    pl.semaphore_wait(barrier, greeted)
 
     def make_block(block):
         block_rows = made.shape[2]
@@ -47,6 +46,12 @@
             )
             total = part if total is None else total + part
         made[block] = total
+
+    if produce:
+        me, n = places[0][0], jobs[0][1]
+        make_block(lax.rem(me + n - 1, n))
+        make_block(lax.rem(me + 1, n))
+    pl.semaphore_wait(barrier, greeted)
 
     def direct_copy(job, offset):
         axis, n, _, _ = jobs[job]
@@ -73,7 +78,7 @@
             if direct or step >= n - 1:
                 continue
             me, right, left = places[job]
-            if produce and job == 0 and 2 * (step + 1) <= n:
+            if produce and job == 0 and 0 < step and 2 * (step + 1) <= n:
                 make_block(lax.rem(me + n - (step + 1), n))
                 if 2 * (step + 1) != n:
                     make_block(lax.rem(me + step + 1, n))

time: 135 us -> 134 us (level)
  no operation moved by 1% of the time
where the time goes in v19:
time: 134 us; the launch traced here: 133 us
  Pallas kernels  79.6 us (59%)
  matrix products  25 us (19%)
  between operations  14.3 us (11%)
  local copies, waits for them, and re-layouts  12.7 us (9%)
  other arithmetic  1.74 us (1%)
    pallas_call x2, Pallas kernels, ring_scatter(): pl.pallas_call(functools.partial(ring_scatter_kernel, jobs, produce), out...  65.8 us
    pallas_call x1, Pallas kernels, exchange_states(): pl.pallas_call(functools.partial(exchange_kernel, n, axis), out_shape=(ja...  13.8 us
    unnamed x29, local copies, waits for them, and re-layouts  6.79 us
    dot_general x1, matrix products, local(): jnp.einsum('td,tk->dk', in_rows, grads, preferred_element_type=jnp.float32)  4.48 us
    dot_general x3, matrix products, project(): jnp.dot(in_rows, weight, preferred_element_type=jnp.float32)  3.5 us
  transfers between devices with their start and end apart: 1, of which 0 were waited for; matrix products, arithmetic and copies ran while one was open for 1% of the time, Pallas kernels for 38%

profile of v19, /device:TPU:8, one launch (start us, length us, event | category | flops | bytes accessed | tf_op | source)
XLA Modules:
  0.0 133.4 jit_solution(16538631310052975147)
XLA Ops:
  8.0 0.8 copy-done
  8.9 2.0 %fusion.28 = bf16[512,256]{0,1:T(8,128)(2,1)S(1)} fusion(bf16[2048,256]{1,0:T(8,128)(2,1)} %refs_3_, bf16[1,512,2048]{2,1,0:T(8,128)(2,1)S(1)} %copy-done), kind=kOutput, calls=%fused_computation.28 | convolution fusion | flops 537001984 | bytes 3407872 | tf_op jit(solution)/shard_map/dot_general | solution.py:290
  13.0 0.8 copy-done.9
  14.8 0.9 fusion.47.qg_ref
  15.7 0.9 fusion.46.kv_ref
  16.6 13.8 %shard_map.101 = (f32[2,128,128]{2,1,0:T(8,128)}, f32[2,128,128]{2,1,0:T(8,128)}) custom-call(f32[2,128,128]{2,1,0:T(8,128)} %fusion.46.kv_ref, f32[2,128,128]{2,1,0:T(8,128)} %fusion.47.qg_ref), custom_call_target="tpu_custom_call" | custom-call | tf_op jit(solution)/shard_map/pallas_call | solution.py:264
  30.4 2.1 %fusion.40 = f32[2,128,512]{2,1,0:T(8,128)} fusion(bf16[512,2,128]{0,2,1:T(8,128)(2,1)} %bitcast.98, f32[2,128,128]{2,1,0:T(8,128)} %get-tuple-element.22), kind=kOutput, calls=%fused_computation.40 | convolution fusion | flops 33587200 | bytes 917504 | tf_op jit(solution)/shard_map/thd,hde->the/dot_general | solution.py:318
  32.6 1.1 fusion.42
  33.7 2.0 %fusion.36 = f32[2,128,512]{2,1,0:T(8,128)} fusion(bf16[512,2,128]{0,2,1:T(8,128)(2,1)S(1)} %bitcast.94, f32[2,128,128]{2,1,0:T(8,128)} %get-tuple-element.23), kind=kOutput, calls=%fused_computation.36 | convolution fusion | flops 33587200 | bytes 917504 | tf_op jit(solution)/shard_map/shd,hde->she/dot_general | solution.py:333
  36.5 1.5 %select_convert_fusion = bf16[2,512,512]{2,1,0:T(8,128)(2,1)} fusion(bf16[512,2,128]{0,2,1:T(8,128)(2,1)S(1)} %bitcast.99, bf16[512,2,128]{0,2,1:T(8,128)(2,1)S(1)} %bitcast.95, pred[512,512]{1,0:T(8,128)(4,1)S(1)} %copy-done.12), kind=kOutput, calls=%fused_computation.13 | convolution fusion | flops 135266304 | bytes 1835008 | tf_op jit(solution)/shard_map/thd,shd->hts/dot_general | solution.py:311
  38.0 1.0 fusion.16
  39.7 1.1 copy.63.refs_1_
  40.8 2.0 %fusion.21 = bf16[2,128,512]{2,1,0:T(8,128)(2,1)S(1)} fusion(f32[2,128,512]{2,1,0:T(8,128)} %fusion.40, bf16[512,2,128]{0,2,1:T(8,128)(2,1)S(1)} %bitcast.88, bf16[2,512,512]{2,1,0:T(8,128)(2,1)} %select_convert_fusion, f32[512]{0:T(512)S(1)} %multiply_rsqrt_fusion), kind=kOutput, calls=%fused_computation.25 | convolution fusion | flops 134610944 | bytes 2099200 | tf_op jit(solution)/shard_map/hts,she->the/dot_general | solution.py:315
  42.7 1.0 fusion.17
  43.8 1.1 copy.64.refs_2_
  44.8 2.5 %fusion = f32[256,2048]{0,1:S(1)} fusion(bf16[512,256]{0,1:T(8,128)(2,1)S(1)} %bitcast.101, bf16[1,512,2048]{2,1,0:T(8,128)(2,1)} %param.11), kind=kOutput, calls=%fused_computation.1 | convolution fusion | flops 536870912 | bytes 4456448
  47.6 1.5 %copy.47 = f32[4,8,64,256]{3,2,1,0:T(8,128)} copy(f32[4,8,64,256]{3,2,0,1:T(8,128)S(1)} %multiply_bitcast_fusion.1) | data formatting | bytes 4194304 | tf_op jit(solution)/shard_map/mul | solution.py:347
  49.1 4.5 %multiply_bitcast_fusion = f32[2048,768]{0,1:T(8,128)} fusion(bf16[1,512,2048]{2,1,0:T(8,128)(2,1)S(1)} %copy-done, bf16[512,256]{1,0:T(8,128)(2,1)S(1)} %copy.64.refs_2_, bf16[512,256]{1,0:T(8,128)(2,1)S(1)} %copy.63.refs_1_, bf16[512,256]{1,0:T(8,128)(2,1)S(1)} %copy.62.refs_0_), kind=kOutput, calls=%fused_computation | convolution fusion | flops 1614544896 | bytes 9175040 | tf_op jit(solution)/shard_map/td,tk->dk/dot_general | solution.py:345
  53.7 1.2 copy-done.2
  54.9 1.2 copy-done.4
  56.1 1.2 copy-done.5
  57.3 50.4 %shard_map.102 = (f32[512,256]{1,0:T(8,128)S(1)}, f32[512,256]{1,0:T(8,128)S(1)}) custom-call(bf16[512,256]{1,0:T(8,128)(2,1)S(1)} %copy.62.refs_0_, bf16[512,256]{1,0:T(8,128)(2,1)S(1)} %copy.63.refs_1_, bf16[512,256]{1,0:T(8,128)(2,1)S(1)} %copy.64.refs_2_, bf16[2048,256]{1,0:T(8,128)(2,1)S(1)} %copy-done.5, bf16[2048,256]{1,0:T(8,128)(2,1)S(1)} %copy-done.2, ...), custom_call_target="tpu_custom_call" | custom-call | flops 3145728 | bytes 12582912 | tf_op jit(solution)/shard_map/pallas_call | solution.py:171
  108.5 1.4 %copy.48 = f32[256,768]{1,0:T(8,128)S(1)} copy(f32[256,768]{0,1:T(8,128)} %reduce-scatter.2.cloned.1.call-done) | data formatting | bytes 1572864 | tf_op jit(solution)/shard_map/optimization_barrier | solution.py:359
  109.9 15.3 %shard_map.103 = (f32[64,768]{1,0:T(8,128)S(1)}, f32[64,256]{1,0:T(8,128)S(1)}) custom-call(f32[4,64,768]{2,1,0:T(8,128)S(1)} %bitcast.80, f32[8,64,256]{2,1,0:T(8,128)S(1)} %bitcast.81), custom_call_target="tpu_custom_call" | custom-call | flops 655360 | bytes 2621440 | tf_op jit(solution)/shard_map/pallas_call | solution.py:171
  (39 shorter events, 7.6 us)
Async XLA Ops:
  7.2 1.7 %copy-start = (bf16[1,512,2048]{2,1,0:T(8,128)(2,1)S(1)}, bf16[1,512,2048]{2,1,0:T(8,128)(2,1)}, u32[]{:S(2)}) copy-start(bf16[1,512,2048]{2,1,0:T(8,128)(2,1)} %param.6) | copy-start | bytes 6291460
  7.2 3.7 %copy-start.1 = (bf16[2048,256]{1,0:T(8,128)(2,1)S(1)}, bf16[2048,256]{1,0:T(8,128)(2,1)}, u32[]{:S(2)}) copy-start(bf16[2048,256]{1,0:T(8,128)(2,1)} %refs_4_) | copy-start | bytes 3145732
  7.2 101.3 %reduce-scatter.2.cloned.1.call-start = ((), (), s32[]{:S(2)}) async-start(), calls=%async_computation.1 | async-start | bytes 7077888 | tf_op jit(solution)/shard_map/reduce_scatter | solution.py:353
  10.8 3.9 %copy-start.7 = (bf16[512,256]{0,1:T(8,128)(2,1)}, bf16[512,256]{0,1:T(8,128)(2,1)S(1)}, u32[]{:S(2)}) copy-start(bf16[512,256]{0,1:T(8,128)(2,1)S(1)} %fusion.28) | copy-start | bytes 786436
  10.9 1.3 copy-start.3
  12.2 1.6 %copy-start.9 = (bf16[1,512,2048]{2,1,0:T(8,128)(2,1)S(1)}, bf16[1,512,2048]{2,1,0:T(8,128)(2,1)}, u32[]{:S(2)}) copy-start(bf16[1,512,2048]{2,1,0:T(8,128)(2,1)} %param.11) | copy-start | bytes 6291460
  12.2 1.9 %copy-start.13 = (bf16[256,2048]{1,0:T(8,128)(2,1)S(1)}, bf16[256,2048]{1,0:T(8,128)(2,1)}, u32[]{:S(2)}) copy-start(bf16[256,2048]{1,0:T(8,128)(2,1)} %param.10) | copy-start | bytes 3145732
  16.6 19.4 %copy-start.12 = (pred[512,512]{1,0:T(8,128)(4,1)S(1)}, pred[512,512]{1,0:T(8,128)(4,1)}, u32[]{:S(2)}) copy-start(pred[512,512]{1,0:T(8,128)(4,1)} %iota_compare_fusion) | copy-start | bytes 786436
  30.4 5.3 %copy-start.11 = (f32[2,128,128]{2,1,0:T(8,128)S(1)}, f32[2,128,128]{2,1,0:T(8,128)}, u32[]{:S(2)}) copy-start(f32[2,128,128]{2,1,0:T(8,128)} %get-tuple-element.23) | copy-start | bytes 393220
  33.7 2.8 %copy-start.8 = (bf16[512,256]{0,1:T(8,128)(2,1)S(1)}, bf16[512,256]{0,1:T(8,128)(2,1)}, u32[]{:S(2)}) copy-start(bf16[512,256]{0,1:T(8,128)(2,1)} %copy-done.7) | copy-start | bytes 786436
  40.7 2.0 %copy-start.6 = (bf16[2,512,512]{2,1,0:T(8,128)(2,1)S(1)}, bf16[2,512,512]{2,1,0:T(8,128)(2,1)}, u32[]{:S(2)}) copy-start(bf16[2,512,512]{2,1,0:T(8,128)(2,1)} %select_convert_fusion) | copy-start | bytes 3145732
  40.8 2.0 %copy-start.10 = (f32[2,128,512]{2,1,0:T(8,128)S(1)}, f32[2,128,512]{2,1,0:T(8,128)}, u32[]{:S(2)}) copy-start(f32[2,128,512]{2,1,0:T(8,128)} %fusion.36) | copy-start | bytes 1572868
  53.6 1.2 copy-start.2
  54.9 1.2 copy-start.4
  56.1 1.2 copy-start.5
Sparse Core Ops, SparseCore 0:
  53.8 47.3 reduce-scatter.1

commit v20 on v19

--- a/solution.py
+++ b/solution.py
@@ -359,7 +359,7 @@
     summed, input_grad, out_shared = lax.optimization_barrier((summed, input_grad, out_shared))
     summed, out_summed = ring_scatter(
         [
-            (summed.reshape(shares, -1, summed.shape[1]), "dp", jnp.float32, 2, False),
+            (summed.reshape(shares, -1, summed.shape[1]), "dp", jnp.float32, 1, False),
             (out_shared.reshape(seqs, -1, width), "seq", jnp.float32, 1, True),
         ],
         1,

time: 134 us -> 134 us (level)
  no operation moved by 1% of the time
where the time goes in v20:
time: 134 us
  Pallas kernels  80.1 us (60%)
  matrix products  25 us (19%)
  between operations  14.3 us (11%)
  local copies, waits for them, and re-layouts  12.7 us (9%)
  other arithmetic  1.74 us (1%)
    pallas_call x2, Pallas kernels, ring_scatter(): pl.pallas_call(functools.partial(ring_scatter_kernel, jobs, produce), out...  66.2 us
    pallas_call x1, Pallas kernels, exchange_states(): pl.pallas_call(functools.partial(exchange_kernel, n, axis), out_shape=(ja...  13.8 us
    unnamed x29, local copies, waits for them, and re-layouts  6.79 us
    dot_general x1, matrix products, local(): jnp.einsum('td,tk->dk', in_rows, grads, preferred_element_type=jnp.float32)  4.48 us
    dot_general x3, matrix products, project(): jnp.dot(in_rows, weight, preferred_element_type=jnp.float32)  3.5 us
  transfers between devices with their start and end apart: 1, of which 0 were waited for; matrix products, arithmetic and copies ran while one was open for 1% of the time, Pallas kernels for 38%

profile of v20, /device:TPU:8, one launch (start us, length us, event | category | flops | bytes accessed | tf_op | source)
XLA Modules:
  0.0 133.9 jit_solution(14142708749967539218)
XLA Ops:
  8.0 0.8 copy-done
  8.9 2.0 %fusion.28 = bf16[512,256]{0,1:T(8,128)(2,1)S(1)} fusion(bf16[2048,256]{1,0:T(8,128)(2,1)} %refs_3_, bf16[1,512,2048]{2,1,0:T(8,128)(2,1)S(1)} %copy-done), kind=kOutput, calls=%fused_computation.28 | convolution fusion | flops 537001984 | bytes 3407872 | tf_op jit(solution)/shard_map/dot_general | solution.py:290
  13.0 0.8 copy-done.9
  14.8 0.9 fusion.47.qg_ref
  15.7 0.9 fusion.46.kv_ref
  16.6 13.8 %shard_map.101 = (f32[2,128,128]{2,1,0:T(8,128)}, f32[2,128,128]{2,1,0:T(8,128)}) custom-call(f32[2,128,128]{2,1,0:T(8,128)} %fusion.46.kv_ref, f32[2,128,128]{2,1,0:T(8,128)} %fusion.47.qg_ref), custom_call_target="tpu_custom_call" | custom-call | tf_op jit(solution)/shard_map/pallas_call | solution.py:264
  30.4 2.1 %fusion.40 = f32[2,128,512]{2,1,0:T(8,128)} fusion(bf16[512,2,128]{0,2,1:T(8,128)(2,1)} %bitcast.98, f32[2,128,128]{2,1,0:T(8,128)} %get-tuple-element.22), kind=kOutput, calls=%fused_computation.40 | convolution fusion | flops 33587200 | bytes 917504 | tf_op jit(solution)/shard_map/thd,hde->the/dot_general | solution.py:318
  32.6 1.1 fusion.42
  33.7 2.0 %fusion.36 = f32[2,128,512]{2,1,0:T(8,128)} fusion(bf16[512,2,128]{0,2,1:T(8,128)(2,1)S(1)} %bitcast.94, f32[2,128,128]{2,1,0:T(8,128)} %get-tuple-element.23), kind=kOutput, calls=%fused_computation.36 | convolution fusion | flops 33587200 | bytes 917504 | tf_op jit(solution)/shard_map/shd,hde->she/dot_general | solution.py:333
  36.5 1.5 %select_convert_fusion = bf16[2,512,512]{2,1,0:T(8,128)(2,1)} fusion(bf16[512,2,128]{0,2,1:T(8,128)(2,1)S(1)} %bitcast.99, bf16[512,2,128]{0,2,1:T(8,128)(2,1)S(1)} %bitcast.95, pred[512,512]{1,0:T(8,128)(4,1)S(1)} %copy-done.12), kind=kOutput, calls=%fused_computation.13 | convolution fusion | flops 135266304 | bytes 1835008 | tf_op jit(solution)/shard_map/thd,shd->hts/dot_general | solution.py:311
  38.0 1.0 fusion.16
  39.7 1.1 copy.63.refs_1_
  40.8 2.0 %fusion.21 = bf16[2,128,512]{2,1,0:T(8,128)(2,1)S(1)} fusion(f32[2,128,512]{2,1,0:T(8,128)} %fusion.40, bf16[512,2,128]{0,2,1:T(8,128)(2,1)S(1)} %bitcast.88, bf16[2,512,512]{2,1,0:T(8,128)(2,1)} %select_convert_fusion, f32[512]{0:T(512)S(1)} %multiply_rsqrt_fusion), kind=kOutput, calls=%fused_computation.25 | convolution fusion | flops 134610944 | bytes 2099200 | tf_op jit(solution)/shard_map/hts,she->the/dot_general | solution.py:315
  42.7 1.0 fusion.17
  43.8 1.1 copy.64.refs_2_
  44.8 2.5 %fusion = f32[256,2048]{0,1:S(1)} fusion(bf16[512,256]{0,1:T(8,128)(2,1)S(1)} %bitcast.101, bf16[1,512,2048]{2,1,0:T(8,128)(2,1)} %param.11), kind=kOutput, calls=%fused_computation.1 | convolution fusion | flops 536870912 | bytes 4456448
  47.6 1.5 %copy.47 = f32[4,8,64,256]{3,2,1,0:T(8,128)} copy(f32[4,8,64,256]{3,2,0,1:T(8,128)S(1)} %multiply_bitcast_fusion.1) | data formatting | bytes 4194304 | tf_op jit(solution)/shard_map/mul | solution.py:347
  49.1 4.5 %multiply_bitcast_fusion = f32[2048,768]{0,1:T(8,128)} fusion(bf16[1,512,2048]{2,1,0:T(8,128)(2,1)S(1)} %copy-done, bf16[512,256]{1,0:T(8,128)(2,1)S(1)} %copy.64.refs_2_, bf16[512,256]{1,0:T(8,128)(2,1)S(1)} %copy.63.refs_1_, bf16[512,256]{1,0:T(8,128)(2,1)S(1)} %copy.62.refs_0_), kind=kOutput, calls=%fused_computation | convolution fusion | flops 1614544896 | bytes 9175040 | tf_op jit(solution)/shard_map/td,tk->dk/dot_general | solution.py:345
  53.7 1.2 copy-done.2
  54.9 1.2 copy-done.4
  56.1 1.2 copy-done.5
  57.3 50.4 %shard_map.102 = (f32[512,256]{1,0:T(8,128)S(1)}, f32[512,256]{1,0:T(8,128)S(1)}) custom-call(bf16[512,256]{1,0:T(8,128)(2,1)S(1)} %copy.62.refs_0_, bf16[512,256]{1,0:T(8,128)(2,1)S(1)} %copy.63.refs_1_, bf16[512,256]{1,0:T(8,128)(2,1)S(1)} %copy.64.refs_2_, bf16[2048,256]{1,0:T(8,128)(2,1)S(1)} %copy-done.5, bf16[2048,256]{1,0:T(8,128)(2,1)S(1)} %copy-done.2, ...), custom_call_target="tpu_custom_call" | custom-call | flops 3145728 | bytes 12582912 | tf_op jit(solution)/shard_map/pallas_call | solution.py:171
  108.5 1.4 %copy.48 = f32[256,768]{1,0:T(8,128)S(1)} copy(f32[256,768]{0,1:T(8,128)} %reduce-scatter.2.cloned.1.call-done) | data formatting | bytes 1572864 | tf_op jit(solution)/shard_map/optimization_barrier | solution.py:359
  109.9 15.8 %shard_map.103 = (f32[64,768]{1,0:T(8,128)S(1)}, f32[64,256]{1,0:T(8,128)S(1)}) custom-call(f32[4,64,768]{2,1,0:T(8,128)S(1)} %bitcast.80, f32[8,64,256]{2,1,0:T(8,128)S(1)} %bitcast.81), custom_call_target="tpu_custom_call" | custom-call | flops 655360 | bytes 2621440 | tf_op jit(solution)/shard_map/pallas_call | solution.py:171
  (39 shorter events, 7.6 us)
Async XLA Ops:
  7.2 1.7 %copy-start = (bf16[1,512,2048]{2,1,0:T(8,128)(2,1)S(1)}, bf16[1,512,2048]{2,1,0:T(8,128)(2,1)}, u32[]{:S(2)}) copy-start(bf16[1,512,2048]{2,1,0:T(8,128)(2,1)} %param.6) | copy-start | bytes 6291460
  7.2 3.7 %copy-start.1 = (bf16[2048,256]{1,0:T(8,128)(2,1)S(1)}, bf16[2048,256]{1,0:T(8,128)(2,1)}, u32[]{:S(2)}) copy-start(bf16[2048,256]{1,0:T(8,128)(2,1)} %refs_4_) | copy-start | bytes 3145732
  7.2 101.3 %reduce-scatter.2.cloned.1.call-start = ((), (), s32[]{:S(2)}) async-start(), calls=%async_computation.1 | async-start | bytes 7077888 | tf_op jit(solution)/shard_map/reduce_scatter | solution.py:353
  10.8 3.9 %copy-start.7 = (bf16[512,256]{0,1:T(8,128)(2,1)}, bf16[512,256]{0,1:T(8,128)(2,1)S(1)}, u32[]{:S(2)}) copy-start(bf16[512,256]{0,1:T(8,128)(2,1)S(1)} %fusion.28) | copy-start | bytes 786436
  10.9 1.3 copy-start.3
  12.2 1.6 %copy-start.9 = (bf16[1,512,2048]{2,1,0:T(8,128)(2,1)S(1)}, bf16[1,512,2048]{2,1,0:T(8,128)(2,1)}, u32[]{:S(2)}) copy-start(bf16[1,512,2048]{2,1,0:T(8,128)(2,1)} %param.11) | copy-start | bytes 6291460
  12.2 1.9 %copy-start.13 = (bf16[256,2048]{1,0:T(8,128)(2,1)S(1)}, bf16[256,2048]{1,0:T(8,128)(2,1)}, u32[]{:S(2)}) copy-start(bf16[256,2048]{1,0:T(8,128)(2,1)} %param.10) | copy-start | bytes 3145732
  16.6 19.4 %copy-start.12 = (pred[512,512]{1,0:T(8,128)(4,1)S(1)}, pred[512,512]{1,0:T(8,128)(4,1)}, u32[]{:S(2)}) copy-start(pred[512,512]{1,0:T(8,128)(4,1)} %iota_compare_fusion) | copy-start | bytes 786436
  30.4 5.3 %copy-start.11 = (f32[2,128,128]{2,1,0:T(8,128)S(1)}, f32[2,128,128]{2,1,0:T(8,128)}, u32[]{:S(2)}) copy-start(f32[2,128,128]{2,1,0:T(8,128)} %get-tuple-element.23) | copy-start | bytes 393220
  33.7 2.8 %copy-start.8 = (bf16[512,256]{0,1:T(8,128)(2,1)S(1)}, bf16[512,256]{0,1:T(8,128)(2,1)}, u32[]{:S(2)}) copy-start(bf16[512,256]{0,1:T(8,128)(2,1)} %copy-done.7) | copy-start | bytes 786436
  40.7 2.0 %copy-start.6 = (bf16[2,512,512]{2,1,0:T(8,128)(2,1)S(1)}, bf16[2,512,512]{2,1,0:T(8,128)(2,1)}, u32[]{:S(2)}) copy-start(bf16[2,512,512]{2,1,0:T(8,128)(2,1)} %select_convert_fusion) | copy-start | bytes 3145732
  40.8 2.0 %copy-start.10 = (f32[2,128,512]{2,1,0:T(8,128)S(1)}, f32[2,128,512]{2,1,0:T(8,128)}, u32[]{:S(2)}) copy-start(f32[2,128,512]{2,1,0:T(8,128)} %fusion.36) | copy-start | bytes 1572868
  53.6 1.2 copy-start.2
  54.9 1.2 copy-start.4
  56.1 1.2 copy-start.5
Sparse Core Ops, SparseCore 0:
  53.8 47.3 reduce-scatter.1

commit v21 on v19

--- a/solution.py
+++ b/solution.py
@@ -352,7 +352,7 @@
     term_qkv, factors, term_out = lax.optimization_barrier((term_qkv, factors, term_out))
     summed = lax.psum_scatter(term_qkv, "seq", scatter_dimension=0, tiled=True)
     input_grad, out_shared = ring_scatter(
-        [(head_terms, "head", jnp.float32, 4, False), (term_out, "dp", jnp.float32, 2, False)], 0,
+        [(head_terms, "head", jnp.float32, 4, False), (term_out, "dp", jnp.float32, 1, False)], 0,
         factors,
     )
     input_grad = input_grad.astype(jnp.bfloat16)[None]

time: 134 us -> 134 us (level)
  no operation moved by 1% of the time
where the time goes in v21:
time: 134 us; the launch traced here: 133 us
  Pallas kernels  79.5 us (59%)
  matrix products  25 us (19%)
  between operations  14.3 us (11%)
  local copies, waits for them, and re-layouts  12.7 us (9%)
  other arithmetic  1.74 us (1%)
    pallas_call x2, Pallas kernels, ring_scatter(): pl.pallas_call(functools.partial(ring_scatter_kernel, jobs, produce), out...  65.7 us
    pallas_call x1, Pallas kernels, exchange_states(): pl.pallas_call(functools.partial(exchange_kernel, n, axis), out_shape=(ja...  13.8 us
    unnamed x29, local copies, waits for them, and re-layouts  6.79 us
    dot_general x1, matrix products, local(): jnp.einsum('td,tk->dk', in_rows, grads, preferred_element_type=jnp.float32)  4.48 us
    dot_general x3, matrix products, project(): jnp.dot(in_rows, weight, preferred_element_type=jnp.float32)  3.5 us
  transfers between devices with their start and end apart: 1, of which 0 were waited for; matrix products, arithmetic and copies ran while one was open for 1% of the time, Pallas kernels for 38%

profile of v21, /device:TPU:8, one launch (start us, length us, event | category | flops | bytes accessed | tf_op | source)
XLA Modules:
  0.0 133.3 jit_solution(16511739681103453424)
XLA Ops:
  8.0 0.8 copy-done
  8.9 2.0 %fusion.28 = bf16[512,256]{0,1:T(8,128)(2,1)S(1)} fusion(bf16[2048,256]{1,0:T(8,128)(2,1)} %refs_3_, bf16[1,512,2048]{2,1,0:T(8,128)(2,1)S(1)} %copy-done), kind=kOutput, calls=%fused_computation.28 | convolution fusion | flops 537001984 | bytes 3407872 | tf_op jit(solution)/shard_map/dot_general | solution.py:290
  13.0 0.8 copy-done.9
  14.8 0.9 fusion.47.qg_ref
  15.7 0.9 fusion.46.kv_ref
  16.6 13.8 %shard_map.101 = (f32[2,128,128]{2,1,0:T(8,128)}, f32[2,128,128]{2,1,0:T(8,128)}) custom-call(f32[2,128,128]{2,1,0:T(8,128)} %fusion.46.kv_ref, f32[2,128,128]{2,1,0:T(8,128)} %fusion.47.qg_ref), custom_call_target="tpu_custom_call" | custom-call | tf_op jit(solution)/shard_map/pallas_call | solution.py:264
  30.4 2.1 %fusion.40 = f32[2,128,512]{2,1,0:T(8,128)} fusion(bf16[512,2,128]{0,2,1:T(8,128)(2,1)} %bitcast.98, f32[2,128,128]{2,1,0:T(8,128)} %get-tuple-element.22), kind=kOutput, calls=%fused_computation.40 | convolution fusion | flops 33587200 | bytes 917504 | tf_op jit(solution)/shard_map/thd,hde->the/dot_general | solution.py:318
  32.6 1.1 fusion.42
  33.7 2.0 %fusion.36 = f32[2,128,512]{2,1,0:T(8,128)} fusion(bf16[512,2,128]{0,2,1:T(8,128)(2,1)S(1)} %bitcast.94, f32[2,128,128]{2,1,0:T(8,128)} %get-tuple-element.23), kind=kOutput, calls=%fused_computation.36 | convolution fusion | flops 33587200 | bytes 917504 | tf_op jit(solution)/shard_map/shd,hde->she/dot_general | solution.py:333
  36.5 1.5 %select_convert_fusion = bf16[2,512,512]{2,1,0:T(8,128)(2,1)} fusion(bf16[512,2,128]{0,2,1:T(8,128)(2,1)S(1)} %bitcast.99, bf16[512,2,128]{0,2,1:T(8,128)(2,1)S(1)} %bitcast.95, pred[512,512]{1,0:T(8,128)(4,1)S(1)} %copy-done.12), kind=kOutput, calls=%fused_computation.13 | convolution fusion | flops 135266304 | bytes 1835008 | tf_op jit(solution)/shard_map/thd,shd->hts/dot_general | solution.py:311
  38.0 1.0 fusion.16
  39.7 1.1 copy.63.refs_1_
  40.8 2.0 %fusion.21 = bf16[2,128,512]{2,1,0:T(8,128)(2,1)S(1)} fusion(f32[2,128,512]{2,1,0:T(8,128)} %fusion.40, bf16[512,2,128]{0,2,1:T(8,128)(2,1)S(1)} %bitcast.88, bf16[2,512,512]{2,1,0:T(8,128)(2,1)} %select_convert_fusion, f32[512]{0:T(512)S(1)} %multiply_rsqrt_fusion), kind=kOutput, calls=%fused_computation.25 | convolution fusion | flops 134610944 | bytes 2099200 | tf_op jit(solution)/shard_map/hts,she->the/dot_general | solution.py:315
  42.7 1.0 fusion.17
  43.8 1.1 copy.64.refs_2_
  44.8 2.5 %fusion = f32[256,2048]{0,1:S(1)} fusion(bf16[512,256]{0,1:T(8,128)(2,1)S(1)} %bitcast.101, bf16[1,512,2048]{2,1,0:T(8,128)(2,1)} %param.11), kind=kOutput, calls=%fused_computation.1 | convolution fusion | flops 536870912 | bytes 4456448
  47.6 1.5 %copy.47 = f32[4,8,64,256]{3,2,1,0:T(8,128)} copy(f32[4,8,64,256]{3,2,0,1:T(8,128)S(1)} %multiply_bitcast_fusion.1) | data formatting | bytes 4194304 | tf_op jit(solution)/shard_map/mul | solution.py:347
  49.1 4.5 %multiply_bitcast_fusion = f32[2048,768]{0,1:T(8,128)} fusion(bf16[1,512,2048]{2,1,0:T(8,128)(2,1)S(1)} %copy-done, bf16[512,256]{1,0:T(8,128)(2,1)S(1)} %copy.64.refs_2_, bf16[512,256]{1,0:T(8,128)(2,1)S(1)} %copy.63.refs_1_, bf16[512,256]{1,0:T(8,128)(2,1)S(1)} %copy.62.refs_0_), kind=kOutput, calls=%fused_computation | convolution fusion | flops 1614544896 | bytes 9175040 | tf_op jit(solution)/shard_map/td,tk->dk/dot_general | solution.py:345
  53.7 1.2 copy-done.2
  54.9 1.2 copy-done.4
  56.1 1.2 copy-done.5
  57.3 50.3 %shard_map.102 = (f32[512,256]{1,0:T(8,128)S(1)}, f32[512,256]{1,0:T(8,128)S(1)}) custom-call(bf16[512,256]{1,0:T(8,128)(2,1)S(1)} %copy.62.refs_0_, bf16[512,256]{1,0:T(8,128)(2,1)S(1)} %copy.63.refs_1_, bf16[512,256]{1,0:T(8,128)(2,1)S(1)} %copy.64.refs_2_, bf16[2048,256]{1,0:T(8,128)(2,1)S(1)} %copy-done.5, bf16[2048,256]{1,0:T(8,128)(2,1)S(1)} %copy-done.2, ...), custom_call_target="tpu_custom_call" | custom-call | flops 3145728 | bytes 12582912 | tf_op jit(solution)/shard_map/pallas_call | solution.py:171
  108.4 1.4 %copy.48 = f32[256,768]{1,0:T(8,128)S(1)} copy(f32[256,768]{0,1:T(8,128)} %reduce-scatter.2.cloned.1.call-done) | data formatting | bytes 1572864 | tf_op jit(solution)/shard_map/optimization_barrier | solution.py:359
  109.8 15.3 %shard_map.103 = (f32[64,768]{1,0:T(8,128)S(1)}, f32[64,256]{1,0:T(8,128)S(1)}) custom-call(f32[4,64,768]{2,1,0:T(8,128)S(1)} %bitcast.80, f32[8,64,256]{2,1,0:T(8,128)S(1)} %bitcast.81), custom_call_target="tpu_custom_call" | custom-call | flops 655360 | bytes 2621440 | tf_op jit(solution)/shard_map/pallas_call | solution.py:171
  (39 shorter events, 7.6 us)
Async XLA Ops:
  7.2 1.7 %copy-start = (bf16[1,512,2048]{2,1,0:T(8,128)(2,1)S(1)}, bf16[1,512,2048]{2,1,0:T(8,128)(2,1)}, u32[]{:S(2)}) copy-start(bf16[1,512,2048]{2,1,0:T(8,128)(2,1)} %param.6) | copy-start | bytes 6291460
  7.2 3.7 %copy-start.1 = (bf16[2048,256]{1,0:T(8,128)(2,1)S(1)}, bf16[2048,256]{1,0:T(8,128)(2,1)}, u32[]{:S(2)}) copy-start(bf16[2048,256]{1,0:T(8,128)(2,1)} %refs_4_) | copy-start | bytes 3145732
  7.2 101.2 %reduce-scatter.2.cloned.1.call-start = ((), (), s32[]{:S(2)}) async-start(), calls=%async_computation.1 | async-start | bytes 7077888 | tf_op jit(solution)/shard_map/reduce_scatter | solution.py:353
  10.8 3.9 %copy-start.7 = (bf16[512,256]{0,1:T(8,128)(2,1)}, bf16[512,256]{0,1:T(8,128)(2,1)S(1)}, u32[]{:S(2)}) copy-start(bf16[512,256]{0,1:T(8,128)(2,1)S(1)} %fusion.28) | copy-start | bytes 786436
  10.9 1.3 copy-start.3
  12.2 1.6 %copy-start.9 = (bf16[1,512,2048]{2,1,0:T(8,128)(2,1)S(1)}, bf16[1,512,2048]{2,1,0:T(8,128)(2,1)}, u32[]{:S(2)}) copy-start(bf16[1,512,2048]{2,1,0:T(8,128)(2,1)} %param.11) | copy-start | bytes 6291460
  12.2 1.9 %copy-start.13 = (bf16[256,2048]{1,0:T(8,128)(2,1)S(1)}, bf16[256,2048]{1,0:T(8,128)(2,1)}, u32[]{:S(2)}) copy-start(bf16[256,2048]{1,0:T(8,128)(2,1)} %param.10) | copy-start | bytes 3145732
  16.6 19.4 %copy-start.12 = (pred[512,512]{1,0:T(8,128)(4,1)S(1)}, pred[512,512]{1,0:T(8,128)(4,1)}, u32[]{:S(2)}) copy-start(pred[512,512]{1,0:T(8,128)(4,1)} %iota_compare_fusion) | copy-start | bytes 786436
  30.4 5.3 %copy-start.11 = (f32[2,128,128]{2,1,0:T(8,128)S(1)}, f32[2,128,128]{2,1,0:T(8,128)}, u32[]{:S(2)}) copy-start(f32[2,128,128]{2,1,0:T(8,128)} %get-tuple-element.23) | copy-start | bytes 393220
  33.7 2.8 %copy-start.8 = (bf16[512,256]{0,1:T(8,128)(2,1)S(1)}, bf16[512,256]{0,1:T(8,128)(2,1)}, u32[]{:S(2)}) copy-start(bf16[512,256]{0,1:T(8,128)(2,1)} %copy-done.7) | copy-start | bytes 786436
  40.7 2.0 %copy-start.6 = (bf16[2,512,512]{2,1,0:T(8,128)(2,1)S(1)}, bf16[2,512,512]{2,1,0:T(8,128)(2,1)}, u32[]{:S(2)}) copy-start(bf16[2,512,512]{2,1,0:T(8,128)(2,1)} %select_convert_fusion) | copy-start | bytes 3145732
  40.8 2.0 %copy-start.10 = (f32[2,128,512]{2,1,0:T(8,128)S(1)}, f32[2,128,512]{2,1,0:T(8,128)}, u32[]{:S(2)}) copy-start(f32[2,128,512]{2,1,0:T(8,128)} %fusion.36) | copy-start | bytes 1572868
  53.6 1.2 copy-start.2
  54.9 1.2 copy-start.4
  56.1 1.2 copy-start.5
Sparse Core Ops, SparseCore 0:
  53.8 47.3 reduce-scatter.1
